TPU v7x, 512 devices: a whole 4x4x16 slice. The times are simulated.
512 devices in a mesh: span: 64 (over z_lo, x, core), chord: 8 (over z_hi, y).
Axes of the slice: x: 4, y: 4, z: 16 (z_hi: 2, z_lo: 8; z = z_hi * 8 + z_lo), core: 2. Of those that a mesh axis runs over, the one named last changes fastest.
Arguments:
- adjoint_flow: float32 [5, 16, 512, 1024], P(None, None, 'span', 'chord'), may hold values from -6 to 6
- flow_grad: float32 [5, 16, 512, 1024], P(None, None, 'span', 'chord'), may hold values from -6 to 6
- diagonal: float32 [16, 512, 1024], P(None, 'span', 'chord'), may hold values from 4 to 6
- couplings: float32 [3, 16, 512, 1024], P(None, None, 'span', 'chord'), may hold values from 0.3 to 1.5
- upwind: float32 [3, 5, 5], replicated, may hold values from -2.5 to 2.5
- downwind: float32 [3, 5, 5], replicated, may hold values from -2.5 to 2.5
- pressure_row: float32 [5], replicated, may hold values from -4 to 4
- face_normal: float32 [3, 512, 1024], P(None, 'span', 'chord'), may hold values from -6 to 6
- face_node: int32 [512, 1024], P('span', 'chord'), may hold values from 0 to 65535, as said below
- face_count: int32 [64, 8], P('span', 'chord'), may hold values from 128 to 1024, as said below
- adjoint_shell: float32 [6, 65536], P(None, 'span'), may hold values from -6 to 6
- shell_grad: float32 [6, 65536], P(None, 'span'), may hold values from -6 to 6
- node_precond: float32 [6, 6, 65536], P(None, None, 'span'), as said below
- element_stiffness: float32 [24, 24, 65536], P(None, None, ('span', 'chord')), as said below
- connectivity: int32 [4, 65536], P(None, ('span', 'chord')), may hold values from 0 to 65535, as said below
Outputs:
- flow_adjoint: float32 [5, 16, 512, 1024], P(None, None, 'span', 'chord')
- shell_adjoint: float32 [6, 65536], P(None, 'span')
Inputs may be any that keep to these rules, and one draw needn't show every extreme that they name: `face_node`: a wall face in the span cells of span index s names a node from max(s - 1, 0) * 1024 to min(s + 2, 64) * 1024 - 1. `face_count`: on each device the wall faces in use are the first ones in span-major, chord-minor order. `connectivity`: the elements of span index s use nodes from s * 1024 to min((s + 1) * 1024 + 64, 65536) - 1. `node_precond`: each node block is near 0.15 times the identity. `element_stiffness`: each element block is symmetric and near the identity.
All inputs are finite; a program needn't handle non-finite values.
Results may differ from a plain program's by a relative error of at most 0.00013.
Values sent between devices are 32-bit elements; how exact they have to be, the bound alone decides.
No kernel may reach another device: no remote copies, remote signals or barrier semaphores. Data moves between devices by JAX's collectives and lax.ppermute only.
A program may use at most 64 MiB of HBM per device.

v0:
```python
import jax
import jax.numpy as jnp
from jax import lax
from jax.sharding import PartitionSpec as P

NB = 64
SW = 4
SS = 3


def shifted(value, axis, steps):
    count = lax.axis_size(axis)
    initial, last = (max(0, -steps), min(count, count - steps))
    return lax.ppermute(value, axis, [(source, source + steps) for source in range(initial, last)])


def with_halo(cells, sides, width):
    for axis, dim in sides:
        count = lax.axis_size(axis)
        ends = count - 1
        head = lax.slice_in_dim(cells, 0, width, axis=dim)
        tail = lax.slice_in_dim(cells, cells.shape[dim] - width, cells.shape[dim], axis=dim)
        cells = jnp.concatenate(
            [
                lax.ppermute(tail, axis, [(i, (i + 1) % count) for i in range(ends)]),
                cells,
                lax.ppermute(head, axis, [((i + 1) % count, i) for i in range(ends)]),
            ],
            axis=dim,
        )
    return cells


def relax_cells(state, inv_diag, couplings, source, upwind, downwind):
    centre = state[:, :, 1:-1, 1:-1]
    normal_pad = jnp.pad(centre, ((0, 0), (1, 1), (0, 0), (0, 0)))
    pairs = (
        (normal_pad[:, 2:], normal_pad[:, :-2]),
        (state[:, :, 2:, 1:-1], state[:, :, :-2, 1:-1]),
        (state[:, :, 1:-1, 2:], state[:, :, 1:-1, :-2]),
    )
    neighbours = jnp.zeros_like(source)
    for direction in range(3):
        forward, backward = pairs[direction]
        flux_term = jnp.einsum(
            "ij,jnsc->insc", upwind[direction], forward, precision=lax.Precision.HIGHEST
        )
        flux_term = flux_term + jnp.einsum(
            "ij,jnsc->insc", downwind[direction], backward, precision=lax.Precision.HIGHEST
        )
        neighbours = neighbours + couplings[direction][None] * flux_term
    return inv_diag[None] * (source + neighbours)


def spread(partial_value, node_dev):
    own_block = partial_value[:, node_dev : 2 * node_dev]
    from_lower = shifted(partial_value[:, 2 * node_dev :], "span", 1)
    from_upper = shifted(partial_value[:, :node_dev], "span", -1)
    return own_block + from_lower + from_upper


def element_terms(field, element_stiffness, local_nodes):
    node_dev = field.shape[1]
    count_elems = local_nodes.shape[1]
    rim_nodes = shifted(field[:, :NB], "span", -1)
    extended = jnp.concatenate([field, rim_nodes], axis=1)
    element_values = extended[:, local_nodes]
    element_values = jnp.transpose(element_values, (1, 0, 2)).reshape(24, count_elems)
    element_forces = jnp.einsum(
        "ije,je->ie", element_stiffness, element_values, precision=lax.Precision.HIGHEST
    )
    element_forces = jnp.transpose(element_forces.reshape(4, 6, count_elems), (1, 0, 2)).reshape(
        6, 4 * count_elems
    )
    assembled = jax.ops.segment_sum(element_forces.T, local_nodes.reshape(-1), node_dev + NB).T
    spill = shifted(assembled[:, node_dev:], "span", 1)
    return assembled[:, :node_dev].at[:, :NB].add(spill)


def per_device(
    adjoint_flow,
    flow_grad,
    diagonal,
    couplings,
    upwind,
    downwind,
    pressure_row,
    face_normal,
    face_node,
    face_count,
    adjoint_shell,
    shell_grad,
    node_precond,
    element_stiffness,
    connectivity,
):
    span_at = lax.axis_index("span")
    node_dev = adjoint_shell.shape[1]
    wall_layer = adjoint_flow[:, 0]
    span_cells = wall_layer.shape[1]
    chord_cells = wall_layer.shape[2]
    local_index = (
        jnp.arange(span_cells, dtype=jnp.int32)[:, None] * chord_cells
        + jnp.arange(chord_cells, dtype=jnp.int32)[None, :]
    )
    active = (local_index < face_count[0, 0]).astype(jnp.float32)
    pressure = (
        jnp.einsum("j,jsc->sc", pressure_row, wall_layer, precision=lax.Precision.HIGHEST) * active
    )
    loads_face = face_normal * pressure[None]
    reach_index = face_node - (span_at - 1) * node_dev
    partial_value = jax.ops.segment_sum(
        loads_face.reshape(3, -1).T, reach_index.reshape(-1), 3 * node_dev
    ).T
    partial_value = lax.psum(partial_value, "chord")
    node_load = spread(partial_value, node_dev)
    load_full = jnp.concatenate([node_load, jnp.zeros((3, node_dev), jnp.float32)], axis=0)
    local_nodes = connectivity - span_at * node_dev
    shell_state = adjoint_shell
    for turn_index in range(SS):
        local_forces = element_terms(shell_state, element_stiffness, local_nodes)
        stiff_total = lax.psum(local_forces, "chord")
        residual = shell_grad - load_full - stiff_total
        shell_state = shell_state + jnp.einsum(
            "ijn,jn->in", node_precond, residual, precision=lax.Precision.HIGHEST
        )
    reach = with_halo(shell_state[:3], (("span", 1),), node_dev)
    picked = reach[:, reach_index]
    disp = jnp.einsum("isc,isc->sc", face_normal, picked, precision=lax.Precision.HIGHEST) * active
    source = flow_grad.at[:, 0].add(-pressure_row[:, None, None] * disp[None])
    inv_diag = 1.0 / diagonal
    state = adjoint_flow
    for turn_index in range(SW):
        padded = with_halo(state, (("span", 2), ("chord", 3)), 1)
        state = relax_cells(padded, inv_diag, couplings, source, upwind, downwind)
    return (state, shell_state)


def solution(mesh):
    return jax.shard_map(
        per_device,
        mesh=mesh,
        in_specs=(
            P(None, None, "span", "chord"),
            P(None, None, "span", "chord"),
            P(None, "span", "chord"),
            P(None, None, "span", "chord"),
            P(),
            P(),
            P(),
            P(None, "span", "chord"),
            P("span", "chord"),
            P("span", "chord"),
            P(None, "span"),
            P(None, "span"),
            P(None, None, "span"),
            P(None, None, ("span", "chord")),
            P(None, ("span", "chord")),
        ),
        out_specs=(P(None, None, "span", "chord"), P(None, "span")),
        check_vma=False,
    )
```

profile of v0, /device:TPU:223, one launch (start us, length us, event | category | flops | bytes accessed | tf_op | source)
XLA Modules:
  0.0 633.0 jit_solution(17247283147842668898)
XLA Ops:
  1.4 2.6 collective-permute-start.2
  5.8 5.1 collective-permute-start.11
  10.9 1.9 collective-permute-start.10
  19.8 2.4 scatter_custom_fusion.1
  22.8 5.7 collective-permute-start.3
  28.8 6.4 %scatter_custom_fusion = f32[3072,3]{1,0:T(8,128)S(1)} fusion(s32[1024]{0:T(1024)S(1)} %subtract_bitcast_fusion.3, f32[1024,3]{1,0:T(8,128)S(1)} %bitcast.192, f32[]{:T(128)} %constant.114.clone.1), kind=kCustom, calls=%fused_computation.52 | custom fusion | flops 3072 | bytes 36868 | tf_op jit(solution)/shard_map/scatter-add | solution.py:112
  36.7 194.2 %all-reduce.5 = (f32[6,1024]{0,1:T(8,128)}, f32[3,3072]{0,1:T(8,128)}) all-reduce(f32[6,1024]{0,1:T(8,128)S(1)} %fusion.84, f32[3,3072]{0,1:T(8,128)S(1)} %bitcast.181), channel_id=1, replica_groups=mesh['span'=64,'chord'=8] {'chord'}, use_global_device_ids=true, to_apply=%region_4.0 | all-reduce | flops 15360 | bytes 122880 | tf_op jit(solution)/shard_map/psum | solution.py:122
  230.9 2.1 fusion.115
  233.0 1.9 collective-permute-start
  234.9 18.2 %collective-permute-start.1 = (f32[3,1024]{0,1:T(8,128)S(1)}, f32[3,1024]{0,1:T(8,128)}, u32[]{:S(2)}, u32[]{:S(2)}) collective-permute-start(f32[3,1024]{0,1:T(8,128)S(1)} %get-tuple-element.61), channel_id=1, source_target_pairs={{8,0},{16,8},{24,16},{32,24},{40,32},{48,40},{56,48},{64,56},{72,6... | collective-permute-start | bytes 36872 | tf_op jit(solution)/shard_map/ppermute | solution.py:14
  257.1 8.7 %collective-permute-start.4 = (f32[6,64]{1,0:T(8,128)S(1)}, f32[6,64]{1,0:T(8,128)S(1)}, u32[]{:S(2)}, u32[]{:S(2)}) collective-permute-start(f32[6,64]{1,0:T(8,128)S(1)} %slice.401), channel_id=1, source_target_pairs={{8,0},{16,8},{24,16},{32,24},{40,32},{48,40},{56,48},{64,56},{72,6... | collective-permute-start | bytes 4616 | tf_op jit(solution)/shard_map/ppermute | solution.py:14
  267.6 1.8 gather_fusion.1
  271.4 2.8 scatter_custom_fusion.2
  274.2 1.9 collective-permute-start.5
  280.1 68.6 %psum.30 = f32[6,1024]{0,1:T(8,128)S(1)} all-reduce(f32[6,1024]{0,1:T(8,128)} %fusion.85), channel_id=1, replica_groups=mesh['span'=64,'chord'=8] {'chord'}, use_global_device_ids=true, to_apply=%region_6.0 | all-reduce | flops 6144 | bytes 49152 | tf_op jit(solution)/shard_map/psum | solution.py:122
  350.9 19.7 %collective-permute-start.6 = (f32[6,64]{1,0:T(8,128)S(1)}, f32[6,64]{1,0:T(8,128)S(1)}, u32[]{:S(2)}, u32[]{:S(2)}) collective-permute-start(f32[6,64]{1,0:T(8,128)S(1)} %slice.405), channel_id=1, source_target_pairs={{8,0},{16,8},{24,16},{32,24},{40,32},{48,40},{56,48},{64,56},{72,6... | collective-permute-start | bytes 4616 | tf_op jit(solution)/shard_map/ppermute | solution.py:14
  370.6 2.2 fusion.3
  374.5 2.5 scatter_custom_fusion.3
  377.0 1.9 collective-permute-start.7
  380.8 78.4 %psum.31 = f32[6,1024]{0,1:T(8,128)S(1)} all-reduce(f32[6,1024]{0,1:T(8,128)S(1)} %fusion.86), channel_id=1, replica_groups=mesh['span'=64,'chord'=8] {'chord'}, use_global_device_ids=true, to_apply=%region_8.0 | all-reduce | flops 6144 | bytes 49152 | tf_op jit(solution)/shard_map/psum | solution.py:122
  460.2 13.6 %collective-permute-start.8 = (f32[3,1024]{1,0:T(4,128)S(1)}, f32[3,1024]{1,0:T(4,128)S(1)}, u32[]{:S(2)}, u32[]{:S(2)}) collective-permute-start(f32[3,1024]{1,0:T(4,128)S(1)} %slice.409), channel_id=1, source_target_pairs={{0,8},{8,16},{16,24},{24,32},{32,40},{40,48},{48,56},{56,64},{64,7... | collective-permute-start | bytes 36872 | tf_op jit(solution)/shard_map/ppermute | solution.py:25
  473.8 1.9 collective-permute-start.9
  477.0 4.0 collective-permute-done.9
  481.5 4.0 gather_fusion.3
  489.5 14.8 %collective-permute-start.13 = (f32[5,16,10,1]{1,3,2,0:T(1,128)S(1)}, f32[5,16,10,1]{1,3,2,0:T(1,128)S(1)}, u32[]{:S(2)}, u32[]{:S(2)}) collective-permute-start(f32[5,16,10,1]{1,3,2,0:T(1,128)S(1)} %copy.116), channel_id=1, source_target_pairs={{0,1},{1,2},{2,3},{3,4},{4,5},{5,6},{6,7},{8,9},{9,10},{10,11},{11... | collective-permute-start | bytes 9608 | tf_op jit(solution)/shard_map/ppermute | solution.py:25
  504.6 1.9 collective-permute-start.12
  506.6 2.2 fusion.37
  510.7 9.3 %collective-permute-done.12 = f32[5,16,10,1]{1,3,2,0:T(1,128)S(1)} collective-permute-done((f32[5,16,10,1]{1,3,2,0:T(1,128)S(1)}, f32[5,16,10,1]{1,3,2,0:T(1,128)S(1)}, u32[]{:S(2)}, u32[]{:S(2)}) %collective-permute-start.12) | collective-permute-done | bytes 3232 | tf_op jit(solution)/shard_map/ppermute | solution.py:27
  520.4 1.9 fusion.23
  522.4 1.8 fusion.25
  524.7 3.5 collective-permute-start.15
  528.2 1.9 collective-permute-start.14
  530.8 5.1 collective-permute-done.14
  536.9 3.9 collective-permute-start.17
  541.8 2.1 collective-permute-start.16
  547.2 10.3 %collective-permute-done.16 = f32[5,16,10,1]{1,3,2,0:T(1,128)} collective-permute-done((f32[5,16,10,1]{1,3,2,0:T(1,128)}, f32[5,16,10,1]{1,3,2,0:T(1,128)}, u32[]{:S(2)}, u32[]{:S(2)}) %collective-permute-start.16) | collective-permute-done | bytes 3232 | tf_op jit(solution)/shard_map/ppermute | solution.py:27
  561.7 3.3 collective-permute-start.19
  565.0 1.9 collective-permute-start.18
  567.5 5.2 collective-permute-done.18
  574.0 3.1 collective-permute-start.21
  578.1 2.3 collective-permute-start.20
  583.0 10.8 %collective-permute-done.20 = f32[5,16,10,1]{1,3,2,0:T(1,128)} collective-permute-done((f32[5,16,10,1]{1,3,2,0:T(1,128)}, f32[5,16,10,1]{1,3,2,0:T(1,128)}, u32[]{:S(2)}, u32[]{:S(2)}) %collective-permute-start.20) | collective-permute-done | bytes 3232 | tf_op jit(solution)/shard_map/ppermute | solution.py:27
  598.1 3.3 collective-permute-start.23
  601.4 1.9 collective-permute-start.22
  603.9 5.4 collective-permute-done.22
  610.7 1.9 collective-permute-start.25
  613.6 3.6 collective-permute-start.24
  618.9 10.4 %collective-permute-done.24 = f32[5,16,10,1]{1,3,2,0:T(1,128)} collective-permute-done((f32[5,16,10,1]{1,3,2,0:T(1,128)}, f32[5,16,10,1]{1,3,2,0:T(1,128)}, u32[]{:S(2)}, u32[]{:S(2)}) %collective-permute-start.24) | collective-permute-done | bytes 3232 | tf_op jit(solution)/shard_map/ppermute | solution.py:27
  (229 shorter events, 65.6 us)
Async XLA Ops:
  0.6 18.9 %copy-start.1 = (f32[24,24,128]{2,1,0:T(8,128)S(1)}, f32[24,24,128]{2,1,0:T(8,128)}, u32[]{:S(2)}) copy-start(f32[24,24,128]{2,1,0:T(8,128)} %param.36) | copy-start | bytes 884740
  1.4 16.0 %collective-permute-start.2 = (f32[6,64]{1,0:T(8,128)S(1)}, f32[6,64]{1,0:T(8,128)S(1)}, u32[]{:S(2)}, u32[]{:S(2)}) collective-permute-start(f32[6,64]{1,0:T(8,128)S(1)} %slice.324), channel_id=1, source_target_pairs={{8,0},{16,8},{24,16},{32,24},{40,32},{48,40},{56,48},{64,56},{72,6... | collective-permute-start | bytes 4616 | tf_op jit(solution)/shard_map/ppermute | solution.py:14
  5.1 23.4 %copy-start.37 = (s32[8,128]{1,0:T(8,128)S(1)}, s32[8,128]{1,0:T(8,128)}, u32[]{:S(2)}) copy-start(s32[8,128]{1,0:T(8,128)} %param.31) | copy-start | bytes 12292
  5.8 481.1 %collective-permute-start.11 = (f32[5,16,1,128]{3,0,2,1:T(8,128)}, f32[5,16,1,128]{3,0,2,1:T(8,128)}, u32[]{:S(2)}, u32[]{:S(2)}) collective-permute-start(f32[5,16,1,128]{3,0,2,1:T(8,128)} %get-tuple-element.77), channel_id=1, source_target_pairs={{0,8},{8,16},{16,24},{24,32},{32,40},{40,48},{48,56},{56,64},{64,7... | collective-permute-start | bytes 122888 | tf_op jit(solution)/shard_map/ppermute | solution.py:25
  10.9 477.1 %collective-permute-start.10 = (f32[5,16,1,128]{3,0,2,1:T(8,128)}, f32[5,16,1,128]{3,0,2,1:T(8,128)}, u32[]{:S(2)}, u32[]{:S(2)}) collective-permute-start(f32[5,16,1,128]{3,0,2,1:T(8,128)} %get-tuple-element.76), channel_id=1, source_target_pairs={{8,0},{16,8},{24,16},{32,24},{40,32},{48,40},{56,48},{64,56},{72,6... | collective-permute-start | bytes 122888 | tf_op jit(solution)/shard_map/ppermute | solution.py:27
  12.8 22.4 %copy-start.39 = (s32[8]{0:T(128)}, s32[8]{0:T(128)S(1)}, u32[]{:S(2)}) copy-start(s32[8]{0:T(128)S(1)} %iota_multiply_fusion) | copy-start | bytes 100
  15.7 19.5 %copy-start.41 = (s32[512]{0:T(512)}, s32[512]{0:T(512)S(1)}, u32[]{:S(2)}) copy-start(s32[512]{0:T(512)S(1)} %get-tuple-element.88) | copy-start | bytes 6148
  22.8 13.2 %collective-permute-start.3 = (f32[6,64]{0,1:T(8,128)}, f32[6,64]{0,1:T(8,128)S(1)}, u32[]{:S(2)}, u32[]{:S(2)}) collective-permute-start(f32[6,64]{0,1:T(8,128)} %slice.400), channel_id=1, source_target_pairs={{0,8},{8,16},{16,24},{24,32},{32,40},{40,48},{48,56},{56,64},{64,7... | collective-permute-start | bytes 4616 | tf_op jit(solution)/shard_map/ppermute | solution.py:14
  230.9 22.2 %copy-start = (f32[5,16,8,128]{3,2,1,0:T(8,128)S(1)}, f32[5,16,8,128]{3,2,1,0:T(8,128)}, u32[]{:S(2)}) copy-start(f32[5,16,8,128]{3,2,1,0:T(8,128)} %param.23) | copy-start | bytes 983044
  230.9 22.8 %copy-start.34 = (f32[6,1024]{1,0:T(8,128)S(1)}, f32[6,1024]{1,0:T(8,128)}, u32[]{:S(2)}) copy-start(f32[6,1024]{1,0:T(8,128)} %param.34) | copy-start | bytes 73732
  233.0 21.0 %collective-permute-start = (f32[3,1024]{0,1:T(8,128)}, f32[3,1024]{0,1:T(8,128)S(1)}, u32[]{:S(2)}, u32[]{:S(2)}) collective-permute-start(f32[3,1024]{0,1:T(8,128)} %get-tuple-element.60), channel_id=1, source_target_pairs={{0,8},{8,16},{16,24},{24,32},{32,40},{40,48},{48,56},{56,64},{64,7... | collective-permute-start | bytes 36872 | tf_op jit(solution)/shard_map/ppermute | solution.py:14
  234.9 19.8 %collective-permute-start.1 = (f32[3,1024]{0,1:T(8,128)S(1)}, f32[3,1024]{0,1:T(8,128)}, u32[]{:S(2)}, u32[]{:S(2)}) collective-permute-start(f32[3,1024]{0,1:T(8,128)S(1)} %get-tuple-element.61), channel_id=1, source_target_pairs={{8,0},{16,8},{24,16},{32,24},{40,32},{48,40},{56,48},{64,56},{72,6... | collective-permute-start | bytes 36872 | tf_op jit(solution)/shard_map/ppermute | solution.py:14
  257.1 10.3 %collective-permute-start.4 = (f32[6,64]{1,0:T(8,128)S(1)}, f32[6,64]{1,0:T(8,128)S(1)}, u32[]{:S(2)}, u32[]{:S(2)}) collective-permute-start(f32[6,64]{1,0:T(8,128)S(1)} %slice.401), channel_id=1, source_target_pairs={{8,0},{16,8},{24,16},{32,24},{40,32},{48,40},{56,48},{64,56},{72,6... | collective-permute-start | bytes 4616 | tf_op jit(solution)/shard_map/ppermute | solution.py:14
  274.2 4.6 collective-permute-start.5
  348.7 21.9 %copy-start.8 = (f32[16,8,128]{2,1,0:T(8,128)S(1)}, f32[16,8,128]{2,1,0:T(8,128)}, u32[]{:S(2)}) copy-start(f32[16,8,128]{2,1,0:T(8,128)} %get-tuple-element.79) | copy-start | bytes 196612
  349.6 23.6 %copy-start.36 = (s32[1024]{0:T(1024)S(1)}, s32[1024]{0:T(1024)}, u32[]{:S(2)}) copy-start(s32[1024]{0:T(1024)} %copy-done.35) | copy-start | bytes 12292
  350.9 22.0 %collective-permute-start.6 = (f32[6,64]{1,0:T(8,128)S(1)}, f32[6,64]{1,0:T(8,128)S(1)}, u32[]{:S(2)}, u32[]{:S(2)}) collective-permute-start(f32[6,64]{1,0:T(8,128)S(1)} %slice.405), channel_id=1, source_target_pairs={{8,0},{16,8},{24,16},{32,24},{40,32},{48,40},{56,48},{64,56},{72,6... | collective-permute-start | bytes 4616 | tf_op jit(solution)/shard_map/ppermute | solution.py:14
  377.0 3.1 collective-permute-start.7
  459.2 16.6 %copy-start.38 = (s32[8,128]{1,0:T(8,128)S(1)}, s32[8,128]{1,0:T(8,128)}, u32[]{:S(2)}) copy-start(s32[8,128]{1,0:T(8,128)} %param.31) | copy-start | bytes 12292
  459.2 16.6 %copy-start.42 = (f32[5]{0:T(128)S(1)}, f32[5]{0:T(128)}, u32[]{:S(2)}) copy-start(f32[5]{0:T(128)} %param.29) | copy-start | bytes 64
  460.2 26.6 %copy-start.31 = (f32[6,1024]{1,0:T(8,128)}, f32[6,1024]{1,0:T(8,128)S(1)}, u32[]{:S(2)}) copy-start(f32[6,1024]{1,0:T(8,128)S(1)} %bitcast_add_fusion) | copy-start | bytes 73732
  460.2 16.8 %collective-permute-start.8 = (f32[3,1024]{1,0:T(4,128)S(1)}, f32[3,1024]{1,0:T(4,128)S(1)}, u32[]{:S(2)}, u32[]{:S(2)}) collective-permute-start(f32[3,1024]{1,0:T(4,128)S(1)} %slice.409), channel_id=1, source_target_pairs={{0,8},{8,16},{16,24},{24,32},{32,40},{40,48},{48,56},{56,64},{64,7... | collective-permute-start | bytes 36872 | tf_op jit(solution)/shard_map/ppermute | solution.py:25
  473.8 7.2 %collective-permute-start.9 = (f32[3,1024]{1,0:T(4,128)S(1)}, f32[3,1024]{1,0:T(4,128)S(1)}, u32[]{:S(2)}, u32[]{:S(2)}) collective-permute-start(f32[3,1024]{1,0:T(4,128)S(1)} %slice.409), channel_id=1, source_target_pairs={{8,0},{16,8},{24,16},{32,24},{40,32},{48,40},{56,48},{64,56},{72,6... | collective-permute-start | bytes 36872 | tf_op jit(solution)/shard_map/ppermute | solution.py:27
  475.8 11.0 %copy-start.33 = (f32[3,8,128]{2,1,0:T(8,128)S(1)}, f32[3,8,128]{2,1,0:T(8,128)}, u32[]{:S(2)}) copy-start(f32[3,8,128]{2,1,0:T(8,128)} %param.30) | copy-start | bytes 36868
  475.8 11.0 %copy-start.40 = (s32[8]{0:T(128)S(1)}, s32[8]{0:T(128)}, u32[]{:S(2)}) copy-start(s32[8]{0:T(128)} %copy-done.39) | copy-start | bytes 100
  488.9 17.7 %copy-start.24 = (f32[1,5,5]{2,0,1:T(1,128)S(1)}, f32[1,5,5]{2,0,1:T(1,128)}, u32[]{:S(2)}) copy-start(f32[1,5,5]{2,0,1:T(1,128)} %get-tuple-element.84) | copy-start | bytes 304
  489.5 19.3 %collective-permute-start.13 = (f32[5,16,10,1]{1,3,2,0:T(1,128)S(1)}, f32[5,16,10,1]{1,3,2,0:T(1,128)S(1)}, u32[]{:S(2)}, u32[]{:S(2)}) collective-permute-start(f32[5,16,10,1]{1,3,2,0:T(1,128)S(1)} %copy.116), channel_id=1, source_target_pairs={{0,1},{1,2},{2,3},{3,4},{4,5},{5,6},{6,7},{8,9},{9,10},{10,11},{11... | collective-permute-start | bytes 9608 | tf_op jit(solution)/shard_map/ppermute | solution.py:25
  504.6 15.4 %collective-permute-start.12 = (f32[5,16,10,1]{1,3,2,0:T(1,128)S(1)}, f32[5,16,10,1]{1,3,2,0:T(1,128)S(1)}, u32[]{:S(2)}, u32[]{:S(2)}) collective-permute-start(f32[5,16,10,1]{1,3,2,0:T(1,128)S(1)} %copy.113), channel_id=1, source_target_pairs={{1,0},{2,1},{3,2},{4,3},{5,4},{6,5},{7,6},{9,8},{10,9},{11,10},{12... | collective-permute-start | bytes 9608 | tf_op jit(solution)/shard_map/ppermute | solution.py:27
  508.8 11.6 %copy-start.6 = (f32[16,8,128]{2,1,0:T(8,128)S(1)}, f32[16,8,128]{2,1,0:T(8,128)}, u32[]{:S(2)}) copy-start(f32[16,8,128]{2,1,0:T(8,128)} %get-tuple-element.80) | copy-start | bytes 196612
  510.7 11.6 %copy-start.2 = (f32[16,8,128,5]{2,3,1,0:T(8,128)S(1)}, f32[16,8,128,5]{2,3,1,0:T(8,128)}, u32[]{:S(2)}) copy-start(f32[16,8,128,5]{2,3,1,0:T(8,128)} %fusion.3) | copy-start | bytes 983044
  510.7 11.6 %copy-start.5 = (f32[16,8,128]{2,1,0:T(8,128)S(1)}, f32[16,8,128]{2,1,0:T(8,128)}, u32[]{:S(2)}) copy-start(f32[16,8,128]{2,1,0:T(8,128)} %get-tuple-element.78) | copy-start | bytes 196612
  524.7 6.0 collective-permute-start.15
  528.2 7.7 %collective-permute-start.14 = (f32[5,16,1,128]{3,0,2,1:T(8,128)S(1)}, f32[5,16,1,128]{3,0,2,1:T(8,128)S(1)}, u32[]{:S(2)}, u32[]{:S(2)}) collective-permute-start(f32[5,16,1,128]{3,0,2,1:T(8,128)S(1)} %get-tuple-element.75), channel_id=1, source_target_pairs={{8,0},{16,8},{24,16},{32,24},{40,32},{48,40},{56,48},{64,56},{72,6... | collective-permute-start | bytes 122888 | tf_op jit(solution)/shard_map/ppermute | solution.py:27
  530.8 13.1 %copy-start.14 = (f32[5,16,1,128]{3,0,2,1:T(8,128)}, f32[5,16,1,128]{3,0,2,1:T(8,128)S(1)}, u32[]{:S(2)}) copy-start(f32[5,16,1,128]{3,0,2,1:T(8,128)S(1)} %collective-permute-done.15) | copy-start | bytes 122884
  536.0 7.9 %copy-start.25 = (f32[1,5,5]{2,0,1:T(1,128)S(1)}, f32[1,5,5]{2,0,1:T(1,128)}, u32[]{:S(2)}) copy-start(f32[1,5,5]{2,0,1:T(1,128)} %get-tuple-element.84) | copy-start | bytes 304
  536.9 7.6 %collective-permute-start.17 = (f32[5,16,10,1]{1,3,2,0:T(1,128)S(1)}, f32[5,16,10,1]{1,3,2,0:T(1,128)}, u32[]{:S(2)}, u32[]{:S(2)}) collective-permute-start(f32[5,16,10,1]{1,3,2,0:T(1,128)S(1)} %copy.121), channel_id=1, source_target_pairs={{0,1},{1,2},{2,3},{3,4},{4,5},{5,6},{6,7},{8,9},{9,10},{10,11},{11... | collective-permute-start | bytes 9608 | tf_op jit(solution)/shard_map/ppermute | solution.py:25
  541.8 15.7 %collective-permute-start.16 = (f32[5,16,10,1]{1,3,2,0:T(1,128)}, f32[5,16,10,1]{1,3,2,0:T(1,128)}, u32[]{:S(2)}, u32[]{:S(2)}) collective-permute-start(f32[5,16,10,1]{1,3,2,0:T(1,128)} %copy.119), channel_id=1, source_target_pairs={{1,0},{2,1},{3,2},{4,3},{5,4},{6,5},{7,6},{9,8},{10,9},{11,10},{12... | collective-permute-start | bytes 9608 | tf_op jit(solution)/shard_map/ppermute | solution.py:27
  561.7 5.8 collective-permute-start.19
  565.0 7.7 %collective-permute-start.18 = (f32[5,16,1,128]{3,0,2,1:T(8,128)S(1)}, f32[5,16,1,128]{3,0,2,1:T(8,128)S(1)}, u32[]{:S(2)}, u32[]{:S(2)}) collective-permute-start(f32[5,16,1,128]{3,0,2,1:T(8,128)S(1)} %get-tuple-element.73), channel_id=1, source_target_pairs={{8,0},{16,8},{24,16},{32,24},{40,32},{48,40},{56,48},{64,56},{72,6... | collective-permute-start | bytes 122888 | tf_op jit(solution)/shard_map/ppermute | solution.py:27
  574.0 7.0 %collective-permute-start.21 = (f32[5,16,10,1]{1,3,2,0:T(1,128)S(1)}, f32[5,16,10,1]{1,3,2,0:T(1,128)S(1)}, u32[]{:S(2)}, u32[]{:S(2)}) collective-permute-start(f32[5,16,10,1]{1,3,2,0:T(1,128)S(1)} %copy.125), channel_id=1, source_target_pairs={{0,1},{1,2},{2,3},{3,4},{4,5},{5,6},{6,7},{8,9},{9,10},{10,11},{11... | collective-permute-start | bytes 9608 | tf_op jit(solution)/shard_map/ppermute | solution.py:25
  578.1 15.7 %collective-permute-start.20 = (f32[5,16,10,1]{1,3,2,0:T(1,128)}, f32[5,16,10,1]{1,3,2,0:T(1,128)}, u32[]{:S(2)}, u32[]{:S(2)}) collective-permute-start(f32[5,16,10,1]{1,3,2,0:T(1,128)} %copy.123), channel_id=1, source_target_pairs={{1,0},{2,1},{3,2},{4,3},{5,4},{6,5},{7,6},{9,8},{10,9},{11,10},{12... | collective-permute-start | bytes 9608 | tf_op jit(solution)/shard_map/ppermute | solution.py:27
  581.0 13.9 %copy-start.7 = (f32[16,8,128]{2,1,0:T(8,128)S(1)}, f32[16,8,128]{2,1,0:T(8,128)}, u32[]{:S(2)}) copy-start(f32[16,8,128]{2,1,0:T(8,128)} %get-tuple-element.80) | copy-start | bytes 196612
  598.1 5.9 collective-permute-start.23
  601.4 8.0 %collective-permute-start.22 = (f32[5,16,1,128]{3,0,2,1:T(8,128)S(1)}, f32[5,16,1,128]{3,0,2,1:T(8,128)S(1)}, u32[]{:S(2)}, u32[]{:S(2)}) collective-permute-start(f32[5,16,1,128]{3,0,2,1:T(8,128)S(1)} %get-tuple-element.71), channel_id=1, source_target_pairs={{8,0},{16,8},{24,16},{32,24},{40,32},{48,40},{56,48},{64,56},{72,6... | collective-permute-start | bytes 122888 | tf_op jit(solution)/shard_map/ppermute | solution.py:27
  603.9 13.8 %copy-start.13 = (f32[5,16,1,128]{3,0,2,1:T(8,128)}, f32[5,16,1,128]{3,0,2,1:T(8,128)S(1)}, u32[]{:S(2)}) copy-start(f32[5,16,1,128]{3,0,2,1:T(8,128)S(1)} %collective-permute-done.23) | copy-start | bytes 122884
  610.3 7.9 %copy-start.12 = (f32[5,16,1,128]{3,0,2,1:T(8,128)S(1)}, f32[5,16,1,128]{3,0,2,1:T(8,128)}, u32[]{:S(2)}) copy-start(f32[5,16,1,128]{3,0,2,1:T(8,128)} %copy-done.11) | copy-start | bytes 122884
  610.7 7.1 %collective-permute-start.25 = (f32[5,16,10,1]{1,3,2,0:T(1,128)S(1)}, f32[5,16,10,1]{1,3,2,0:T(1,128)S(1)}, u32[]{:S(2)}, u32[]{:S(2)}) collective-permute-start(f32[5,16,10,1]{1,3,2,0:T(1,128)S(1)} %copy.129), channel_id=1, source_target_pairs={{0,1},{1,2},{2,3},{3,4},{4,5},{5,6},{6,7},{8,9},{9,10},{10,11},{11... | collective-permute-start | bytes 9608 | tf_op jit(solution)/shard_map/ppermute | solution.py:25
  613.6 15.7 %collective-permute-start.24 = (f32[5,16,10,1]{1,3,2,0:T(1,128)}, f32[5,16,10,1]{1,3,2,0:T(1,128)}, u32[]{:S(2)}, u32[]{:S(2)}) collective-permute-start(f32[5,16,10,1]{1,3,2,0:T(1,128)} %copy.127), channel_id=1, source_target_pairs={{1,0},{2,1},{3,2},{4,3},{5,4},{6,5},{7,6},{9,8},{10,9},{11,10},{12... | collective-permute-start | bytes 9608 | tf_op jit(solution)/shard_map/ppermute | solution.py:27
  (21 other events, 90.3 us)
where the time goes:
time: 643 us; the launch traced here: 633 us
  blocking collectives  341 us (53%)
  starting transfers between devices  132 us (21%)
  waiting for transfers between devices  62.9 us (10%)
  local copies, waits for them, and re-layouts  44.4 us (7%)
  matrix products  26.3 us (4%)
  other arithmetic  22.7 us (4%)
    psum x3, blocking collectives, per_device(): stiff_total = lax.psum(local_forces, 'chord')  341 us
    ppermute x9, waiting for transfers between devices, with_halo(): lax.ppermute(head, axis, [((i + 1) % count, i) for i in range(ends)])  60.6 us
    ppermute x8, starting transfers between devices, shifted(): lax.ppermute(value, axis, [(source, source + steps) for source in range(i...  60.6 us
    ppermute x9, starting transfers between devices, with_halo(): lax.ppermute(tail, axis, [(i, (i + 1) % count) for i in range(ends)])  52.4 us
    ppermute x9, starting transfers between devices, with_halo(): lax.ppermute(head, axis, [((i + 1) % count, i) for i in range(ends)])  19.4 us
    dot_general x12, matrix products, relax_cells(): jnp.einsum('ij,jnsc->insc', downwind[direction], backward, precision=lax....  13.2 us
  transfers between devices with their start and end apart: 26, of which 11 were waited for; matrix products, arithmetic and copies ran while one was open for 11% of the time, Pallas kernels for 0%

commit v1 on v0

v1 whole, which is shorter than its diff:
```python
import functools

import jax
import jax.numpy as jnp
from jax import lax
from jax.experimental import pallas as pl
from jax.experimental.pallas import tpu as pltpu
from jax.sharding import Mesh
from jax.sharding import PartitionSpec as P


F32 = jnp.float32
BF16 = jnp.bfloat16
NB = 64
SW = 4
LAYERS = 16
NODE_DEV = 1024
TILES = 9
EXT = TILES * 128
PLANES = 228
HALF = PLANES // 2
FIELDS = 15
SLOTS = 2 * PLANES
WIDTH = 4
PACKED = 49
BLOCKS = ((0, 0), (1, 0), (1, 1), (2, 0), (2, 1), (2, 2))
VM = pl.BlockSpec(memory_space=pltpu.VMEM)
SM = pl.BlockSpec(memory_space=pltpu.SMEM)
PARAMS = pltpu.CompilerParams(vmem_limit_bytes=48 << 20)


def call(body, out, ins, specs, flops, scratch=(), aliases=None):
    return pl.pallas_call(
        body,
        out_shape=out,
        in_specs=specs,
        out_specs=jax.tree.map(lambda _: VM, out),
        scratch_shapes=list(scratch),
        input_output_aliases=aliases or {},
        compiler_params=PARAMS,
        cost_estimate=pl.CostEstimate(flops=flops, bytes_accessed=flops // 8, transcendentals=0),
    )(*ins)


def sds(*shape):
    return jax.ShapeDtypeStruct(shape, F32)


def iota(shape, dim):
    return lax.broadcasted_iota(jnp.int32, shape, dim)


def front_kernel(
    span, count, state, grad, diag, coup, normal, fnode, stiff, conn, shell_in, sgrad_in, precond_in,
    pack, rim, planes, up, down, shell, sgrad, precond, inverse, faces, elems, sems,
):
    moves = []

    def move(source, target):
        copy = pltpu.make_async_copy(source, target, sems.at[len(moves)])
        copy.start()
        moves.append(copy)

    move(shell_in, shell)
    move(sgrad_in, sgrad)
    move(precond_in, precond)
    move(conn, elems)
    move(fnode, faces)
    move(normal, planes.at[pl.ds(224, 3)])
    move(diag, inverse)
    for j in range(5):
        move(state.at[j], planes.at[pl.ds(16 * j, 16)])
        move(grad.at[j], planes.at[pl.ds(80 + 16 * j, 16)])
    for k in range(3):
        move(coup.at[k], planes.at[pl.ds(176 + 16 * k, 16)])
    early = len(moves)
    for b, (bj, bi) in enumerate(BLOCKS):
        move(stiff.at[pl.ds(8 * bj, 8), pl.ds(8 * bi, 8)], pack.at[pl.ds(8 * b, 8)])
    for copy in moves[:early]:
        copy.wait()
    pack[48] = jnp.zeros((8, 128), F32)
    pack[48, 0:4] = (elems[...] - span[0] * NODE_DEV).astype(F32)
    lead = iota((6, 128), 1) < NB
    zero = jnp.zeros((6, 128), F32)
    rim[0:6, :] = jnp.where(lead, shell[:, 0:128], zero)
    rim[6:12, :] = jnp.where(lead, sgrad[:, 0:128], zero)
    for i in range(6):
        rim[12 + 6 * i : 18 + 6 * i, :] = jnp.where(lead, precond[i, :, 0:128], zero)
    planes[160:176] = 1.0 / inverse[...]
    active = iota((8, 128), 0) * 128 + iota((8, 128), 1) < count[0, 0]
    for i in range(3):
        planes[224 + i] = jnp.where(active, planes[224 + i], 0.0)
    planes[227] = faces[...].astype(F32)
    low = iota((8, 128), 0) < 4

    def body(k, carry):
        a, b = planes[k], planes[k + HALF]
        up[k] = jnp.where(low, pltpu.roll(a, 4, 0), b)
        down[k] = jnp.where(low, a, pltpu.roll(b, 4, 0))
        return carry

    lax.fori_loop(0, HALF, body, 0, unroll=6)
    for copy in moves[early:]:
        copy.wait()


def parts(value):
    high = value.astype(BF16).astype(F32)
    return jnp.concatenate([high, value - high], axis=0).astype(BF16)


def stiff_apply(field, packs, onehot, uvec, fvec):
    for q, pack in enumerate(packs):
        for a in range(4):
            row = pack[48, a : a + 1, :].astype(jnp.int32)
            lane = (4 * q + a) * 128
            hit = iota((EXT, 128), 0) == row
            onehot[:, lane : lane + 128] = jnp.where(hit, 1.0, 0.0).astype(BF16)
    picked = jnp.dot(parts(field), onehot[...], preferred_element_type=F32)
    picked = picked[0:8] + picked[8:16]
    for q, pack in enumerate(packs):
        for a in range(4):
            lane = (4 * q + a) * 128
            uvec[6 * a : 6 * a + 6, :] = picked[0:6, lane : lane + 128]
        out = [jnp.zeros((8, 128), F32) for _ in range(3)]
        for b, (bj, bi) in enumerate(BLOCKS):
            for j in range(8):
                rows = pack[8 * b + j]
                out[bi] = out[bi] + rows * uvec[8 * bj + j : 8 * bj + j + 1, :]
            if bj != bi:
                for i in range(8):
                    rows = pack[8 * b : 8 * b + 8, i, :]
                    out[bj] = out[bj] + rows * uvec[8 * bi + i : 8 * bi + i + 1, :]
        for b in range(3):
            uvec[8 * b : 8 * b + 8, :] = out[b]
        for a in range(4):
            lane = (4 * q + a) * 128
            fvec[0:6, lane : lane + 128] = uvec[6 * a : 6 * a + 6, :]
            fvec[6:8, lane : lane + 128] = jnp.zeros((2, 128), F32)
    forces = lax.dot_general(
        parts(fvec[...]), onehot[...], (((1,), (1,)), ((), ())), preferred_element_type=F32
    )
    return forces[0:8] + forces[8:16]


def first_kernel(
    span, prow, planes, shell, rim, pack,
    own, up, down, down2, faces, nodes, loads, field, onehot, uvec, fvec,
):
    press = prow[0] * planes[0]
    for j in range(1, 5):
        press = press + prow[j] * planes[16 * j]
    local = planes[227].astype(jnp.int32) - (span[0] - 1) * NODE_DEV
    faces[...] = jnp.zeros((8, 1024), F32)
    for r in range(8):
        nodes[0:1, r * 128 : r * 128 + 128] = local[r : r + 1]
    for i in range(3):
        load = planes[224 + i] * press
        for r in range(8):
            faces[i : i + 1, r * 128 : r * 128 + 128] = load[r : r + 1]
    face_parts = parts(faces[...])
    node_row = nodes[0:1, :]

    def chunk(b, carry):
        hit = iota((256, 1024), 0) + b * 256 == node_row
        hot = jnp.where(hit, 1.0, 0.0).astype(BF16)
        got = lax.dot_general(
            face_parts, hot, (((1,), (1,)), ((), ())), preferred_element_type=F32
        )
        got = got[0:8] + got[8:16]
        loads[2 * b] = got[:, 0:128]
        loads[2 * b + 1] = got[:, 128:256]
        return carry

    lax.fori_loop(0, 12, chunk, 0)
    field[...] = jnp.zeros((8, EXT), F32)
    field[0:6, 0:NODE_DEV] = shell[...]
    field[0:6, NODE_DEV:EXT] = rim[0:6, :]
    force = stiff_apply(field[...], (pack,), onehot, uvec, fvec)
    lead = iota((8, 128), 1) < NB
    for t in range(8):
        own[t] = force[:, t * 128 : t * 128 + 128] + loads[8 + t]
        up[t] = loads[16 + t]
        down[t] = loads[t]
    edge = force[:, NODE_DEV:EXT]
    own[8] = edge + jnp.where(lead, loads[16], 0.0)
    up[8] = edge
    down[8] = jnp.where(lead, force[:, 0:128] + loads[8], 0.0)
    down2[...] = jnp.where(lead, loads[0], 0.0)


def precondition(t, precond, rim, res):
    rows = []
    for i in range(6):
        if t < 8:
            block = precond[i, :, t * 128 : t * 128 + 128]
        else:
            block = rim[12 + 6 * i : 18 + 6 * i, :]
        rows.append(jnp.sum(block * res[0:6], axis=0, keepdims=True))
    rows.append(jnp.zeros((2, 128), F32))
    return jnp.concatenate(rows, axis=0)


def shell_residual(first, t, ins):
    if first:
        total, remote, sgrad, rim = ins
        base = sgrad[:, t * 128 : t * 128 + 128] if t < 8 else rim[6:12, :]
        base = jnp.concatenate([base, jnp.zeros((2, 128), F32)], axis=0)
        return base - total[t] - remote[PACKED + t]
    force, rise, fall, prev = ins
    res = prev[t] - force[t]
    if t == 0:
        res = res - rise[...]
    return res - fall[...] if t == 8 else res


def step_kernel(first, *refs):
    refs, (res_out, sum_out, force_out, field, onehot, uvec, fvec) = refs[:-7], refs[-7:]
    own_pack, far_pack, rim, precond, prev_sum = refs[:5]
    for t in range(TILES):
        res = shell_residual(first, t, refs[5:])
        res_out[t] = res
        delta = precondition(t, precond, rim, res)
        sum_out[t] = delta if first else prev_sum[t] + delta
        field[:, t * 128 : t * 128 + 128] = delta
    force = stiff_apply(field[...], (own_pack, far_pack), onehot, uvec, fvec)
    for t in range(TILES):
        force_out[t] = force[:, t * 128 : t * 128 + 128]


def last_kernel(*refs):
    refs, (shell_out, reach_out) = refs[:-2], refs[-2:]
    shell, rim, precond, prev_sum = refs[:4]
    for t in range(8):
        delta = precondition(t, precond, rim, shell_residual(False, t, refs[4:]))
        value = shell[:, t * 128 : t * 128 + 128] + (prev_sum[t] + delta)[0:6]
        shell_out[:, t * 128 : t * 128 + 128] = value
        for i in range(3):
            reach_out[8 * i + t : 8 * i + t + 1, :] = value[i : i + 1]


def pack_chord_kernel(planes, from_lower, from_upper, full, edges):
    low = iota((8, 128), 0) < 4
    full[0:PLANES] = planes[...]

    def unpack(k, carry):
        a, b = from_upper[k], from_lower[k]
        full[PLANES + k] = jnp.where(low, a, pltpu.roll(b, 4, 0))
        full[PLANES + HALF + k] = jnp.where(low, pltpu.roll(a, 4, 0), b)
        return carry

    lax.fori_loop(0, HALF, unpack, 0, unroll=6)
    lane = iota((16, 128), 1)

    def columns(field, count):
        packed = jnp.zeros((16, 128), F32)
        for n in range(count):
            k = 16 * field + n
            value = jnp.concatenate([full[k], full[PLANES + k]], axis=0)
            value = jnp.where(lane < WIDTH, value, pltpu.roll(value, 8, 1))
            value = pltpu.roll(value, 8 * n, 1) if n else value
            packed = jnp.where(lane // 8 == n, value, packed)
        edges[field] = packed

    def one(field, carry):
        columns(field, LAYERS)
        return carry

    lax.fori_loop(0, FIELDS - 1, one, 0)
    columns(FIELDS - 1, 4)


def fluxes(coefs, pairs, upwind, downwind):
    total = [None] * 5
    for k in range(3):
        flux = [None] * 5
        for j in range(5):
            ahead, behind = pairs[k](j)
            for i in range(5):
                term = upwind[k, i, j] * ahead + downwind[k, i, j] * behind
                flux[i] = term if j == 0 else flux[i] + term
        for i in range(5):
            term = coefs[k] * flux[i]
            total[i] = term if k == 0 else total[i] + term
    return total


def sweep(slot, layers, state, halo, first, last, rolled, coef, source, edge_coef, edge_source,
          upwind, downwind, own=None):
    lane = iota((16, 128), 1)

    def layer(n, carry):
        shift = 8 * n
        for j in range(5):
            value, side = state[slot, j, n + 1], halo[slot, j]
            rolled[j, 0] = pltpu.roll(value, 15, 0)
            rolled[j, 1] = pltpu.roll(value, 1, 0)
            rolled[j, 2] = jnp.where(
                lane == 127, pltpu.roll(side, 127 - shift, 1), pltpu.roll(value, 127, 1)
            )
            rolled[j, 3] = jnp.where(
                lane == 0, pltpu.roll(side, 121 - shift, 1), pltpu.roll(value, 1, 1)
            )
            if own is None:
                first[j] = jnp.where(lane == shift + 7, pltpu.roll(value, shift + 7, 1), first[j])
                last[j] = jnp.where(lane == shift, pltpu.roll(value, shift + 1, 1), last[j])
        rows = slice(0, 8) if own is not None else slice(0, 16)
        pairs = (
            lambda j: (state[slot, j, n + 2, rows], state[slot, j, n, rows]),
            lambda j: (rolled[j, 0, rows], rolled[j, 1, rows]),
            lambda j: (rolled[j, 2, rows], rolled[j, 3, rows]),
        )
        total = fluxes([coef(1 + k, n)[rows] for k in range(3)], pairs, upwind, downwind)
        for i in range(5):
            value = coef(0, n)[rows] * (source(i, n)[rows] + total[i])
            if own is not None:
                own(i, n, value)
            else:
                state[1 - slot, i, n + 1] = value
        return carry

    lax.fori_loop(0, layers, layer, 0)
    if own is not None:
        return
    pairs = (
        lambda j: (
            jnp.where(lane < 120, pltpu.roll(halo[slot, j], 120, 1), 0.0),
            jnp.where(lane >= 8, pltpu.roll(halo[slot, j], 8, 1), 0.0),
        ),
        lambda j: (pltpu.roll(halo[slot, j], 15, 0), pltpu.roll(halo[slot, j], 1, 0)),
        lambda j: (
            jnp.where(lane % 8 == 7, first[j], pltpu.roll(halo[slot, j], 127, 1)),
            jnp.where(lane % 8 == 0, last[j], pltpu.roll(halo[slot, j], 1, 1)),
        ),
    )
    total = fluxes([edge_coef(1 + k) for k in range(3)], pairs, upwind, downwind)
    for i in range(5):
        halo[1 - slot, i] = edge_coef(0) * (edge_source(i) + total[i])


def tall(full, k):
    return jnp.concatenate([full[k], full[PLANES + k]], axis=0)


def coef_of(full):
    return lambda k, n: tall(full, 160 + 16 * k + n)


def base_kernel(
    odd, full, near, far, upwind, downwind, out, edge_out, state, halo, first, last, rolled
):
    lane = iota((16, 128), 1)
    right = lane % 8 < WIDTH
    even = odd[0] == 0
    for field in range(FIELDS):
        x, y = near[field], far[field]
        edge_out[field] = jnp.where(right, jnp.where(even, x, y), jnp.where(even, y, x))
    for slot in range(2):
        for j in range(5):
            state[slot, j, 0] = jnp.zeros((16, 128), F32)
            state[slot, j, LAYERS + 1] = jnp.zeros((16, 128), F32)
    for j in range(5):
        halo[0, j] = edge_out[j]
        first[j] = jnp.zeros((16, 128), F32)
        last[j] = jnp.zeros((16, 128), F32)

    def start(n, carry):
        for j in range(5):
            state[0, j, n + 1] = tall(full, 16 * j + n)
        return carry

    lax.fori_loop(0, LAYERS, start, 0)

    def store(i, n, value):
        out[i, n] = value

    for turn in range(SW):
        sweep(
            turn % 2, LAYERS, state, halo, first, last, rolled,
            coef_of(full), lambda i, n: tall(full, 80 + 16 * i + n),
            lambda k: edge_out[10 + k], lambda i: edge_out[5 + i],
            upwind, downwind, store if turn == SW - 1 else None,
        )


def final_kernel(
    span, prow, upwind, downwind, base, full, edges, r0, r1, r2, r3, r4,
    out, reach, state, halo, first, last, rolled,
):
    for b, ref in enumerate((r0, r1, r2, r3, r4)):
        for i in range(3):
            reach[40 * i + 8 * b : 40 * i + 8 * b + 8, :] = ref[8 * i : 8 * i + 8, :]
    walls = edges[FIELDS - 1]
    wall_planes = [pltpu.roll(walls, 128 - 8 * i, 1) if i else walls for i in range(4)]
    node = jnp.concatenate([tall(full, 227), wall_planes[3]], axis=0)
    index = node.astype(jnp.int32) - (span[0] - 2) * NODE_DEV
    block, low = index >> 7, index & 127
    blocks = [block[8 * q : 8 * q + 8] for q in range(4)]
    lows = [low[8 * q : 8 * q + 8] for q in range(4)]

    def pick(h, got):
        got = list(got)
        for i in range(3):
            row = jnp.broadcast_to(reach[pl.ds(40 * i + h, 1), :], (8, 128))
            for q in range(4):
                value = jnp.take_along_axis(row, lows[q], axis=1)
                got[4 * i + q] = jnp.where(blocks[q] == h, value, got[4 * i + q])
        return tuple(got)

    got = lax.fori_loop(
        0, 40, pick, tuple(jnp.zeros((8, 128), F32) for _ in range(12)), unroll=4
    )
    lane = iota((16, 128), 1)
    disp = sum(tall(full, 224 + i) * jnp.concatenate(got[4 * i : 4 * i + 2], axis=0) for i in range(3))
    side = sum(wall_planes[i] * jnp.concatenate(got[4 * i + 2 : 4 * i + 4], axis=0) for i in range(3))
    side = jnp.where(lane < 8, side, 0.0)
    state[...] = jnp.zeros(state.shape, F32)
    for j in range(5):
        state[0, j, 1] = tall(full, 160) * (-prow[j] * disp)
        halo[0, j] = edges[10] * (-prow[j] * side)
        first[j] = jnp.zeros((16, 128), F32)
        last[j] = jnp.zeros((16, 128), F32)
    out[...] = base[...]

    def store(i, n, value):
        out[i, n] = base[i, n] + value

    for turn in range(1, SW):
        sweep(
            (turn + 1) % 2, turn + 1, state, halo, first, last, rolled,
            coef_of(full), lambda i, n: (-prow[i] * jnp.where(n == 0, 1.0, 0.0)) * disp,
            lambda k: edges[10 + k], lambda i: -prow[i] * side,
            upwind, downwind, store if turn == SW - 1 else None,
        )


def along_span(value, steps):
    count = lax.axis_size("span")
    first, last = max(0, -steps), min(count, count - steps)
    return lax.ppermute(value, "span", [(i, i + steps) for i in range(first, last)])


CHORD = ("far_z", "y")


def swap(value, bit):
    count = lax.axis_size(CHORD)
    return lax.ppermute(value, CHORD, [(c, c ^ bit) for c in range(count)])


def ring_sum(value):
    count = lax.axis_size("y")
    pieces = lax.all_to_all(jnp.broadcast_to(value[None], (count, *value.shape)), "y", 0, 0)
    return pieces.sum(0)


def per_device(
    adjoint_flow, flow_grad, diagonal, couplings, upwind, downwind, pressure_row, face_normal,
    face_node, face_count, adjoint_shell, shell_grad, node_precond, element_stiffness, connectivity,
):
    span = lax.axis_index("span").astype(jnp.int32).reshape(1)
    odd = (lax.axis_index("y") % 2).astype(jnp.int32).reshape(1)
    pack, rim, planes, to_upper, to_lower, shell, sgrad, precond = call(
        front_kernel,
        (
            sds(PACKED, 8, 128), sds(48, 128), sds(PLANES, 8, 128), sds(HALF, 8, 128),
            sds(HALF, 8, 128), sds(6, NODE_DEV), sds(6, NODE_DEV), sds(6, 6, NODE_DEV),
        ),
        (
            span, face_count, adjoint_flow, flow_grad, diagonal, couplings, face_normal, face_node,
            element_stiffness, connectivity, adjoint_shell, shell_grad, node_precond,
        ),
        [SM] * 2 + [pl.BlockSpec(memory_space=pltpu.MemorySpace.HBM)] * 11,
        4 << 20,
        (
            pltpu.VMEM((LAYERS, 8, 128), F32), pltpu.VMEM((8, 128), jnp.int32),
            pltpu.VMEM((4, 128), jnp.int32), pltpu.SemaphoreType.DMA((32,)),
        ),
    )
    rim = along_span(rim, -1)
    from_lower, from_upper = along_span(to_upper, 1), along_span(to_lower, -1)
    apply_scratch = lambda nb: (
        pltpu.VMEM((8, EXT), F32),
        pltpu.VMEM((EXT, 512 * nb), BF16),
        pltpu.VMEM((24, 128), F32),
        pltpu.VMEM((8, 512 * nb), F32),
    )
    own, up, down, down2 = call(
        first_kernel,
        (sds(TILES, 8, 128), sds(TILES, 8, 128), sds(TILES, 8, 128), sds(8, 128)),
        (span, pressure_row, planes, shell, rim, pack),
        [SM] * 2 + [VM] * 4,
        8 << 20,
        (pltpu.VMEM((8, 1024), F32), pltpu.VMEM((8, 1024), jnp.int32), pltpu.VMEM((24, 8, 128), F32))
        + apply_scratch(1),
    )
    up, down, down2 = along_span(up, 1), along_span(down, -1), along_span(down2, -2)
    full, edges = call(
        pack_chord_kernel,
        (sds(SLOTS, 8, 128), sds(FIELDS, 16, 128)),
        (planes, from_lower, from_upper),
        [VM] * 3,
        4 << 20,
    )
    near = swap(edges, 1)
    total = own + jnp.concatenate([up[:8] + down[:8], (down[8] + down2)[None]], axis=0)
    total = ring_sum(total.at[0].add(up[8]))
    scratch = lambda layers: (
        pltpu.VMEM((2, 5, layers + 2, 16, 128), F32),
        pltpu.VMEM((2, 5, 16, 128), F32),
        pltpu.VMEM((5, 16, 128), F32),
        pltpu.VMEM((5, 16, 128), F32),
        pltpu.VMEM((5, 4, 16, 128), F32),
    )
    count = lax.axis_size(CHORD)
    pairs = [(c, c - 1 + 2 * (c % 2)) for c in range(1, count - 1)]
    remote = swap(jnp.concatenate([pack, total], axis=0), 4)
    far = lax.ppermute(edges, CHORD, pairs)
    base, edges = call(
        base_kernel,
        (sds(5, LAYERS, 8, 128), sds(FIELDS, 16, 128)),
        (odd, full, near, far, upwind, downwind),
        [SM] + [VM] * 3 + [SM] * 2,
        16 << 20,
        scratch(LAYERS),
    )
    pieces = (total, remote, sgrad, rim)
    res = sums = total
    lead = jnp.arange(128) < NB
    for turn in range(2):
        res, sums, force = call(
            functools.partial(step_kernel, turn == 0),
            (sds(TILES, 8, 128),) * 3,
            (pack, remote if turn == 0 else far_pack, rim, precond, sums) + pieces,
            [VM] * (5 + len(pieces)),
            8 << 20,
            apply_scratch(2),
        )
        far_pack = remote if turn == 0 else far_pack
        force = ring_sum(force)
        rise = along_span(force[8], 1)
        fall = along_span(jnp.where(lead, force[0], 0.0), -1)
        pieces = (force, rise, fall, res)
    shell, reach = call(
        last_kernel,
        (sds(6, NODE_DEV), sds(24, 128)),
        (shell, rim, precond, sums) + pieces,
        [VM] * (4 + len(pieces)),
        1 << 20,
    )
    reaches = [along_span(reach, k) for k in (2, 1)] + [reach] + [along_span(reach, -k) for k in (1, 2)]
    flow = call(
        final_kernel,
        sds(5, LAYERS, 8, 128),
        (span, pressure_row, upwind, downwind, base, full, edges, *reaches),
        [SM] * 4 + [VM] * 8,
        8 << 20,
        (pltpu.VMEM((120, 128), F32), *scratch(SW)),
    )
    return flow, shell


def solution(mesh):
    spans, chords = mesh.devices.shape
    split = Mesh(mesh.devices.reshape(spans, 2, chords // 2), ("span", *CHORD))
    return jax.shard_map(
        per_device,
        mesh=split,
        in_specs=(
            P(None, None, "span", CHORD),
            P(None, None, "span", CHORD),
            P(None, "span", CHORD),
            P(None, None, "span", CHORD),
            P(),
            P(),
            P(),
            P(None, "span", CHORD),
            P("span", CHORD),
            P("span", CHORD),
            P(None, "span"),
            P(None, "span"),
            P(None, None, "span"),
            P(None, None, ("span", *CHORD)),
            P(None, ("span", *CHORD)),
        ),
        out_specs=(P(None, None, "span", CHORD), P(None, "span")),
        check_vma=False,
    )
```

time: 643 us -> 174 us (0.27)
  the two profiles are of different devices: /device:TPU:223 before, /device:TPU:56 now
where the time goes in v1:
time: 174 us; the launch traced here: 172 us
  starting transfers between devices  86.1 us (49%)
  Pallas kernels  31.2 us (18%)
  waiting for transfers between devices  28.1 us (16%)
  local copies, waits for them, and re-layouts  15.8 us (9%)
  blocking collectives  8.48 us (5%)
    ppermute x14, starting transfers between devices, along_span(): lax.ppermute(value, 'span', [(i, i + steps) for i in range(first, last)])  43.5 us
    pallas_call x8, Pallas kernels, call(): pl.pallas_call(body, out_shape=out, in_specs=specs, out_specs=jax.tree.ma...  31.2 us
    ppermute x2, starting transfers between devices, swap(): return lax.ppermute(value, CHORD, [(c, c ^ bit) for c in range(count)])  18.5 us
    unnamed x44, local copies, waits for them, and re-layouts  14.4 us
    ppermute x14, waiting for transfers between devices, along_span(): lax.ppermute(value, 'span', [(i, i + steps) for i in range(first, last)])  13.9 us
    ppermute x1, starting transfers between devices, per_device(): far = lax.ppermute(edges, CHORD, pairs)  12.7 us
    all_to_all x2, starting transfers between devices, ring_sum(): lax.all_to_all(jnp.broadcast_to(value[None], (count, *value.shape)), 'y',...  11.5 us
    ppermute x2, waiting for transfers between devices, swap(): return lax.ppermute(value, CHORD, [(c, c ^ bit) for c in range(count)])  10.2 us
  transfers between devices with their start and end apart: 19, of which 6 were waited for; matrix products, arithmetic and copies ran while one was open for 1% of the time, Pallas kernels for 11%

profile of v1, /device:TPU:56, one launch (start us, length us, event | category | flops | bytes accessed | tf_op | source)
XLA Modules:
  0.0 172.3 jit_solution(13191273876671099016)
XLA Ops:
  1.3 1.0 copy-done.2
  2.3 1.0 copy-done.3
  3.2 1.0 copy-done.4
  4.2 0.9 copy-done.5
  5.1 0.9 copy-done.6
  6.1 0.8 copy-done.7
  6.9 0.8 copy-done.12
  7.6 0.8 copy-done.13
  8.4 0.7 copy-done.14
  10.5 3.0 %shard_map.158 = (f32[49,8,128]{2,1,0:T(8,128)S(1)}, f32[48,128]{1,0:T(8,128)S(1)}, f32[228,8,128]{2,1,0:T(8,128)S(1)}, f32[114,8,128]{2,1,0:T(8,128)}, f32[114,...) custom-call(s32[1]{0:T(128)} %bitcast.span, ...), custom_call_target="tpu_custom_call" | custom-call | flops 4194304 | bytes 524288 | tf_op jit(solution)/shard_map/pallas_call | solution.py:33
  13.5 3.7 %collective-permute-start.4 = (f32[48,128]{1,0:T(8,128)S(1)}, f32[48,128]{1,0:T(8,128)S(1)}, u32[]{:S(2)}, u32[]{:S(2)}) collective-permute-start(f32[48,128]{1,0:T(8,128)S(1)} %get-tuple-element.46), channel_id=1, source_target_pairs={{8,0},{16,8},{24,16},{32,24},{40,32},{48,40},{56,48},{64,56},{72,6... | collective-permute-start | bytes 73736 | tf_op jit(solution)/shard_map/ppermute | solution.py:440
  17.1 1.5 collective-permute-done.4.rim.refs_2_.refs_8_.refs_1_
  19.3 4.6 %shard_map.161 = (f32[9,8,128]{2,1,0:T(8,128)S(1)}, f32[9,8,128]{2,1,0:T(8,128)S(1)}, f32[9,8,128]{2,1,0:T(8,128)S(1)}, f32[8,128]{1,0:T(8,128)S(1)}) custom-call(s32[1]{0:T(128)} %bitcast.span, f32[5]{0:T(128)S(1)} %copy-done.17, f32[228,8,128]{2,1,0:T(8,128)S(1)} %get-tuple-element.38.planes, f32[6,1024]{1,0:T(8,128)S(1)} %get-tuple-element.45.shell.refs_0_, ...), custom_call_target="tpu_custom_call" | custom-call | flops 8388608 | bytes 1048576 | tf_op jit(solution)/shard_map/pallas_call | solution.py:33
  23.9 1.9 %collective-permute-start.5 = (f32[9,8,128]{2,1,0:T(8,128)S(1)}, f32[9,8,128]{2,1,0:T(8,128)S(1)}, u32[]{:S(2)}, u32[]{:S(2)}) collective-permute-start(f32[9,8,128]{2,1,0:T(8,128)S(1)} %get-tuple-element.50), channel_id=1, source_target_pairs={{0,8},{8,16},{16,24},{24,32},{32,40},{40,48},{48,56},{56,64},{64,7... | collective-permute-start | bytes 110600 | tf_op jit(solution)/shard_map/ppermute | solution.py:440
  25.9 5.8 %collective-permute-start.6 = (f32[9,8,128]{2,1,0:T(8,128)S(1)}, f32[9,8,128]{2,1,0:T(8,128)S(1)}, u32[]{:S(2)}, u32[]{:S(2)}) collective-permute-start(f32[9,8,128]{2,1,0:T(8,128)S(1)} %get-tuple-element.51), channel_id=1, source_target_pairs={{8,0},{16,8},{24,16},{32,24},{40,32},{48,40},{56,48},{64,56},{72,6... | collective-permute-start | bytes 110600 | tf_op jit(solution)/shard_map/ppermute | solution.py:440
  31.6 2.3 %collective-permute-start.7 = (f32[8,128]{1,0:T(8,128)S(1)}, f32[8,128]{1,0:T(8,128)S(1)}, u32[]{:S(2)}, u32[]{:S(2)}) collective-permute-start(f32[8,128]{1,0:T(8,128)S(1)} %get-tuple-element.52), channel_id=1, source_target_pairs={{16,0},{24,8},{32,16},{40,24},{48,32},{56,40},{64,48},{72,56},{80,... | collective-permute-start | bytes 12296 | tf_op jit(solution)/shard_map/ppermute | solution.py:440
  34.0 3.2 %collective-permute-done.7 = f32[8,128]{1,0:T(8,128)S(1)} collective-permute-done((f32[8,128]{1,0:T(8,128)S(1)}, f32[8,128]{1,0:T(8,128)S(1)}, u32[]{:S(2)}, u32[]{:S(2)}) %collective-permute-start.7) | collective-permute-done | bytes 4128 | tf_op jit(solution)/shard_map/ppermute | solution.py:440
  37.2 8.5 %all_to_all.15 = f32[4,9,8,128]{3,2,1,0:T(8,128)S(1)} all-to-all(f32[4,9,8,128]{3,2,1,0:T(8,128)S(1)} %broadcast_in_dim.34), channel_id=1, replica_groups=mesh['span'=64,'far_z'=2,'y'=4] {'y'}, dimensions={0} | all-to-all | bytes 294912 | tf_op jit(solution)/shard_map/all_to_all | solution.py:453
  45.7 15.7 %collective-permute-start.8 = (f32[58,8,128]{2,1,0:T(8,128)S(1)}, f32[58,8,128]{2,1,0:T(8,128)S(1)}, u32[]{:S(2)}, u32[]{:S(2)}) collective-permute-start(f32[58,8,128]{2,1,0:T(8,128)S(1)} %pad_maximum_fusion), channel_id=1, source_target_pairs={{0,4},{1,5},{2,6},{3,7},{4,0},{5,1},{6,2},{7,3},{8,12},{9,13},{10,... | collective-permute-start | bytes 712712 | tf_op jit(solution)/shard_map/ppermute | solution.py:448
  61.4 1.9 %collective-permute-start = (f32[114,8,128]{2,1,0:T(8,128)}, f32[114,8,128]{2,1,0:T(8,128)S(1)}, u32[]{:S(2)}, u32[]{:S(2)}) collective-permute-start(f32[114,8,128]{2,1,0:T(8,128)} %get-tuple-element.39), channel_id=1, source_target_pairs={{0,8},{8,16},{16,24},{24,32},{32,40},{40,48},{48,56},{56,64},{64,7... | collective-permute-start | bytes 1400840 | tf_op jit(solution)/shard_map/ppermute | solution.py:440
  63.4 5.8 %collective-permute-start.1 = (f32[114,8,128]{2,1,0:T(8,128)S(1)}, f32[114,8,128]{2,1,0:T(8,128)S(1)}, u32[]{:S(2)}, u32[]{:S(2)}) collective-permute-start(f32[114,8,128]{2,1,0:T(8,128)S(1)} %get-tuple-element.40), channel_id=1, source_target_pairs={{8,0},{16,8},{24,16},{32,24},{40,32},{48,40},{56,48},{64,56},{72,6... | collective-permute-start | bytes 1400840 | tf_op jit(solution)/shard_map/ppermute | solution.py:440
  69.1 10.2 %collective-permute-done.8.refs_1_.refs_6_ = f32[58,8,128]{2,1,0:T(8,128)S(1)} collective-permute-done((f32[58,8,128]{2,1,0:T(8,128)S(1)}, f32[58,8,128]{2,1,0:T(8,128)S(1)}, u32[]{:S(2)}, u32[]{:S(2)}) %collective-permute-start.8) | collective-permute-done | bytes 237600 | tf_op jit(solution)/shard_map/ppermute | solution.py:448
  79.3 1.8 %shard_map.162 = (f32[9,8,128]{2,1,0:T(8,128)S(1)}, f32[9,8,128]{2,1,0:T(8,128)S(1)}, f32[9,8,128]{2,1,0:T(8,128)S(1)}) custom-call(f32[49,8,128]{2,1,0:T(8,128)S(1)} %get-tuple-element.48.pack.refs_0_, f32[58,8,128]{2,1,0:T(8,128)S(1)} %collective-permute-done.8.refs_1_.refs_6_, f32[48,128]{1,0:T(8,128)S(1)} %collective-permute-done.4.rim.refs_2_.refs_8_.refs_1_, ...), custom_call_target="tpu_custom_call" | custom-call | flops 8388608 | bytes 1048576 | tf_op jit(solution)/shard_map/pallas_call | solution.py:33
  81.0 0.7 broadcast_in_dim.35
  81.7 5.4 %all-to-all-start.1 = ((f32[4,9,8,128]{3,2,1,0:T(8,128)}), f32[4,9,8,128]{3,2,1,0:T(8,128)S(1)}, u32[]{:S(2)}, u32[]{:S(2)}) async-start(f32[4,9,8,128]{3,2,1,0:T(8,128)} %broadcast_in_dim.35), calls=%async_computation.1 | async-start | bytes 294912 | tf_op jit(solution)/shard_map/all_to_all | solution.py:453
  87.1 4.0 %all-to-all-done.1 = f32[4,9,8,128]{3,2,1,0:T(8,128)S(1)} async-done(((f32[4,9,8,128]{3,2,1,0:T(8,128)}), f32[4,9,8,128]{3,2,1,0:T(8,128)S(1)}, u32[]{:S(2)}, u32[]{:S(2)}) %all-to-all-start.1) | async-done | bytes 147488 | tf_op jit(solution)/shard_map/all_to_all | solution.py:453
  91.2 1.9 %collective-permute-start.10 = (f32[8,128]{1,0:T(8,128)S(1)}, f32[8,128]{1,0:T(8,128)S(1)}, u32[]{:S(2)}, u32[]{:S(2)}) collective-permute-start(f32[8,128]{1,0:T(8,128)S(1)} %fusion.1), channel_id=1, source_target_pairs={{8,0},{16,8},{24,16},{32,24},{40,32},{48,40},{56,48},{64,56},{72,6... | collective-permute-start | bytes 12296 | tf_op jit(solution)/shard_map/ppermute | solution.py:440
  93.1 2.4 %collective-permute-start.9 = (f32[8,128]{1,0:T(8,128)S(1)}, f32[8,128]{1,0:T(8,128)S(1)}, u32[]{:S(2)}, u32[]{:S(2)}) collective-permute-start(f32[8,128]{1,0:T(8,128)S(1)} %slice_bitcast_fusion.3), channel_id=1, source_target_pairs={{0,8},{8,16},{16,24},{24,32},{32,40},{40,48},{48,56},{56,64},{64,7... | collective-permute-start | bytes 12296 | tf_op jit(solution)/shard_map/ppermute | solution.py:440
  95.5 4.6 %collective-permute-done.9.refs_6_ = f32[8,128]{1,0:T(8,128)S(1)} collective-permute-done((f32[8,128]{1,0:T(8,128)S(1)}, f32[8,128]{1,0:T(8,128)S(1)}, u32[]{:S(2)}, u32[]{:S(2)}) %collective-permute-start.9) | collective-permute-done | bytes 4128 | tf_op jit(solution)/shard_map/ppermute | solution.py:440
  100.1 1.8 %shard_map.163 = (f32[9,8,128]{2,1,0:T(8,128)S(1)}, f32[9,8,128]{2,1,0:T(8,128)S(1)}, f32[9,8,128]{2,1,0:T(8,128)S(1)}) custom-call(f32[49,8,128]{2,1,0:T(8,128)S(1)} %get-tuple-element.48.pack.refs_0_, f32[58,8,128]{2,1,0:T(8,128)S(1)} %collective-permute-done.8.refs_1_.refs_6_, f32[48,128]{1,0:T(8,128)S(1)} %collective-permute-done.4.rim.refs_2_.refs_8_.refs_1_, ...), custom_call_target="tpu_custom_call" | custom-call | flops 8388608 | bytes 1048576 | tf_op jit(solution)/shard_map/pallas_call | solution.py:33
  103.8 6.1 %all-to-all-start.2 = ((f32[4,9,8,128]{3,2,1,0:T(8,128)}), f32[4,9,8,128]{3,2,1,0:T(8,128)}, u32[]{:S(2)}, u32[]{:S(2)}) async-start(f32[4,9,8,128]{3,2,1,0:T(8,128)} %broadcast_in_dim.38), calls=%async_computation.2 | async-start | bytes 294912 | tf_op jit(solution)/shard_map/all_to_all | solution.py:453
  109.9 0.8 copy-done
  110.7 1.0 copy-done.1
  111.7 3.3 %shard_map.159 = (f32[456,8,128]{2,1,0:T(8,128)S(1)}, f32[15,16,128]{2,1,0:T(8,128)}) custom-call(f32[228,8,128]{2,1,0:T(8,128)S(1)} %get-tuple-element.38.planes, f32[114,8,128]{2,1,0:T(8,128)S(1)} %collective-permute-done.from_lower, f32[114,8,128]{2,1,0:T(8,128)S(1)} %copy-done.1), custom_call_target="tpu_custom_call" | custom-call | flops 4194304 | bytes 524288 | tf_op jit(solution)/shard_map/pallas_call | solution.py:33
  115.0 2.8 %collective-permute-start.2 = (f32[15,16,128]{2,1,0:T(8,128)}, f32[15,16,128]{2,1,0:T(8,128)S(1)}, u32[]{:S(2)}, u32[]{:S(2)}) collective-permute-start(f32[15,16,128]{2,1,0:T(8,128)} %get-tuple-element.42), channel_id=1, source_target_pairs={{0,1},{1,0},{2,3},{3,2},{4,5},{5,4},{6,7},{7,6},{8,9},{9,8},{10,11... | collective-permute-start | bytes 368648 | tf_op jit(solution)/shard_map/ppermute | solution.py:448
  117.8 12.7 %collective-permute-start.3 = (f32[15,16,128]{2,1,0:T(8,128)}, f32[15,16,128]{2,1,0:T(8,128)S(1)}, u32[]{:S(2)}, u32[]{:S(2)}) collective-permute-start(f32[15,16,128]{2,1,0:T(8,128)} %get-tuple-element.42), channel_id=1, source_target_pairs={{1,2},{2,1},{3,4},{4,3},{5,6},{6,5},{9,10},{10,9},{11,12},{12,11},... | collective-permute-start | bytes 368648 | tf_op jit(solution)/shard_map/ppermute | solution.py:518
  130.5 0.9 reduce_sum.29.refs_4_
  131.4 1.9 %collective-permute-start.12 = (f32[8,128]{1,0:T(8,128)S(1)}, f32[8,128]{1,0:T(8,128)S(1)}, u32[]{:S(2)}, u32[]{:S(2)}) collective-permute-start(f32[8,128]{1,0:T(8,128)S(1)} %fusion), channel_id=1, source_target_pairs={{8,0},{16,8},{24,16},{32,24},{40,32},{48,40},{56,48},{64,56},{72,6... | collective-permute-start | bytes 12296 | tf_op jit(solution)/shard_map/ppermute | solution.py:440
  133.4 2.4 %collective-permute-start.11 = (f32[8,128]{1,0:T(8,128)S(1)}, f32[8,128]{1,0:T(8,128)S(1)}, u32[]{:S(2)}, u32[]{:S(2)}) collective-permute-start(f32[8,128]{1,0:T(8,128)S(1)} %slice_bitcast_fusion.1), channel_id=1, source_target_pairs={{0,8},{8,16},{16,24},{24,32},{32,40},{40,48},{48,56},{56,64},{64,7... | collective-permute-start | bytes 12296 | tf_op jit(solution)/shard_map/ppermute | solution.py:440
  135.8 4.6 %collective-permute-done.11.refs_5_ = f32[8,128]{1,0:T(8,128)S(1)} collective-permute-done((f32[8,128]{1,0:T(8,128)S(1)}, f32[8,128]{1,0:T(8,128)S(1)}, u32[]{:S(2)}, u32[]{:S(2)}) %collective-permute-start.11) | collective-permute-done | bytes 4128 | tf_op jit(solution)/shard_map/ppermute | solution.py:440
  140.4 0.8 copy-done.9
  141.2 0.8 copy-done.11
  142.6 1.9 %collective-permute-start.13 = (f32[24,128]{1,0:T(8,128)S(1)}, f32[24,128]{1,0:T(8,128)S(1)}, u32[]{:S(2)}, u32[]{:S(2)}) collective-permute-start(f32[24,128]{1,0:T(8,128)S(1)} %get-tuple-element.60.r2), channel_id=1, source_target_pairs={{0,16},{8,24},{16,32},{24,40},{32,48},{40,56},{48,64},{56,72},{64,... | collective-permute-start | bytes 36872 | tf_op jit(solution)/shard_map/ppermute | solution.py:440
  144.5 1.9 %collective-permute-start.14 = (f32[24,128]{1,0:T(8,128)S(1)}, f32[24,128]{1,0:T(8,128)S(1)}, u32[]{:S(2)}, u32[]{:S(2)}) collective-permute-start(f32[24,128]{1,0:T(8,128)S(1)} %get-tuple-element.60.r2), channel_id=1, source_target_pairs={{0,8},{8,16},{16,24},{24,32},{32,40},{40,48},{48,56},{56,64},{64,7... | collective-permute-start | bytes 36872 | tf_op jit(solution)/shard_map/ppermute | solution.py:440
  146.5 5.8 %collective-permute-start.15 = (f32[24,128]{1,0:T(8,128)S(1)}, f32[24,128]{1,0:T(8,128)S(1)}, u32[]{:S(2)}, u32[]{:S(2)}) collective-permute-start(f32[24,128]{1,0:T(8,128)S(1)} %get-tuple-element.60.r2), channel_id=1, source_target_pairs={{8,0},{16,8},{24,16},{32,24},{40,32},{48,40},{56,48},{64,56},{72,6... | collective-permute-start | bytes 36872 | tf_op jit(solution)/shard_map/ppermute | solution.py:440
  152.2 3.9 %collective-permute-start.16 = (f32[24,128]{1,0:T(8,128)S(1)}, f32[24,128]{1,0:T(8,128)S(1)}, u32[]{:S(2)}, u32[]{:S(2)}) collective-permute-start(f32[24,128]{1,0:T(8,128)S(1)} %get-tuple-element.60.r2), channel_id=1, source_target_pairs={{16,0},{24,8},{32,16},{40,24},{48,32},{56,40},{64,48},{72,56},{80,... | collective-permute-start | bytes 36872 | tf_op jit(solution)/shard_map/ppermute | solution.py:440
  156.2 10.7 %shard_map.160 = (f32[5,16,8,128]{3,2,1,0:T(8,128)S(1)}, f32[15,16,128]{2,1,0:T(8,128)S(1)}) custom-call(s32[1]{0:T(128)} %bitcast.1.odd, f32[456,8,128]{2,1,0:T(8,128)S(1)} %get-tuple-element.41.full, f32[15,16,128]{2,1,0:T(8,128)S(1)} %collective-permute-done.2.near, f32[15,16,128]{2,1,0:T(8,128)S(1)} %collective-permute-done.3.far, ...), custom_call_target="tpu_custom_call" | custom-call | flops 16777216 | bytes 2097152 | tf_op jit(solution)/shard_map/pallas_call | solution.py:33
  167.0 5.3 %shard_map.165 = f32[5,16,8,128]{3,2,1,0:T(8,128)} custom-call(s32[1]{0:T(128)} %bitcast.span, f32[5]{0:T(128)S(1)} %copy-done.18, f32[3,5,5]{2,1,0:T(8,128)S(1)} %copy.23.upwind, f32[3,5,5]{2,1,0:T(8,128)S(1)} %copy.24.downwind, f32[5,16,8,128]{3,2,1,0:T(8,128)S(1)} %get-tuple-element.43.base, f32[456,8,128]{2,1,0:T(8,128)S(1)} %get-tuple-element.41.full, ...), custom_call_target="tpu_custom_call" | custom-call | flops 8388608 | bytes 1048576 | tf_op jit(solution)/shard_map/pallas_call | solution.py:33
  (59 shorter events, 4.8 us)
Async XLA Ops:
  1.3 1.0 copy-start.2
  2.3 1.0 copy-start.3
  3.2 1.0 copy-start.4
  4.2 0.9 copy-start.5
  5.1 0.9 copy-start.6
  6.0 0.8 copy-start.7
  6.9 0.8 copy-start.12
  7.6 0.8 copy-start.13
  8.4 0.7 copy-start.14
  9.1 0.7 copy-start.15
  9.8 0.7 copy-start.16
  13.5 5.2 %collective-permute-start.4 = (f32[48,128]{1,0:T(8,128)S(1)}, f32[48,128]{1,0:T(8,128)S(1)}, u32[]{:S(2)}, u32[]{:S(2)}) collective-permute-start(f32[48,128]{1,0:T(8,128)S(1)} %get-tuple-element.46), channel_id=1, source_target_pairs={{8,0},{16,8},{24,16},{32,24},{40,32},{48,40},{56,48},{64,56},{72,6... | collective-permute-start | bytes 73736 | tf_op jit(solution)/shard_map/ppermute | solution.py:440
  18.6 0.7 copy-start.17
  23.9 10.0 %collective-permute-start.5 = (f32[9,8,128]{2,1,0:T(8,128)S(1)}, f32[9,8,128]{2,1,0:T(8,128)S(1)}, u32[]{:S(2)}, u32[]{:S(2)}) collective-permute-start(f32[9,8,128]{2,1,0:T(8,128)S(1)} %get-tuple-element.50), channel_id=1, source_target_pairs={{0,8},{8,16},{16,24},{24,32},{32,40},{40,48},{48,56},{56,64},{64,7... | collective-permute-start | bytes 110600 | tf_op jit(solution)/shard_map/ppermute | solution.py:440
  25.9 8.1 %collective-permute-start.6 = (f32[9,8,128]{2,1,0:T(8,128)S(1)}, f32[9,8,128]{2,1,0:T(8,128)S(1)}, u32[]{:S(2)}, u32[]{:S(2)}) collective-permute-start(f32[9,8,128]{2,1,0:T(8,128)S(1)} %get-tuple-element.51), channel_id=1, source_target_pairs={{8,0},{16,8},{24,16},{32,24},{40,32},{48,40},{56,48},{64,56},{72,6... | collective-permute-start | bytes 110600 | tf_op jit(solution)/shard_map/ppermute | solution.py:440
  31.6 5.5 %collective-permute-start.7 = (f32[8,128]{1,0:T(8,128)S(1)}, f32[8,128]{1,0:T(8,128)S(1)}, u32[]{:S(2)}, u32[]{:S(2)}) collective-permute-start(f32[8,128]{1,0:T(8,128)S(1)} %get-tuple-element.52), channel_id=1, source_target_pairs={{16,0},{24,8},{32,16},{40,24},{48,32},{56,40},{64,48},{72,56},{80,... | collective-permute-start | bytes 12296 | tf_op jit(solution)/shard_map/ppermute | solution.py:440
  45.7 33.6 %collective-permute-start.8 = (f32[58,8,128]{2,1,0:T(8,128)S(1)}, f32[58,8,128]{2,1,0:T(8,128)S(1)}, u32[]{:S(2)}, u32[]{:S(2)}) collective-permute-start(f32[58,8,128]{2,1,0:T(8,128)S(1)} %pad_maximum_fusion), channel_id=1, source_target_pairs={{0,4},{1,5},{2,6},{3,7},{4,0},{5,1},{6,2},{7,3},{8,12},{9,13},{10,... | collective-permute-start | bytes 712712 | tf_op jit(solution)/shard_map/ppermute | solution.py:448
  61.4 48.5 %collective-permute-start = (f32[114,8,128]{2,1,0:T(8,128)}, f32[114,8,128]{2,1,0:T(8,128)S(1)}, u32[]{:S(2)}, u32[]{:S(2)}) collective-permute-start(f32[114,8,128]{2,1,0:T(8,128)} %get-tuple-element.39), channel_id=1, source_target_pairs={{0,8},{8,16},{16,24},{24,32},{32,40},{40,48},{48,56},{56,64},{64,7... | collective-permute-start | bytes 1400840 | tf_op jit(solution)/shard_map/ppermute | solution.py:440
  63.4 46.5 %collective-permute-start.1 = (f32[114,8,128]{2,1,0:T(8,128)S(1)}, f32[114,8,128]{2,1,0:T(8,128)S(1)}, u32[]{:S(2)}, u32[]{:S(2)}) collective-permute-start(f32[114,8,128]{2,1,0:T(8,128)S(1)} %get-tuple-element.40), channel_id=1, source_target_pairs={{8,0},{16,8},{24,16},{32,24},{40,32},{48,40},{56,48},{64,56},{72,6... | collective-permute-start | bytes 1400840 | tf_op jit(solution)/shard_map/ppermute | solution.py:440
  81.7 9.4 %all-to-all-start.1 = ((f32[4,9,8,128]{3,2,1,0:T(8,128)}), f32[4,9,8,128]{3,2,1,0:T(8,128)S(1)}, u32[]{:S(2)}, u32[]{:S(2)}) async-start(f32[4,9,8,128]{3,2,1,0:T(8,128)} %broadcast_in_dim.35), calls=%async_computation.1 | async-start | bytes 294912 | tf_op jit(solution)/shard_map/all_to_all | solution.py:453
  91.1 65.0 %copy-start.19 = (f32[3,5,5]{2,0,1:T(4,128)S(1)}, f32[3,5,5]{2,0,1:T(4,128)}, u32[]{:S(2)}) copy-start(f32[3,5,5]{2,0,1:T(4,128)} %param.21) | copy-start | bytes 904
  91.2 4.3 %collective-permute-start.10 = (f32[8,128]{1,0:T(8,128)S(1)}, f32[8,128]{1,0:T(8,128)S(1)}, u32[]{:S(2)}, u32[]{:S(2)}) collective-permute-start(f32[8,128]{1,0:T(8,128)S(1)} %fusion.1), channel_id=1, source_target_pairs={{8,0},{16,8},{24,16},{32,24},{40,32},{48,40},{56,48},{64,56},{72,6... | collective-permute-start | bytes 12296 | tf_op jit(solution)/shard_map/ppermute | solution.py:440
  93.1 7.0 %collective-permute-start.9 = (f32[8,128]{1,0:T(8,128)S(1)}, f32[8,128]{1,0:T(8,128)S(1)}, u32[]{:S(2)}, u32[]{:S(2)}) collective-permute-start(f32[8,128]{1,0:T(8,128)S(1)} %slice_bitcast_fusion.3), channel_id=1, source_target_pairs={{0,8},{8,16},{16,24},{24,32},{32,40},{40,48},{48,56},{56,64},{64,7... | collective-permute-start | bytes 12296 | tf_op jit(solution)/shard_map/ppermute | solution.py:440
  100.1 56.1 %copy-start.20 = (f32[3,5,5]{2,0,1:T(4,128)S(1)}, f32[3,5,5]{2,0,1:T(4,128)}, u32[]{:S(2)}) copy-start(f32[3,5,5]{2,0,1:T(4,128)} %param.22) | copy-start | bytes 904
  101.9 0.6 copy-start.8
  102.5 0.6 copy-start.10
  103.8 63.2 %copy-start.18 = (f32[5]{0:T(128)S(1)}, f32[5]{0:T(128)}, u32[]{:S(2)}) copy-start(f32[5]{0:T(128)} %prow.3) | copy-start | bytes 64
  103.8 26.7 %all-to-all-start.2 = ((f32[4,9,8,128]{3,2,1,0:T(8,128)}), f32[4,9,8,128]{3,2,1,0:T(8,128)}, u32[]{:S(2)}, u32[]{:S(2)}) async-start(f32[4,9,8,128]{3,2,1,0:T(8,128)} %broadcast_in_dim.38), calls=%async_computation.2 | async-start | bytes 294912 | tf_op jit(solution)/shard_map/all_to_all | solution.py:453
  109.9 0.8 copy-start
  110.7 1.0 copy-start.1
  115.0 37.2 %collective-permute-start.2 = (f32[15,16,128]{2,1,0:T(8,128)}, f32[15,16,128]{2,1,0:T(8,128)S(1)}, u32[]{:S(2)}, u32[]{:S(2)}) collective-permute-start(f32[15,16,128]{2,1,0:T(8,128)} %get-tuple-element.42), channel_id=1, source_target_pairs={{0,1},{1,0},{2,3},{3,2},{4,5},{5,4},{6,7},{7,6},{8,9},{9,8},{10,11... | collective-permute-start | bytes 368648 | tf_op jit(solution)/shard_map/ppermute | solution.py:448
  117.8 38.4 %collective-permute-start.3 = (f32[15,16,128]{2,1,0:T(8,128)}, f32[15,16,128]{2,1,0:T(8,128)S(1)}, u32[]{:S(2)}, u32[]{:S(2)}) collective-permute-start(f32[15,16,128]{2,1,0:T(8,128)} %get-tuple-element.42), channel_id=1, source_target_pairs={{1,2},{2,1},{3,4},{4,3},{5,6},{6,5},{9,10},{10,9},{11,12},{12,11},... | collective-permute-start | bytes 368648 | tf_op jit(solution)/shard_map/ppermute | solution.py:518
  131.4 4.3 %collective-permute-start.12 = (f32[8,128]{1,0:T(8,128)S(1)}, f32[8,128]{1,0:T(8,128)S(1)}, u32[]{:S(2)}, u32[]{:S(2)}) collective-permute-start(f32[8,128]{1,0:T(8,128)S(1)} %fusion), channel_id=1, source_target_pairs={{8,0},{16,8},{24,16},{32,24},{40,32},{48,40},{56,48},{64,56},{72,6... | collective-permute-start | bytes 12296 | tf_op jit(solution)/shard_map/ppermute | solution.py:440
  133.4 7.0 %collective-permute-start.11 = (f32[8,128]{1,0:T(8,128)S(1)}, f32[8,128]{1,0:T(8,128)S(1)}, u32[]{:S(2)}, u32[]{:S(2)}) collective-permute-start(f32[8,128]{1,0:T(8,128)S(1)} %slice_bitcast_fusion.1), channel_id=1, source_target_pairs={{0,8},{8,16},{16,24},{24,32},{32,40},{40,48},{48,56},{56,64},{64,7... | collective-permute-start | bytes 12296 | tf_op jit(solution)/shard_map/ppermute | solution.py:440
  140.4 0.8 copy-start.9
  141.2 0.8 copy-start.11
  142.6 24.4 %collective-permute-start.13 = (f32[24,128]{1,0:T(8,128)S(1)}, f32[24,128]{1,0:T(8,128)S(1)}, u32[]{:S(2)}, u32[]{:S(2)}) collective-permute-start(f32[24,128]{1,0:T(8,128)S(1)} %get-tuple-element.60.r2), channel_id=1, source_target_pairs={{0,16},{8,24},{16,32},{24,40},{32,48},{40,56},{48,64},{56,72},{64,... | collective-permute-start | bytes 36872 | tf_op jit(solution)/shard_map/ppermute | solution.py:440
  144.5 22.5 %collective-permute-start.14 = (f32[24,128]{1,0:T(8,128)S(1)}, f32[24,128]{1,0:T(8,128)S(1)}, u32[]{:S(2)}, u32[]{:S(2)}) collective-permute-start(f32[24,128]{1,0:T(8,128)S(1)} %get-tuple-element.60.r2), channel_id=1, source_target_pairs={{0,8},{8,16},{16,24},{24,32},{32,40},{40,48},{48,56},{56,64},{64,7... | collective-permute-start | bytes 36872 | tf_op jit(solution)/shard_map/ppermute | solution.py:440
  146.5 20.5 %collective-permute-start.15 = (f32[24,128]{1,0:T(8,128)S(1)}, f32[24,128]{1,0:T(8,128)S(1)}, u32[]{:S(2)}, u32[]{:S(2)}) collective-permute-start(f32[24,128]{1,0:T(8,128)S(1)} %get-tuple-element.60.r2), channel_id=1, source_target_pairs={{8,0},{16,8},{24,16},{32,24},{40,32},{48,40},{56,48},{64,56},{72,6... | collective-permute-start | bytes 36872 | tf_op jit(solution)/shard_map/ppermute | solution.py:440
  152.2 14.8 %collective-permute-start.16 = (f32[24,128]{1,0:T(8,128)S(1)}, f32[24,128]{1,0:T(8,128)S(1)}, u32[]{:S(2)}, u32[]{:S(2)}) collective-permute-start(f32[24,128]{1,0:T(8,128)S(1)} %get-tuple-element.60.r2), channel_id=1, source_target_pairs={{16,0},{24,8},{32,16},{40,24},{48,32},{56,40},{64,48},{72,56},{80,... | collective-permute-start | bytes 36872 | tf_op jit(solution)/shard_map/ppermute | solution.py:440

commit v2 on v1

--- a/solution.py
+++ b/solution.py
@@ -23,21 +23,20 @@
 SLOTS = 2 * PLANES
 WIDTH = 4
 PACKED = 49
+RING = 4
 BLOCKS = ((0, 0), (1, 0), (1, 1), (2, 0), (2, 1), (2, 2))
 VM = pl.BlockSpec(memory_space=pltpu.VMEM)
 SM = pl.BlockSpec(memory_space=pltpu.SMEM)
-PARAMS = pltpu.CompilerParams(vmem_limit_bytes=48 << 20)
-
-
-def call(body, out, ins, specs, flops, scratch=(), aliases=None):
+
+
+def call(body, out, ins, specs, flops, scratch=(), vmem=16):
     return pl.pallas_call(
         body,
         out_shape=out,
         in_specs=specs,
         out_specs=jax.tree.map(lambda _: VM, out),
         scratch_shapes=list(scratch),
-        input_output_aliases=aliases or {},
-        compiler_params=PARAMS,
+        compiler_params=pltpu.CompilerParams(vmem_limit_bytes=vmem << 20),
         cost_estimate=pl.CostEstimate(flops=flops, bytes_accessed=flops // 8, transcendentals=0),
     )(*ins)
 
@@ -52,7 +51,7 @@
 
 def front_kernel(
     span, count, state, grad, diag, coup, normal, fnode, stiff, conn, shell_in, sgrad_in, precond_in,
-    pack, rim, planes, up, down, shell, sgrad, precond, inverse, faces, elems, sems,
+    pack, rim, planes, up, down, shell, sgrad, precond, walls, inverse, faces, elems, sems,
 ):
     moves = []
 
@@ -91,6 +90,9 @@
     for i in range(3):
         planes[224 + i] = jnp.where(active, planes[224 + i], 0.0)
     planes[227] = faces[...].astype(F32)
+    for j in range(5):
+        walls[j] = planes[16 * j]
+    walls[5:9] = planes[224:228]
     low = iota((8, 128), 0) < 4
 
     def body(k, carry):
@@ -143,19 +145,16 @@
     return forces[0:8] + forces[8:16]
 
 
-def first_kernel(
-    span, prow, planes, shell, rim, pack,
-    own, up, down, down2, faces, nodes, loads, field, onehot, uvec, fvec,
-):
-    press = prow[0] * planes[0]
+def load_kernel(span, prow, walls, loads, faces, nodes):
+    press = prow[0] * walls[0]
     for j in range(1, 5):
-        press = press + prow[j] * planes[16 * j]
-    local = planes[227].astype(jnp.int32) - (span[0] - 1) * NODE_DEV
+        press = press + prow[j] * walls[j]
+    local = walls[8].astype(jnp.int32) - (span[0] - 1) * NODE_DEV
     faces[...] = jnp.zeros((8, 1024), F32)
     for r in range(8):
         nodes[0:1, r * 128 : r * 128 + 128] = local[r : r + 1]
     for i in range(3):
-        load = planes[224 + i] * press
+        load = walls[5 + i] * press
         for r in range(8):
             faces[i : i + 1, r * 128 : r * 128 + 128] = load[r : r + 1]
     face_parts = parts(faces[...])
@@ -173,6 +172,9 @@
         return carry
 
     lax.fori_loop(0, 12, chunk, 0)
+
+
+def first_kernel(loads, shell, rim, pack, own, up, down, down2, field, onehot, uvec, fvec):
     field[...] = jnp.zeros((8, EXT), F32)
     field[0:6, 0:NODE_DEV] = shell[...]
     field[0:6, NODE_DEV:EXT] = rim[0:6, :]
@@ -207,11 +209,15 @@
         base = sgrad[:, t * 128 : t * 128 + 128] if t < 8 else rim[6:12, :]
         base = jnp.concatenate([base, jnp.zeros((2, 128), F32)], axis=0)
         return base - total[t] - remote[PACKED + t]
-    force, rise, fall, prev = ins
-    res = prev[t] - force[t]
-    if t == 0:
-        res = res - rise[...]
-    return res - fall[...] if t == 8 else res
+    force, prev = ins[:2]
+    res = prev[t] - ring_total(force, t)
+    if t == 0 and len(ins) > 2:
+        res = res - ins[2][...]
+    return res - ins[3][...] if t == 8 else res
+
+
+def ring_total(force, t):
+    return (force[0, t] + force[1, t]) + (force[2, t] + force[3, t])
 
 
 def step_kernel(first, *refs):
@@ -225,18 +231,18 @@
         field[:, t * 128 : t * 128 + 128] = delta
     force = stiff_apply(field[...], (own_pack, far_pack), onehot, uvec, fvec)
     for t in range(TILES):
-        force_out[t] = force[:, t * 128 : t * 128 + 128]
-
-
-def last_kernel(*refs):
-    refs, (shell_out, reach_out) = refs[:-2], refs[-2:]
-    shell, rim, precond, prev_sum = refs[:4]
+        for q in range(RING):
+            force_out[q, t] = force[:, t * 128 : t * 128 + 128]
+
+
+def last_kernel(shell, rim, precond, prev_sum, force, prev, shell_out, reach_out):
     for t in range(8):
-        delta = precondition(t, precond, rim, shell_residual(False, t, refs[4:]))
+        delta = precondition(t, precond, rim, shell_residual(False, t, (force, prev)))
         value = shell[:, t * 128 : t * 128 + 128] + (prev_sum[t] + delta)[0:6]
         shell_out[:, t * 128 : t * 128 + 128] = value
         for i in range(3):
             reach_out[8 * i + t : 8 * i + t + 1, :] = value[i : i + 1]
+    reach_out[24:32, :] = -precondition(8, precond, rim, ring_total(force, 8))
 
 
 def pack_chord_kernel(planes, from_lower, from_upper, full, edges):
@@ -448,10 +454,8 @@
     return lax.ppermute(value, CHORD, [(c, c ^ bit) for c in range(count)])
 
 
-def ring_sum(value):
-    count = lax.axis_size("y")
-    pieces = lax.all_to_all(jnp.broadcast_to(value[None], (count, *value.shape)), "y", 0, 0)
-    return pieces.sum(0)
+def ring_parts(copies):
+    return lax.all_to_all(copies, "y", 0, 0)
 
 
 def per_device(
@@ -460,11 +464,12 @@
 ):
     span = lax.axis_index("span").astype(jnp.int32).reshape(1)
     odd = (lax.axis_index("y") % 2).astype(jnp.int32).reshape(1)
-    pack, rim, planes, to_upper, to_lower, shell, sgrad, precond = call(
+    pack, rim, planes, to_upper, to_lower, shell, sgrad, precond, walls = call(
         front_kernel,
         (
             sds(PACKED, 8, 128), sds(48, 128), sds(PLANES, 8, 128), sds(HALF, 8, 128),
             sds(HALF, 8, 128), sds(6, NODE_DEV), sds(6, NODE_DEV), sds(6, 6, NODE_DEV),
+            sds(9, 8, 128),
         ),
         (
             span, face_count, adjoint_flow, flow_grad, diagonal, couplings, face_normal, face_node,
@@ -476,9 +481,19 @@
             pltpu.VMEM((LAYERS, 8, 128), F32), pltpu.VMEM((8, 128), jnp.int32),
             pltpu.VMEM((4, 128), jnp.int32), pltpu.SemaphoreType.DMA((32,)),
         ),
+        vmem=60,
     )
     rim = along_span(rim, -1)
-    from_lower, from_upper = along_span(to_upper, 1), along_span(to_lower, -1)
+    from_lower = along_span(to_upper, 1)
+    from_upper = along_span(to_lower, -1)
+    loads = call(
+        load_kernel,
+        sds(24, 8, 128),
+        (span, pressure_row, walls),
+        [SM] * 2 + [VM],
+        4 << 20,
+        (pltpu.VMEM((8, 1024), F32), pltpu.VMEM((8, 1024), jnp.int32)),
+    )
     apply_scratch = lambda nb: (
         pltpu.VMEM((8, EXT), F32),
         pltpu.VMEM((EXT, 512 * nb), BF16),
@@ -488,13 +503,14 @@
     own, up, down, down2 = call(
         first_kernel,
         (sds(TILES, 8, 128), sds(TILES, 8, 128), sds(TILES, 8, 128), sds(8, 128)),
-        (span, pressure_row, planes, shell, rim, pack),
-        [SM] * 2 + [VM] * 4,
-        8 << 20,
-        (pltpu.VMEM((8, 1024), F32), pltpu.VMEM((8, 1024), jnp.int32), pltpu.VMEM((24, 8, 128), F32))
-        + apply_scratch(1),
-    )
-    up, down, down2 = along_span(up, 1), along_span(down, -1), along_span(down2, -2)
+        (loads, shell, rim, pack),
+        [VM] * 4,
+        4 << 20,
+        apply_scratch(1),
+    )
+    up = along_span(up, 1)
+    down = along_span(down, -1)
+    down2 = along_span(down2, -2)
     full, edges = call(
         pack_chord_kernel,
         (sds(SLOTS, 8, 128), sds(FIELDS, 16, 128)),
@@ -502,9 +518,13 @@
         [VM] * 3,
         4 << 20,
     )
+    count = lax.axis_size(CHORD)
+    pairs = [(c, c - 1 + 2 * (c % 2)) for c in range(1, count - 1)]
+    far = lax.ppermute(edges, CHORD, pairs)
     near = swap(edges, 1)
     total = own + jnp.concatenate([up[:8] + down[:8], (down[8] + down2)[None]], axis=0)
-    total = ring_sum(total.at[0].add(up[8]))
+    total = total.at[0].add(up[8])
+    total = ring_parts(jnp.broadcast_to(total[None], (RING, *total.shape))).sum(0)
     scratch = lambda layers: (
         pltpu.VMEM((2, 5, layers + 2, 16, 128), F32),
         pltpu.VMEM((2, 5, 16, 128), F32),
@@ -512,10 +532,7 @@
         pltpu.VMEM((5, 16, 128), F32),
         pltpu.VMEM((5, 4, 16, 128), F32),
     )
-    count = lax.axis_size(CHORD)
-    pairs = [(c, c - 1 + 2 * (c % 2)) for c in range(1, count - 1)]
     remote = swap(jnp.concatenate([pack, total], axis=0), 4)
-    far = lax.ppermute(edges, CHORD, pairs)
     base, edges = call(
         base_kernel,
         (sds(5, LAYERS, 8, 128), sds(FIELDS, 16, 128)),
@@ -530,25 +547,34 @@
     for turn in range(2):
         res, sums, force = call(
             functools.partial(step_kernel, turn == 0),
-            (sds(TILES, 8, 128),) * 3,
+            (sds(TILES, 8, 128), sds(TILES, 8, 128), sds(RING, TILES, 8, 128)),
             (pack, remote if turn == 0 else far_pack, rim, precond, sums) + pieces,
             [VM] * (5 + len(pieces)),
             8 << 20,
             apply_scratch(2),
         )
         far_pack = remote if turn == 0 else far_pack
-        force = ring_sum(force)
-        rise = along_span(force[8], 1)
-        fall = along_span(jnp.where(lead, force[0], 0.0), -1)
-        pieces = (force, rise, fall, res)
+        force = ring_parts(force)
+        pieces = (force, res)
+        if turn == 0:
+            pieces += (
+                along_span(force[:, 8].sum(0), 1),
+                along_span(jnp.where(lead, force[:, 0].sum(0), 0.0), -1),
+            )
     shell, reach = call(
         last_kernel,
-        (sds(6, NODE_DEV), sds(24, 128)),
+        (sds(6, NODE_DEV), sds(32, 128)),
         (shell, rim, precond, sums) + pieces,
         [VM] * (4 + len(pieces)),
         1 << 20,
     )
-    reaches = [along_span(reach, k) for k in (2, 1)] + [reach] + [along_span(reach, -k) for k in (1, 2)]
+    below, above, lower = along_span(reach, 1), along_span(reach, -1), along_span(reach[24:], 2)
+    mend = lambda value, part: (
+        value[:24].reshape(3, 8, 128).at[:, 0].add(part[:3]).reshape(24, 128)
+    )
+    shell = shell.at[:, :128].add(below[24:30])
+    reach, below, above = mend(reach, below[24:]), mend(below, lower), mend(above, reach[24:])
+    reaches = (along_span(below, 1), below, reach, above, along_span(above, -1))
     flow = call(
         final_kernel,
         sds(5, LAYERS, 8, 128),

time: 174 us -> 165 us (0.948)
  the two profiles are of different devices: /device:TPU:56 before, /device:TPU:40 now
where the time goes in v2:
time: 165 us; the launch traced here: 164 us
  starting transfers between devices  84.5 us (51%)
  Pallas kernels  33.7 us (20%)
  waiting for transfers between devices  32.2 us (20%)
  local copies, waits for them, and re-layouts  8.25 us (5%)
  other arithmetic  3.32 us (2%)
  between operations  1.69 us (1%)
    ppermute x13, starting transfers between devices, along_span(): lax.ppermute(value, 'span', [(i, i + steps) for i in range(first, last)])  41.9 us
    pallas_call x9, Pallas kernels, call(): pl.pallas_call(body, out_shape=out, in_specs=specs, out_specs=jax.tree.ma...  33.7 us
    ppermute x2, waiting for transfers between devices, swap(): return lax.ppermute(value, CHORD, [(c, c ^ bit) for c in range(count)])  20.3 us
    all_to_all x3, starting transfers between devices, ring_parts(): return lax.all_to_all(copies, 'y', 0, 0)  20.3 us
    ppermute x2, starting transfers between devices, swap(): return lax.ppermute(value, CHORD, [(c, c ^ bit) for c in range(count)])  17.8 us
    ppermute x13, waiting for transfers between devices, along_span(): lax.ppermute(value, 'span', [(i, i + steps) for i in range(first, last)])  11.8 us
    unnamed x32, local copies, waits for them, and re-layouts  7.46 us
    ppermute x1, starting transfers between devices, per_device(): far = lax.ppermute(edges, CHORD, pairs)  4.53 us
  transfers between devices with their start and end apart: 19, of which 5 were waited for; matrix products, arithmetic and copies ran while one was open for 3% of the time, Pallas kernels for 14%

profile of v2, /device:TPU:40, one launch (start us, length us, event | category | flops | bytes accessed | tf_op | source)
XLA Modules:
  0.0 163.7 jit_solution(14779595289372344766)
XLA Ops:
  1.3 3.2 %shard_map.158 = (f32[49,8,128]{2,1,0:T(8,128)}, f32[48,128]{1,0:T(8,128)}, f32[228,8,128]{2,1,0:T(8,128)}, f32[114,8,128]{2,1,0:T(8,128)}, f32[114,8,128]{2,1,0...) custom-call(s32[1]{0:T(128)} %bitcast.span, ...), custom_call_target="tpu_custom_call" | custom-call | flops 4194304 | bytes 524288 | tf_op jit(solution)/shard_map/pallas_call | solution.py:33
  4.5 3.7 %collective-permute-start.4 = (f32[48,128]{1,0:T(8,128)}, f32[48,128]{1,0:T(8,128)S(1)}, u32[]{:S(2)}, u32[]{:S(2)}) collective-permute-start(f32[48,128]{1,0:T(8,128)} %get-tuple-element.95), channel_id=1, source_target_pairs={{8,0},{16,8},{24,16},{32,24},{40,32},{48,40},{56,48},{64,56},{72,6... | collective-permute-start | bytes 73736 | tf_op jit(solution)/shard_map/ppermute | solution.py:446
  8.1 0.8 copy-done.10
  8.9 0.7 copy-done.12
  9.5 3.7 %shard_map.161.loads = f32[24,8,128]{2,1,0:T(8,128)S(1)} custom-call(s32[1]{0:T(128)} %bitcast.span, f32[5]{0:T(128)S(1)} %copy-done.12, f32[9,8,128]{2,1,0:T(8,128)S(1)} %copy-done.10), custom_call_target="tpu_custom_call" | custom-call | flops 4194304 | bytes 524288 | tf_op jit(solution)/shard_map/pallas_call | solution.py:33
  13.3 0.0 collective-permute-done.4.rim.refs_2_.refs_8_
  13.3 0.0 copy-start
  13.3 0.9 copy-done
  14.2 0.8 copy-done.8
  15.0 0.9 shard_map.162
  15.9 1.9 %collective-permute-start.5 = (f32[9,8,128]{2,1,0:T(8,128)S(1)}, f32[9,8,128]{2,1,0:T(8,128)S(1)}, u32[]{:S(2)}, u32[]{:S(2)}) collective-permute-start(f32[9,8,128]{2,1,0:T(8,128)S(1)} %get-tuple-element.100), channel_id=1, source_target_pairs={{0,8},{8,16},{16,24},{24,32},{32,40},{40,48},{48,56},{56,64},{64,7... | collective-permute-start | bytes 110600 | tf_op jit(solution)/shard_map/ppermute | solution.py:446
  17.9 5.8 %collective-permute-start.6 = (f32[9,8,128]{2,1,0:T(8,128)S(1)}, f32[9,8,128]{2,1,0:T(8,128)S(1)}, u32[]{:S(2)}, u32[]{:S(2)}) collective-permute-start(f32[9,8,128]{2,1,0:T(8,128)S(1)} %get-tuple-element.101), channel_id=1, source_target_pairs={{8,0},{16,8},{24,16},{32,24},{40,32},{48,40},{56,48},{64,56},{72,6... | collective-permute-start | bytes 110600 | tf_op jit(solution)/shard_map/ppermute | solution.py:446
  23.6 1.9 %collective-permute-start.7 = (f32[8,128]{1,0:T(8,128)S(1)}, f32[8,128]{1,0:T(8,128)S(1)}, u32[]{:S(2)}, u32[]{:S(2)}) collective-permute-start(f32[8,128]{1,0:T(8,128)S(1)} %get-tuple-element.102), channel_id=1, source_target_pairs={{16,0},{24,8},{32,16},{40,24},{48,32},{56,40},{64,48},{72,56},{80,... | collective-permute-start | bytes 12296 | tf_op jit(solution)/shard_map/ppermute | solution.py:446
  25.6 3.5 %collective-permute-done.7 = f32[8,128]{1,0:T(8,128)S(1)} collective-permute-done((f32[8,128]{1,0:T(8,128)S(1)}, f32[8,128]{1,0:T(8,128)S(1)}, u32[]{:S(2)}, u32[]{:S(2)}) %collective-permute-start.7) | collective-permute-done | bytes 4128 | tf_op jit(solution)/shard_map/ppermute | solution.py:446
  29.1 0.7 broadcast_in_dim.18
  29.8 4.9 %all-to-all-start = ((f32[4,9,8,128]{3,2,1,0:T(8,128)}), f32[4,9,8,128]{3,2,1,0:T(8,128)S(1)}, u32[]{:S(2)}, u32[]{:S(2)}) async-start(f32[4,9,8,128]{3,2,1,0:T(8,128)} %broadcast_in_dim.18), calls=%async_computation | async-start | bytes 294912 | tf_op jit(solution)/shard_map/all_to_all | solution.py:458
  34.7 1.9 %collective-permute-start = (f32[114,8,128]{2,1,0:T(8,128)}, f32[114,8,128]{2,1,0:T(8,128)S(1)}, u32[]{:S(2)}, u32[]{:S(2)}) collective-permute-start(f32[114,8,128]{2,1,0:T(8,128)} %get-tuple-element.88), channel_id=1, source_target_pairs={{0,8},{8,16},{16,24},{24,32},{32,40},{40,48},{48,56},{56,64},{64,7... | collective-permute-start | bytes 1400840 | tf_op jit(solution)/shard_map/ppermute | solution.py:446
  36.6 5.8 %collective-permute-start.1 = (f32[114,8,128]{2,1,0:T(8,128)}, f32[114,8,128]{2,1,0:T(8,128)S(1)}, u32[]{:S(2)}, u32[]{:S(2)}) collective-permute-start(f32[114,8,128]{2,1,0:T(8,128)} %get-tuple-element.89), channel_id=1, source_target_pairs={{8,0},{16,8},{24,16},{32,24},{40,32},{48,40},{56,48},{64,56},{72,6... | collective-permute-start | bytes 1400840 | tf_op jit(solution)/shard_map/ppermute | solution.py:446
  42.4 15.7 %collective-permute-start.8 = (f32[58,8,128]{2,1,0:T(8,128)S(1)}, f32[58,8,128]{2,1,0:T(8,128)S(1)}, u32[]{:S(2)}, u32[]{:S(2)}) collective-permute-start(f32[58,8,128]{2,1,0:T(8,128)S(1)} %pad_maximum_fusion), channel_id=1, source_target_pairs={{0,4},{1,5},{2,6},{3,7},{4,0},{5,1},{6,2},{7,3},{8,12},{9,13},{10,... | collective-permute-start | bytes 712712 | tf_op jit(solution)/shard_map/ppermute | solution.py:454
  58.2 20.3 %collective-permute-done.8.refs_1_.refs_6_ = f32[58,8,128]{2,1,0:T(8,128)S(1)} collective-permute-done((f32[58,8,128]{2,1,0:T(8,128)S(1)}, f32[58,8,128]{2,1,0:T(8,128)S(1)}, u32[]{:S(2)}, u32[]{:S(2)}) %collective-permute-start.8) | collective-permute-done | bytes 237600 | tf_op jit(solution)/shard_map/ppermute | solution.py:454
  78.5 2.5 %shard_map.163 = (f32[9,8,128]{2,1,0:T(8,128)S(1)}, f32[9,8,128]{2,1,0:T(8,128)S(1)}, f32[4,9,8,128]{3,2,1,0:T(8,128)}) custom-call(f32[49,8,128]{2,1,0:T(8,128)S(1)} %copy-done.1, f32[58,8,128]{2,1,0:T(8,128)S(1)} %collective-permute-done.8.refs_1_.refs_6_, f32[48,128]{1,0:T(8,128)S(1)} %collective-permute-done.4.rim.refs_2_.refs_8_, ...), custom_call_target="tpu_custom_call" | custom-call | flops 8388608 | bytes 1048576 | tf_op jit(solution)/shard_map/pallas_call | solution.py:33
  81.0 4.9 %all-to-all-start.1 = ((f32[4,9,8,128]{3,2,1,0:T(8,128)}), f32[4,9,8,128]{3,2,1,0:T(8,128)}, u32[]{:S(2)}, u32[]{:S(2)}) async-start(f32[4,9,8,128]{3,2,1,0:T(8,128)} %get-tuple-element.105), calls=%async_computation.1 | async-start | bytes 294912 | tf_op jit(solution)/shard_map/all_to_all | solution.py:458
  85.9 0.8 copy-done.4
  86.7 0.8 copy-done.6
  87.5 1.0 copy-done.5
  88.5 1.0 copy-done.7
  89.6 3.3 %shard_map.159 = (f32[456,8,128]{2,1,0:T(8,128)S(1)}, f32[15,16,128]{2,1,0:T(8,128)}) custom-call(f32[228,8,128]{2,1,0:T(8,128)S(1)} %copy-done.3, f32[114,8,128]{2,1,0:T(8,128)S(1)} %copy-done.5, f32[114,8,128]{2,1,0:T(8,128)S(1)} %copy-done.7), custom_call_target="tpu_custom_call" | custom-call | flops 4194304 | bytes 524288 | tf_op jit(solution)/shard_map/pallas_call | solution.py:33
  92.9 2.0 %collective-permute-start.2 = (f32[15,16,128]{2,1,0:T(8,128)}, f32[15,16,128]{2,1,0:T(8,128)S(1)}, u32[]{:S(2)}, u32[]{:S(2)}) collective-permute-start(f32[15,16,128]{2,1,0:T(8,128)} %get-tuple-element.91), channel_id=1, source_target_pairs={{0,1},{1,0},{2,3},{3,2},{4,5},{5,4},{6,7},{7,6},{8,9},{9,8},{10,11... | collective-permute-start | bytes 368648 | tf_op jit(solution)/shard_map/ppermute | solution.py:454
  94.9 4.5 %collective-permute-start.3 = (f32[15,16,128]{2,1,0:T(8,128)}, f32[15,16,128]{2,1,0:T(8,128)S(1)}, u32[]{:S(2)}, u32[]{:S(2)}) collective-permute-start(f32[15,16,128]{2,1,0:T(8,128)} %get-tuple-element.91), channel_id=1, source_target_pairs={{1,2},{2,1},{3,4},{4,3},{5,6},{6,5},{9,10},{10,9},{11,12},{12,11},... | collective-permute-start | bytes 368648 | tf_op jit(solution)/shard_map/ppermute | solution.py:523
  99.5 0.7 slice_reduce_fusion
  100.2 1.9 %collective-permute-start.10 = (f32[8,128]{1,0:T(8,128)S(1)}, f32[8,128]{1,0:T(8,128)S(1)}, u32[]{:S(2)}, u32[]{:S(2)}) collective-permute-start(f32[8,128]{1,0:T(8,128)S(1)} %broadcast_select_fusion), channel_id=1, source_target_pairs={{8,0},{16,8},{24,16},{32,24},{40,32},{48,40},{56,48},{64,56},{72,6... | collective-permute-start | bytes 12296 | tf_op jit(solution)/shard_map/ppermute | solution.py:446
  102.1 2.4 %collective-permute-start.9 = (f32[8,128]{1,0:T(8,128)S(1)}, f32[8,128]{1,0:T(8,128)S(1)}, u32[]{:S(2)}, u32[]{:S(2)}) collective-permute-start(f32[8,128]{1,0:T(8,128)S(1)} %get-tuple-element.113), channel_id=1, source_target_pairs={{0,8},{8,16},{16,24},{24,32},{32,40},{40,48},{48,56},{56,64},{64,7... | collective-permute-start | bytes 12296 | tf_op jit(solution)/shard_map/ppermute | solution.py:446
  104.6 4.6 %collective-permute-done.9.refs_7_ = f32[8,128]{1,0:T(8,128)S(1)} collective-permute-done((f32[8,128]{1,0:T(8,128)S(1)}, f32[8,128]{1,0:T(8,128)S(1)}, u32[]{:S(2)}, u32[]{:S(2)}) %collective-permute-start.9) | collective-permute-done | bytes 4128 | tf_op jit(solution)/shard_map/ppermute | solution.py:446
  109.2 3.4 %shard_map.164 = (f32[9,8,128]{2,1,0:T(8,128)S(1)}, f32[9,8,128]{2,1,0:T(8,128)S(1)}, f32[4,9,8,128]{3,2,1,0:T(8,128)}) custom-call(f32[49,8,128]{2,1,0:T(8,128)S(1)} %copy-done.1, f32[58,8,128]{2,1,0:T(8,128)S(1)} %collective-permute-done.8.refs_1_.refs_6_, f32[48,128]{1,0:T(8,128)S(1)} %collective-permute-done.4.rim.refs_2_.refs_8_, ...), custom_call_target="tpu_custom_call" | custom-call | flops 8388608 | bytes 1048576 | tf_op jit(solution)/shard_map/pallas_call | solution.py:33
  112.6 10.5 %all-to-all-start.2 = ((f32[4,9,8,128]{3,2,1,0:T(8,128)}), f32[4,9,8,128]{3,2,1,0:T(8,128)S(1)}, u32[]{:S(2)}, u32[]{:S(2)}) async-start(f32[4,9,8,128]{3,2,1,0:T(8,128)} %get-tuple-element.108), calls=%async_computation.2 | async-start | bytes 294912 | tf_op jit(solution)/shard_map/all_to_all | solution.py:458
  123.1 0.7 copy.44.downwind
  123.8 0.6 compare_reduce_fusion
  124.4 10.7 %shard_map.160 = (f32[5,16,8,128]{3,2,1,0:T(8,128)S(1)}, f32[15,16,128]{2,1,0:T(8,128)S(1)}) custom-call(s32[1]{0:T(128)} %bitcast.1.odd, f32[456,8,128]{2,1,0:T(8,128)S(1)} %get-tuple-element.90.full, f32[15,16,128]{2,1,0:T(8,128)S(1)} %collective-permute-done.2.near, f32[15,16,128]{2,1,0:T(8,128)S(1)} %collective-permute-done.3.far, ...), custom_call_target="tpu_custom_call" | custom-call | flops 16777216 | bytes 2097152 | tf_op jit(solution)/shard_map/pallas_call | solution.py:33
  135.2 0.7 shard_map.165
  135.9 1.9 %collective-permute-start.11 = (f32[32,128]{1,0:T(8,128)S(1)}, f32[32,128]{1,0:T(8,128)S(1)}, u32[]{:S(2)}, u32[]{:S(2)}) collective-permute-start(f32[32,128]{1,0:T(8,128)S(1)} %get-tuple-element.110), channel_id=1, source_target_pairs={{0,8},{8,16},{16,24},{24,32},{32,40},{40,48},{48,56},{56,64},{64,7... | collective-permute-start | bytes 49160 | tf_op jit(solution)/shard_map/ppermute | solution.py:446
  137.8 5.8 %collective-permute-start.14 = (f32[32,128]{1,0:T(8,128)S(1)}, f32[32,128]{1,0:T(8,128)S(1)}, u32[]{:S(2)}, u32[]{:S(2)}) collective-permute-start(f32[32,128]{1,0:T(8,128)S(1)} %get-tuple-element.110), channel_id=1, source_target_pairs={{8,0},{16,8},{24,16},{32,24},{40,32},{48,40},{56,48},{64,56},{72,6... | collective-permute-start | bytes 49160 | tf_op jit(solution)/shard_map/ppermute | solution.py:446
  143.6 1.9 %collective-permute-start.12 = (f32[8,128]{1,0:T(8,128)S(1)}, f32[8,128]{1,0:T(8,128)S(1)}, u32[]{:S(2)}, u32[]{:S(2)}) collective-permute-start(f32[8,128]{1,0:T(8,128)S(1)} %slice.162), channel_id=1, source_target_pairs={{0,16},{8,24},{16,32},{24,40},{32,48},{40,56},{48,64},{56,72},{64,... | collective-permute-start | bytes 12296 | tf_op jit(solution)/shard_map/ppermute | solution.py:446
  145.6 5.2 %collective-permute-start.15 = (f32[24,128]{1,0:T(8,128)S(1)}, f32[24,128]{1,0:T(8,128)S(1)}, u32[]{:S(2)}, u32[]{:S(2)}) collective-permute-start(f32[24,128]{1,0:T(8,128)S(1)} %bitcast.30), channel_id=1, source_target_pairs={{8,0},{16,8},{24,16},{32,24},{40,32},{48,40},{56,48},{64,56},{72,6... | collective-permute-start | bytes 36872 | tf_op jit(solution)/shard_map/ppermute | solution.py:446
  150.8 0.4 collective-permute-done.12
  151.2 1.9 %collective-permute-start.13 = (f32[24,128]{1,0:T(8,128)S(1)}, f32[24,128]{1,0:T(8,128)S(1)}, u32[]{:S(2)}, u32[]{:S(2)}) collective-permute-start(f32[24,128]{1,0:T(8,128)S(1)} %bitcast.28), channel_id=1, source_target_pairs={{0,8},{8,16},{16,24},{24,32},{32,40},{40,48},{48,56},{56,64},{64,7... | collective-permute-start | bytes 36872 | tf_op jit(solution)/shard_map/ppermute | solution.py:446
  153.2 1.9 %fusion = f32[6,1024]{1,0:T(8,128)} fusion(f32[6,1024]{1,0:T(8,128)} %get-tuple-element.111, f32[32,128]{1,0:T(8,128)S(1)} %collective-permute-done.11, pred[]{:T(512)} %compare_reduce_fusion), kind=kLoop, calls=%fused_computation.9 | loop fusion | flops 1536 | bytes 11776 | tf_op jit(solution)/shard_map/scatter-add | solution.py:575
  155.1 3.3 %collective-permute-done.13.r0 = f32[24,128]{1,0:T(8,128)S(1)} collective-permute-done((f32[24,128]{1,0:T(8,128)S(1)}, f32[24,128]{1,0:T(8,128)S(1)}, u32[]{:S(2)}, u32[]{:S(2)}) %collective-permute-start.13) | collective-permute-done | bytes 12320 | tf_op jit(solution)/shard_map/ppermute | solution.py:446
  158.4 5.3 %shard_map.166 = f32[5,16,8,128]{3,2,1,0:T(8,128)} custom-call(s32[1]{0:T(128)} %bitcast.span, f32[5]{0:T(128)S(1)} %copy-done.13, f32[3,5,5]{2,1,0:T(8,128)S(1)} %copy.43.upwind, f32[3,5,5]{2,1,0:T(8,128)S(1)} %copy.44.downwind, f32[5,16,8,128]{3,2,1,0:T(8,128)S(1)} %get-tuple-element.92.base, f32[456,8,128]{2,1,0:T(8,128)S(1)} %get-tuple-element.90.full, ...), custom_call_target="tpu_custom_call" | custom-call | flops 8388608 | bytes 1048576 | tf_op jit(solution)/shard_map/pallas_call | solution.py:33
  (59 shorter events, 0.3 us)
Async XLA Ops:
  4.5 8.8 %collective-permute-start.4 = (f32[48,128]{1,0:T(8,128)}, f32[48,128]{1,0:T(8,128)S(1)}, u32[]{:S(2)}, u32[]{:S(2)}) collective-permute-start(f32[48,128]{1,0:T(8,128)} %get-tuple-element.95), channel_id=1, source_target_pairs={{8,0},{16,8},{24,16},{32,24},{40,32},{48,40},{56,48},{64,56},{72,6... | collective-permute-start | bytes 73736 | tf_op jit(solution)/shard_map/ppermute | solution.py:446
  8.1 0.8 copy-start.10
  8.9 0.7 copy-start.12
  9.5 69.0 %copy-start.11 = (f32[6,1024]{1,0:T(8,128)S(1)}, f32[6,1024]{1,0:T(8,128)}, u32[]{:S(2)}) copy-start(f32[6,1024]{1,0:T(8,128)} %get-tuple-element.103.refs_7_) | copy-start | bytes 73732
  13.3 0.9 copy-start
  14.2 0.8 copy-start.8
  15.0 63.5 %copy-start.1 = (f32[49,8,128]{2,1,0:T(8,128)S(1)}, f32[49,8,128]{2,1,0:T(8,128)}, u32[]{:S(2)}) copy-start(f32[49,8,128]{2,1,0:T(8,128)} %get-tuple-element.97.pack.refs_0_) | copy-start | bytes 602116
  15.0 63.5 %copy-start.2 = (f32[6,6,1024]{2,1,0:T(8,128)S(1)}, f32[6,6,1024]{2,1,0:T(8,128)}, u32[]{:S(2)}) copy-start(f32[6,6,1024]{2,1,0:T(8,128)} %get-tuple-element.96.refs_3_.precond) | copy-start | bytes 442372
  15.0 72.5 %copy-start.3 = (f32[228,8,128]{2,1,0:T(8,128)S(1)}, f32[228,8,128]{2,1,0:T(8,128)}, u32[]{:S(2)}) copy-start(f32[228,8,128]{2,1,0:T(8,128)} %get-tuple-element.87.planes) | copy-start | bytes 2801668
  15.9 9.6 %collective-permute-start.5 = (f32[9,8,128]{2,1,0:T(8,128)S(1)}, f32[9,8,128]{2,1,0:T(8,128)S(1)}, u32[]{:S(2)}, u32[]{:S(2)}) collective-permute-start(f32[9,8,128]{2,1,0:T(8,128)S(1)} %get-tuple-element.100), channel_id=1, source_target_pairs={{0,8},{8,16},{16,24},{24,32},{32,40},{40,48},{48,56},{56,64},{64,7... | collective-permute-start | bytes 110600 | tf_op jit(solution)/shard_map/ppermute | solution.py:446
  17.9 7.7 %collective-permute-start.6 = (f32[9,8,128]{2,1,0:T(8,128)S(1)}, f32[9,8,128]{2,1,0:T(8,128)S(1)}, u32[]{:S(2)}, u32[]{:S(2)}) collective-permute-start(f32[9,8,128]{2,1,0:T(8,128)S(1)} %get-tuple-element.101), channel_id=1, source_target_pairs={{8,0},{16,8},{24,16},{32,24},{40,32},{48,40},{56,48},{64,56},{72,6... | collective-permute-start | bytes 110600 | tf_op jit(solution)/shard_map/ppermute | solution.py:446
  23.6 5.5 %collective-permute-start.7 = (f32[8,128]{1,0:T(8,128)S(1)}, f32[8,128]{1,0:T(8,128)S(1)}, u32[]{:S(2)}, u32[]{:S(2)}) collective-permute-start(f32[8,128]{1,0:T(8,128)S(1)} %get-tuple-element.102), channel_id=1, source_target_pairs={{16,0},{24,8},{32,16},{40,24},{48,32},{56,40},{64,48},{72,56},{80,... | collective-permute-start | bytes 12296 | tf_op jit(solution)/shard_map/ppermute | solution.py:446
  29.8 12.6 %all-to-all-start = ((f32[4,9,8,128]{3,2,1,0:T(8,128)}), f32[4,9,8,128]{3,2,1,0:T(8,128)S(1)}, u32[]{:S(2)}, u32[]{:S(2)}) async-start(f32[4,9,8,128]{3,2,1,0:T(8,128)} %broadcast_in_dim.18), calls=%async_computation | async-start | bytes 294912 | tf_op jit(solution)/shard_map/all_to_all | solution.py:458
  34.7 51.2 %collective-permute-start = (f32[114,8,128]{2,1,0:T(8,128)}, f32[114,8,128]{2,1,0:T(8,128)S(1)}, u32[]{:S(2)}, u32[]{:S(2)}) collective-permute-start(f32[114,8,128]{2,1,0:T(8,128)} %get-tuple-element.88), channel_id=1, source_target_pairs={{0,8},{8,16},{16,24},{24,32},{32,40},{40,48},{48,56},{56,64},{64,7... | collective-permute-start | bytes 1400840 | tf_op jit(solution)/shard_map/ppermute | solution.py:446
  36.6 50.1 %collective-permute-start.1 = (f32[114,8,128]{2,1,0:T(8,128)}, f32[114,8,128]{2,1,0:T(8,128)S(1)}, u32[]{:S(2)}, u32[]{:S(2)}) collective-permute-start(f32[114,8,128]{2,1,0:T(8,128)} %get-tuple-element.89), channel_id=1, source_target_pairs={{8,0},{16,8},{24,16},{32,24},{40,32},{48,40},{56,48},{64,56},{72,6... | collective-permute-start | bytes 1400840 | tf_op jit(solution)/shard_map/ppermute | solution.py:446
  42.4 36.1 %collective-permute-start.8 = (f32[58,8,128]{2,1,0:T(8,128)S(1)}, f32[58,8,128]{2,1,0:T(8,128)S(1)}, u32[]{:S(2)}, u32[]{:S(2)}) collective-permute-start(f32[58,8,128]{2,1,0:T(8,128)S(1)} %pad_maximum_fusion), channel_id=1, source_target_pairs={{0,4},{1,5},{2,6},{3,7},{4,0},{5,1},{6,2},{7,3},{8,12},{9,13},{10,... | collective-permute-start | bytes 712712 | tf_op jit(solution)/shard_map/ppermute | solution.py:454
  81.0 42.1 %copy-start.14 = (f32[3,5,5]{2,0,1:T(4,128)S(1)}, f32[3,5,5]{2,0,1:T(4,128)}, u32[]{:S(2)}) copy-start(f32[3,5,5]{2,0,1:T(4,128)} %param.29) | copy-start | bytes 904
  81.0 18.5 %all-to-all-start.1 = ((f32[4,9,8,128]{3,2,1,0:T(8,128)}), f32[4,9,8,128]{3,2,1,0:T(8,128)}, u32[]{:S(2)}, u32[]{:S(2)}) async-start(f32[4,9,8,128]{3,2,1,0:T(8,128)} %get-tuple-element.105), calls=%async_computation.1 | async-start | bytes 294912 | tf_op jit(solution)/shard_map/all_to_all | solution.py:458
  85.9 0.8 copy-start.4
  86.7 0.8 copy-start.6
  87.5 1.0 copy-start.5
  88.5 1.0 copy-start.7
  92.9 42.3 %copy-start.9 = (f32[6,1024]{1,0:T(8,128)S(1)}, f32[6,1024]{1,0:T(8,128)}, u32[]{:S(2)}) copy-start(f32[6,1024]{1,0:T(8,128)} %get-tuple-element.94.shell) | copy-start | bytes 73732
  92.9 31.5 %collective-permute-start.2 = (f32[15,16,128]{2,1,0:T(8,128)}, f32[15,16,128]{2,1,0:T(8,128)S(1)}, u32[]{:S(2)}, u32[]{:S(2)}) collective-permute-start(f32[15,16,128]{2,1,0:T(8,128)} %get-tuple-element.91), channel_id=1, source_target_pairs={{0,1},{1,0},{2,3},{3,2},{4,5},{5,4},{6,7},{7,6},{8,9},{9,8},{10,11... | collective-permute-start | bytes 368648 | tf_op jit(solution)/shard_map/ppermute | solution.py:454
  94.9 29.5 %collective-permute-start.3 = (f32[15,16,128]{2,1,0:T(8,128)}, f32[15,16,128]{2,1,0:T(8,128)S(1)}, u32[]{:S(2)}, u32[]{:S(2)}) collective-permute-start(f32[15,16,128]{2,1,0:T(8,128)} %get-tuple-element.91), channel_id=1, source_target_pairs={{1,2},{2,1},{3,4},{4,3},{5,6},{6,5},{9,10},{10,9},{11,12},{12,11},... | collective-permute-start | bytes 368648 | tf_op jit(solution)/shard_map/ppermute | solution.py:523
  100.2 4.3 %collective-permute-start.10 = (f32[8,128]{1,0:T(8,128)S(1)}, f32[8,128]{1,0:T(8,128)S(1)}, u32[]{:S(2)}, u32[]{:S(2)}) collective-permute-start(f32[8,128]{1,0:T(8,128)S(1)} %broadcast_select_fusion), channel_id=1, source_target_pairs={{8,0},{16,8},{24,16},{32,24},{40,32},{48,40},{56,48},{64,56},{72,6... | collective-permute-start | bytes 12296 | tf_op jit(solution)/shard_map/ppermute | solution.py:446
  102.1 7.0 %collective-permute-start.9 = (f32[8,128]{1,0:T(8,128)S(1)}, f32[8,128]{1,0:T(8,128)S(1)}, u32[]{:S(2)}, u32[]{:S(2)}) collective-permute-start(f32[8,128]{1,0:T(8,128)S(1)} %get-tuple-element.113), channel_id=1, source_target_pairs={{0,8},{8,16},{16,24},{24,32},{32,40},{40,48},{48,56},{56,64},{64,7... | collective-permute-start | bytes 12296 | tf_op jit(solution)/shard_map/ppermute | solution.py:446
  109.2 49.2 %copy-start.13 = (f32[5]{0:T(128)S(1)}, f32[5]{0:T(128)}, u32[]{:S(2)}) copy-start(f32[5]{0:T(128)} %prow.3) | copy-start | bytes 64
  112.6 22.6 %all-to-all-start.2 = ((f32[4,9,8,128]{3,2,1,0:T(8,128)}), f32[4,9,8,128]{3,2,1,0:T(8,128)S(1)}, u32[]{:S(2)}, u32[]{:S(2)}) async-start(f32[4,9,8,128]{3,2,1,0:T(8,128)} %get-tuple-element.108), calls=%async_computation.2 | async-start | bytes 294912 | tf_op jit(solution)/shard_map/all_to_all | solution.py:458
  135.9 14.9 %collective-permute-start.11 = (f32[32,128]{1,0:T(8,128)S(1)}, f32[32,128]{1,0:T(8,128)S(1)}, u32[]{:S(2)}, u32[]{:S(2)}) collective-permute-start(f32[32,128]{1,0:T(8,128)S(1)} %get-tuple-element.110), channel_id=1, source_target_pairs={{0,8},{8,16},{16,24},{24,32},{32,40},{40,48},{48,56},{56,64},{64,7... | collective-permute-start | bytes 49160 | tf_op jit(solution)/shard_map/ppermute | solution.py:446
  137.8 7.7 %collective-permute-start.14 = (f32[32,128]{1,0:T(8,128)S(1)}, f32[32,128]{1,0:T(8,128)S(1)}, u32[]{:S(2)}, u32[]{:S(2)}) collective-permute-start(f32[32,128]{1,0:T(8,128)S(1)} %get-tuple-element.110), channel_id=1, source_target_pairs={{8,0},{16,8},{24,16},{32,24},{40,32},{48,40},{56,48},{64,56},{72,6... | collective-permute-start | bytes 49160 | tf_op jit(solution)/shard_map/ppermute | solution.py:446
  143.6 7.6 %collective-permute-start.12 = (f32[8,128]{1,0:T(8,128)S(1)}, f32[8,128]{1,0:T(8,128)S(1)}, u32[]{:S(2)}, u32[]{:S(2)}) collective-permute-start(f32[8,128]{1,0:T(8,128)S(1)} %slice.162), channel_id=1, source_target_pairs={{0,16},{8,24},{16,32},{24,40},{32,48},{40,56},{48,64},{56,72},{64,... | collective-permute-start | bytes 12296 | tf_op jit(solution)/shard_map/ppermute | solution.py:446
  145.6 9.4 %collective-permute-start.15 = (f32[24,128]{1,0:T(8,128)S(1)}, f32[24,128]{1,0:T(8,128)S(1)}, u32[]{:S(2)}, u32[]{:S(2)}) collective-permute-start(f32[24,128]{1,0:T(8,128)S(1)} %bitcast.30), channel_id=1, source_target_pairs={{8,0},{16,8},{24,16},{32,24},{40,32},{48,40},{56,48},{64,56},{72,6... | collective-permute-start | bytes 36872 | tf_op jit(solution)/shard_map/ppermute | solution.py:446
  151.2 7.1 %collective-permute-start.13 = (f32[24,128]{1,0:T(8,128)S(1)}, f32[24,128]{1,0:T(8,128)S(1)}, u32[]{:S(2)}, u32[]{:S(2)}) collective-permute-start(f32[24,128]{1,0:T(8,128)S(1)} %bitcast.28), channel_id=1, source_target_pairs={{0,8},{8,16},{16,24},{24,32},{32,40},{40,48},{48,56},{56,64},{64,7... | collective-permute-start | bytes 36872 | tf_op jit(solution)/shard_map/ppermute | solution.py:446

commit v3 on v2

--- a/solution.py
+++ b/solution.py
@@ -16,7 +16,6 @@
 LAYERS = 16
 NODE_DEV = 1024
 TILES = 9
-EXT = TILES * 128
 PLANES = 228
 HALF = PLANES // 2
 FIELDS = 15
@@ -94,11 +93,14 @@
         walls[j] = planes[16 * j]
     walls[5:9] = planes[224:228]
     low = iota((8, 128), 0) < 4
+    even = span[0] % 2 == 0
 
     def body(k, carry):
         a, b = planes[k], planes[k + HALF]
-        up[k] = jnp.where(low, pltpu.roll(a, 4, 0), b)
-        down[k] = jnp.where(low, a, pltpu.roll(b, 4, 0))
+        to_upper = jnp.where(low, pltpu.roll(a, 4, 0), b)
+        to_lower = jnp.where(low, a, pltpu.roll(b, 4, 0))
+        up[k] = jnp.where(even, to_upper, to_lower)
+        down[k] = jnp.where(even, to_lower, to_upper)
         return carry
 
     lax.fori_loop(0, HALF, body, 0, unroll=6)
@@ -111,15 +113,35 @@
     return jnp.concatenate([high, value - high], axis=0).astype(BF16)
 
 
-def stiff_apply(field, packs, onehot, uvec, fvec):
+def split_index(index, low_hot):
+    place = iota(low_hot.shape, 0) == (index & 127)
+    low_hot[...] = jnp.where(place, 1.0, 0.0).astype(BF16)
+    return index >> 7
+
+
+def scatter(values, tile, low_hot, tiles):
+    spread = jnp.concatenate([jnp.where(tile == t, values, 0.0) for t in range(tiles)], axis=0)
+    sums = lax.dot_general(
+        parts(spread), low_hot[...], (((1,), (1,)), ((), ())), preferred_element_type=F32
+    )
+    half = 8 * tiles
+    return [sums[8 * t : 8 * t + 8] + sums[half + 8 * t : half + 8 * t + 8] for t in range(tiles)]
+
+
+def stiff_apply(field, packs, index, low_hot, uvec, fvec):
     for q, pack in enumerate(packs):
         for a in range(4):
-            row = pack[48, a : a + 1, :].astype(jnp.int32)
             lane = (4 * q + a) * 128
-            hit = iota((EXT, 128), 0) == row
-            onehot[:, lane : lane + 128] = jnp.where(hit, 1.0, 0.0).astype(BF16)
-    picked = jnp.dot(parts(field), onehot[...], preferred_element_type=F32)
-    picked = picked[0:8] + picked[8:16]
+            index[0:1, lane : lane + 128] = pack[48, a : a + 1, :].astype(jnp.int32)
+    tile = split_index(index[0:1, :], low_hot)
+    found = jnp.dot(
+        parts(jnp.concatenate(field, axis=0)), low_hot[...], preferred_element_type=F32
+    )
+    half = 8 * TILES
+    picked = jnp.zeros((8, low_hot.shape[1]), F32)
+    for t in range(TILES):
+        value = found[8 * t : 8 * t + 8] + found[half + 8 * t : half + 8 * t + 8]
+        picked = jnp.where(tile == t, value, picked)
     for q, pack in enumerate(packs):
         for a in range(4):
             lane = (4 * q + a) * 128
@@ -139,13 +161,10 @@
             lane = (4 * q + a) * 128
             fvec[0:6, lane : lane + 128] = uvec[6 * a : 6 * a + 6, :]
             fvec[6:8, lane : lane + 128] = jnp.zeros((2, 128), F32)
-    forces = lax.dot_general(
-        parts(fvec[...]), onehot[...], (((1,), (1,)), ((), ())), preferred_element_type=F32
-    )
-    return forces[0:8] + forces[8:16]
-
-
-def load_kernel(span, prow, walls, loads, faces, nodes):
+    return scatter(fvec[...], tile, low_hot, TILES)
+
+
+def load_kernel(span, prow, walls, loads, faces, nodes, low_hot):
     press = prow[0] * walls[0]
     for j in range(1, 5):
         press = press + prow[j] * walls[j]
@@ -157,37 +176,31 @@
         load = walls[5 + i] * press
         for r in range(8):
             faces[i : i + 1, r * 128 : r * 128 + 128] = load[r : r + 1]
-    face_parts = parts(faces[...])
-    node_row = nodes[0:1, :]
-
-    def chunk(b, carry):
-        hit = iota((256, 1024), 0) + b * 256 == node_row
-        hot = jnp.where(hit, 1.0, 0.0).astype(BF16)
-        got = lax.dot_general(
-            face_parts, hot, (((1,), (1,)), ((), ())), preferred_element_type=F32
-        )
-        got = got[0:8] + got[8:16]
-        loads[2 * b] = got[:, 0:128]
-        loads[2 * b + 1] = got[:, 128:256]
-        return carry
-
-    lax.fori_loop(0, 12, chunk, 0)
-
-
-def first_kernel(loads, shell, rim, pack, own, up, down, down2, field, onehot, uvec, fvec):
-    field[...] = jnp.zeros((8, EXT), F32)
-    field[0:6, 0:NODE_DEV] = shell[...]
-    field[0:6, NODE_DEV:EXT] = rim[0:6, :]
-    force = stiff_apply(field[...], (pack,), onehot, uvec, fvec)
+    tile = split_index(nodes[0:1, :], low_hot)
+    for t, value in enumerate(scatter(faces[...], tile, low_hot, 24)):
+        loads[t] = value
+
+
+def first_kernel(
+    span, loads, shell, rim, pack, own, inside, across, down2, index, low_hot, uvec, fvec
+):
+    zero = jnp.zeros((2, 128), F32)
+    field = [shell[:, t * 128 : t * 128 + 128] for t in range(8)] + [rim[0:6, :]]
+    field = [jnp.concatenate([value, zero], axis=0) for value in field]
+    force = stiff_apply(field, (pack,), index, low_hot, uvec, fvec)
     lead = iota((8, 128), 1) < NB
+    even = span[0] % 2 == 0
+
+    def send(t, to_upper, to_lower):
+        inside[t] = jnp.where(even, to_upper, to_lower)
+        across[t] = jnp.where(even, to_lower, to_upper)
+
     for t in range(8):
-        own[t] = force[:, t * 128 : t * 128 + 128] + loads[8 + t]
-        up[t] = loads[16 + t]
-        down[t] = loads[t]
-    edge = force[:, NODE_DEV:EXT]
+        own[t] = force[t] + loads[8 + t]
+        send(t, loads[16 + t], loads[t])
+    edge = force[8]
     own[8] = edge + jnp.where(lead, loads[16], 0.0)
-    up[8] = edge
-    down[8] = jnp.where(lead, force[:, 0:128] + loads[8], 0.0)
+    send(8, edge, jnp.where(lead, force[0] + loads[8], 0.0))
     down2[...] = jnp.where(lead, loads[0], 0.0)
 
 
@@ -221,18 +234,19 @@
 
 
 def step_kernel(first, *refs):
-    refs, (res_out, sum_out, force_out, field, onehot, uvec, fvec) = refs[:-7], refs[-7:]
+    refs, (res_out, sum_out, force_out, index, low_hot, uvec, fvec) = refs[:-7], refs[-7:]
     own_pack, far_pack, rim, precond, prev_sum = refs[:5]
+    field = []
     for t in range(TILES):
         res = shell_residual(first, t, refs[5:])
         res_out[t] = res
         delta = precondition(t, precond, rim, res)
         sum_out[t] = delta if first else prev_sum[t] + delta
-        field[:, t * 128 : t * 128 + 128] = delta
-    force = stiff_apply(field[...], (own_pack, far_pack), onehot, uvec, fvec)
+        field.append(delta)
+    force = stiff_apply(field, (own_pack, far_pack), index, low_hot, uvec, fvec)
     for t in range(TILES):
         for q in range(RING):
-            force_out[q, t] = force[:, t * 128 : t * 128 + 128]
+            force_out[q, t] = force[t]
 
 
 def last_kernel(shell, rim, precond, prev_sum, force, prev, shell_out, reach_out):
@@ -245,12 +259,14 @@
     reach_out[24:32, :] = -precondition(8, precond, rim, ring_total(force, 8))
 
 
-def pack_chord_kernel(planes, from_lower, from_upper, full, edges):
+def pack_chord_kernel(span, planes, inside, across, full, edges):
     low = iota((8, 128), 0) < 4
     full[0:PLANES] = planes[...]
+    even = span[0] % 2 == 0
 
     def unpack(k, carry):
-        a, b = from_upper[k], from_lower[k]
+        x, y = inside[k], across[k]
+        a, b = jnp.where(even, x, y), jnp.where(even, y, x)
         full[PLANES + k] = jnp.where(low, a, pltpu.roll(b, 4, 0))
         full[PLANES + HALF + k] = jnp.where(low, pltpu.roll(a, 4, 0), b)
         return carry
@@ -390,12 +406,17 @@
 
 
 def final_kernel(
-    span, prow, upwind, downwind, base, full, edges, r0, r1, r2, r3, r4,
-    out, reach, state, halo, first, last, rolled,
+    span, prow, upwind, downwind, base, full, edges, across, r1, r2, r3, inside, shell, part,
+    out, shell_out, reach, state, halo, first, last, rolled,
 ):
-    for b, ref in enumerate((r0, r1, r2, r3, r4)):
+    shell_out[...] = shell[...]
+    shell_out[:, 0:128] = shell[:, 0:128] + part[24:30, :]
+    even = span[0] % 2 == 0
+    x, y = across[...], inside[...]
+    blocks = (jnp.where(even, x, y), r1[...], r2[...], r3[...], jnp.where(even, y, x))
+    for b, value in enumerate(blocks):
         for i in range(3):
-            reach[40 * i + 8 * b : 40 * i + 8 * b + 8, :] = ref[8 * i : 8 * i + 8, :]
+            reach[40 * i + 8 * b : 40 * i + 8 * b + 8, :] = value[8 * i : 8 * i + 8]
     walls = edges[FIELDS - 1]
     wall_planes = [pltpu.roll(walls, 128 - 8 * i, 1) if i else walls for i in range(4)]
     node = jnp.concatenate([tall(full, 227), wall_planes[3]], axis=0)
@@ -446,6 +467,24 @@
     return lax.ppermute(value, "span", [(i, i + steps) for i in range(first, last)])
 
 
+def exchange(to_upper, to_lower):
+    even = lax.axis_index("span") % 2 == 0
+    count = lax.axis_size("span")
+    across = jnp.where(even, to_lower, to_upper)
+    across = lax.ppermute(across, "span", cross_pairs(count))
+    inside = jnp.where(even, to_upper, to_lower)
+    inside = lax.ppermute(inside, "span", inside_pairs(count))
+    return jnp.where(even, across, inside), jnp.where(even, inside, across)
+
+
+def cross_pairs(count):
+    return [(s, s - 1 + 2 * (s % 2)) for s in range(1, count - 1)]
+
+
+def inside_pairs(count):
+    return [(s, s ^ 1) for s in range(count)]
+
+
 CHORD = ("far_z", "y")
 
 
@@ -464,7 +503,7 @@
 ):
     span = lax.axis_index("span").astype(jnp.int32).reshape(1)
     odd = (lax.axis_index("y") % 2).astype(jnp.int32).reshape(1)
-    pack, rim, planes, to_upper, to_lower, shell, sgrad, precond, walls = call(
+    pack, rim, planes, to_inside, to_across, shell, sgrad, precond, walls = call(
         front_kernel,
         (
             sds(PACKED, 8, 128), sds(48, 128), sds(PLANES, 8, 128), sds(HALF, 8, 128),
@@ -484,38 +523,45 @@
         vmem=60,
     )
     rim = along_span(rim, -1)
-    from_lower = along_span(to_upper, 1)
-    from_upper = along_span(to_lower, -1)
+    spans = lax.axis_size("span")
+    halo_across = lax.ppermute(to_across, "span", cross_pairs(spans))
+    halo_inside = lax.ppermute(to_inside, "span", inside_pairs(spans))
     loads = call(
         load_kernel,
         sds(24, 8, 128),
         (span, pressure_row, walls),
         [SM] * 2 + [VM],
         4 << 20,
-        (pltpu.VMEM((8, 1024), F32), pltpu.VMEM((8, 1024), jnp.int32)),
+        (
+            pltpu.VMEM((8, 1024), F32),
+            pltpu.VMEM((8, 1024), jnp.int32),
+            pltpu.VMEM((128, 1024), BF16),
+        ),
     )
     apply_scratch = lambda nb: (
-        pltpu.VMEM((8, EXT), F32),
-        pltpu.VMEM((EXT, 512 * nb), BF16),
+        pltpu.VMEM((8, 512 * nb), jnp.int32),
+        pltpu.VMEM((128, 512 * nb), BF16),
         pltpu.VMEM((24, 128), F32),
         pltpu.VMEM((8, 512 * nb), F32),
     )
-    own, up, down, down2 = call(
+    own, inside, across, down2 = call(
         first_kernel,
         (sds(TILES, 8, 128), sds(TILES, 8, 128), sds(TILES, 8, 128), sds(8, 128)),
-        (loads, shell, rim, pack),
-        [VM] * 4,
+        (span, loads, shell, rim, pack),
+        [SM] + [VM] * 4,
         4 << 20,
         apply_scratch(1),
     )
-    up = along_span(up, 1)
-    down = along_span(down, -1)
+    across = lax.ppermute(across, "span", cross_pairs(spans))
+    inside = lax.ppermute(inside, "span", inside_pairs(spans))
+    even = span[0] % 2 == 0
+    up, down = jnp.where(even, across, inside), jnp.where(even, inside, across)
     down2 = along_span(down2, -2)
     full, edges = call(
         pack_chord_kernel,
         (sds(SLOTS, 8, 128), sds(FIELDS, 16, 128)),
-        (planes, from_lower, from_upper),
-        [VM] * 3,
+        (span, planes, halo_inside, halo_across),
+        [SM] + [VM] * 3,
         4 << 20,
     )
     count = lax.axis_size(CHORD)
@@ -557,10 +603,7 @@
         force = ring_parts(force)
         pieces = (force, res)
         if turn == 0:
-            pieces += (
-                along_span(force[:, 8].sum(0), 1),
-                along_span(jnp.where(lead, force[:, 0].sum(0), 0.0), -1),
-            )
+            pieces += exchange(force[:, 8].sum(0), jnp.where(lead, force[:, 0].sum(0), 0.0))
     shell, reach = call(
         last_kernel,
         (sds(6, NODE_DEV), sds(32, 128)),
@@ -568,18 +611,22 @@
         [VM] * (4 + len(pieces)),
         1 << 20,
     )
-    below, above, lower = along_span(reach, 1), along_span(reach, -1), along_span(reach[24:], 2)
+    lower = along_span(reach[24:], 2)
+    below, above = exchange(reach, reach)
     mend = lambda value, part: (
         value[:24].reshape(3, 8, 128).at[:, 0].add(part[:3]).reshape(24, 128)
     )
-    shell = shell.at[:, :128].add(below[24:30])
+    part = below
     reach, below, above = mend(reach, below[24:]), mend(below, lower), mend(above, reach[24:])
-    reaches = (along_span(below, 1), below, reach, above, along_span(above, -1))
-    flow = call(
+    even = span[0] % 2 == 0
+    across = lax.ppermute(jnp.where(even, above, below), "span", cross_pairs(spans))
+    inside = lax.ppermute(jnp.where(even, below, above), "span", inside_pairs(spans))
+    reaches = (across, below, reach, above, inside, shell, part)
+    flow, shell = call(
         final_kernel,
-        sds(5, LAYERS, 8, 128),
+        (sds(5, LAYERS, 8, 128), sds(6, NODE_DEV)),
         (span, pressure_row, upwind, downwind, base, full, edges, *reaches),
-        [SM] * 4 + [VM] * 8,
+        [SM] * 4 + [VM] * 10,
         8 << 20,
         (pltpu.VMEM((120, 128), F32), *scratch(SW)),
     )

time: 165 us -> 159 us (0.964)
  the two profiles are of different devices: /device:TPU:40 before, /device:TPU:416 now
where the time goes in v3:
time: 159 us; the launch traced here: 158 us
  starting transfers between devices  68.7 us (43%)
  waiting for transfers between devices  40.7 us (26%)
  Pallas kernels  26.9 us (17%)
  blocking collectives  10.3 us (6%)
  local copies, waits for them, and re-layouts  8.25 us (5%)
  between operations  1.79 us (1%)
    pallas_call x9, Pallas kernels, call(): pl.pallas_call(body, out_shape=out, in_specs=specs, out_specs=jax.tree.ma...  26.9 us
    ppermute x2, starting transfers between devices, exchange(): across = lax.ppermute(across, 'span', cross_pairs(count))  20.8 us
    ppermute x2, waiting for transfers between devices, swap(): return lax.ppermute(value, CHORD, [(c, c ^ bit) for c in range(count)])  14.2 us
    all_to_all x1, blocking collectives, ring_parts(): return lax.all_to_all(copies, 'y', 0, 0)  10.3 us
    ppermute x3, starting transfers between devices, along_span(): lax.ppermute(value, 'span', [(i, i + steps) for i in range(first, last)])  9.52 us
    ppermute x1, waiting for transfers between devices, per_device(): far = lax.ppermute(edges, CHORD, pairs)  9.32 us
    all_to_all x2, starting transfers between devices, ring_parts(): return lax.all_to_all(copies, 'y', 0, 0)  8.25 us
    unnamed x38, local copies, waits for them, and re-layouts  8.1 us
  transfers between devices with their start and end apart: 18, of which 6 were waited for; matrix products, arithmetic and copies ran while one was open for 1% of the time, Pallas kernels for 11%

profile of v3, /device:TPU:416, one launch (start us, length us, event | category | flops | bytes accessed | tf_op | source)
XLA Modules:
  0.0 157.8 jit_solution(11558427814392425778)
XLA Ops:
  1.3 3.2 %shard_map.158 = (f32[49,8,128]{2,1,0:T(8,128)}, f32[48,128]{1,0:T(8,128)}, f32[228,8,128]{2,1,0:T(8,128)}, f32[114,8,128]{2,1,0:T(8,128)}, f32[114,8,128]{2,1,0...) custom-call(s32[1]{0:T(128)} %bitcast.span, ...), custom_call_target="tpu_custom_call" | custom-call | flops 4194304 | bytes 524288 | tf_op jit(solution)/shard_map/pallas_call | solution.py:32
  4.5 4.5 %collective-permute-start.4 = (f32[48,128]{1,0:T(8,128)}, f32[48,128]{1,0:T(8,128)S(1)}, u32[]{:S(2)}, u32[]{:S(2)}) collective-permute-start(f32[48,128]{1,0:T(8,128)} %get-tuple-element.83), channel_id=1, source_target_pairs={{8,0},{16,8},{24,16},{32,24},{40,32},{48,40},{56,48},{64,56},{72,6... | collective-permute-start | bytes 73736 | tf_op jit(solution)/shard_map/ppermute | solution.py:467
  9.1 0.8 copy-done.12
  9.8 0.7 copy-done.14
  10.5 1.0 shard_map.161.loads
  11.5 0.0 collective-permute-done.4.rim.refs_2_.refs_8_
  11.5 0.0 copy-start
  11.5 0.9 copy-done
  12.5 0.8 copy-done.10
  13.2 0.4 shard_map.162
  13.7 5.1 %collective-permute-start.5 = (f32[9,8,128]{2,1,0:T(8,128)S(1)}, f32[9,8,128]{2,1,0:T(8,128)S(1)}, u32[]{:S(2)}, u32[]{:S(2)}) collective-permute-start(f32[9,8,128]{2,1,0:T(8,128)S(1)} %get-tuple-element.88), channel_id=1, source_target_pairs={{8,16},{16,8},{24,32},{32,24},{40,48},{48,40},{56,64},{64,56},{72,... | collective-permute-start | bytes 110600 | tf_op jit(solution)/shard_map/ppermute | solution.py:555
  18.8 1.9 %collective-permute-start.6 = (f32[9,8,128]{2,1,0:T(8,128)S(1)}, f32[9,8,128]{2,1,0:T(8,128)S(1)}, u32[]{:S(2)}, u32[]{:S(2)}) collective-permute-start(f32[9,8,128]{2,1,0:T(8,128)S(1)} %get-tuple-element.89), channel_id=1, source_target_pairs={{0,8},{8,0},{16,24},{24,16},{32,40},{40,32},{48,56},{56,48},{64,72... | collective-permute-start | bytes 110600 | tf_op jit(solution)/shard_map/ppermute | solution.py:556
  20.7 3.1 %collective-permute-start.7 = (f32[8,128]{1,0:T(8,128)S(1)}, f32[8,128]{1,0:T(8,128)S(1)}, u32[]{:S(2)}, u32[]{:S(2)}) collective-permute-start(f32[8,128]{1,0:T(8,128)S(1)} %get-tuple-element.90), channel_id=1, source_target_pairs={{16,0},{24,8},{32,16},{40,24},{48,32},{56,40},{64,48},{72,56},{80,... | collective-permute-start | bytes 12296 | tf_op jit(solution)/shard_map/ppermute | solution.py:467
  23.9 2.4 %collective-permute-done.7 = f32[8,128]{1,0:T(8,128)S(1)} collective-permute-done((f32[8,128]{1,0:T(8,128)S(1)}, f32[8,128]{1,0:T(8,128)S(1)}, u32[]{:S(2)}, u32[]{:S(2)}) %collective-permute-start.7) | collective-permute-done | bytes 4128 | tf_op jit(solution)/shard_map/ppermute | solution.py:467
  26.3 10.3 %all_to_all.15 = f32[4,9,8,128]{3,2,1,0:T(8,128)S(1)} all-to-all(f32[4,9,8,128]{3,2,1,0:T(8,128)S(1)} %broadcast_in_dim.18), channel_id=1, replica_groups=mesh['span'=64,'far_z'=2,'y'=4] {'y'}, dimensions={0} | all-to-all | bytes 294912 | tf_op jit(solution)/shard_map/all_to_all | solution.py:497
  36.6 0.9 pad_maximum_fusion
  37.6 3.6 %collective-permute-start.8 = (f32[58,8,128]{2,1,0:T(8,128)S(1)}, f32[58,8,128]{2,1,0:T(8,128)S(1)}, u32[]{:S(2)}, u32[]{:S(2)}) collective-permute-start(f32[58,8,128]{2,1,0:T(8,128)S(1)} %pad_maximum_fusion), channel_id=1, source_target_pairs={{0,4},{1,5},{2,6},{3,7},{4,0},{5,1},{6,2},{7,3},{8,12},{9,13},{10,... | collective-permute-start | bytes 712712 | tf_op jit(solution)/shard_map/ppermute | solution.py:493
  41.2 1.9 %collective-permute-start = (f32[114,8,128]{2,1,0:T(8,128)}, f32[114,8,128]{2,1,0:T(8,128)S(1)}, u32[]{:S(2)}, u32[]{:S(2)}) collective-permute-start(f32[114,8,128]{2,1,0:T(8,128)} %get-tuple-element.76), channel_id=1, source_target_pairs={{0,8},{8,0},{16,24},{24,16},{32,40},{40,32},{48,56},{56,48},{64,72... | collective-permute-start | bytes 1400840 | tf_op jit(solution)/shard_map/ppermute | solution.py:528
  43.2 5.3 %collective-permute-start.1 = (f32[114,8,128]{2,1,0:T(8,128)S(1)}, f32[114,8,128]{2,1,0:T(8,128)S(1)}, u32[]{:S(2)}, u32[]{:S(2)}) collective-permute-start(f32[114,8,128]{2,1,0:T(8,128)S(1)} %copy-done.17), channel_id=1, source_target_pairs={{8,16},{16,8},{24,32},{32,24},{40,48},{48,40},{56,64},{64,56},{72,... | collective-permute-start | bytes 1400840 | tf_op jit(solution)/shard_map/ppermute | solution.py:527
  48.4 14.2 %collective-permute-done.8.refs_1_.refs_6_ = f32[58,8,128]{2,1,0:T(8,128)S(1)} collective-permute-done((f32[58,8,128]{2,1,0:T(8,128)S(1)}, f32[58,8,128]{2,1,0:T(8,128)S(1)}, u32[]{:S(2)}, u32[]{:S(2)}) %collective-permute-start.8) | collective-permute-done | bytes 237600 | tf_op jit(solution)/shard_map/ppermute | solution.py:493
  62.7 1.4 shard_map.163
  64.1 3.5 %all-to-all-start.1 = ((f32[4,9,8,128]{3,2,1,0:T(8,128)}), f32[4,9,8,128]{3,2,1,0:T(8,128)S(1)}, u32[]{:S(2)}, u32[]{:S(2)}) async-start(f32[4,9,8,128]{3,2,1,0:T(8,128)} %get-tuple-element.93), calls=%async_computation.1 | async-start | bytes 294912 | tf_op jit(solution)/shard_map/all_to_all | solution.py:497
  67.5 6.0 %all-to-all-done.1.refs_5_ = f32[4,9,8,128]{3,2,1,0:T(8,128)S(1)} async-done(((f32[4,9,8,128]{3,2,1,0:T(8,128)}), f32[4,9,8,128]{3,2,1,0:T(8,128)S(1)}, u32[]{:S(2)}, u32[]{:S(2)}) %all-to-all-start.1) | async-done | bytes 147488 | tf_op jit(solution)/shard_map/all_to_all | solution.py:497
  73.6 0.7 copy-done.4
  74.2 2.0 %collective-permute-start.10 = (f32[8,128]{1,0:T(8,128)S(1)}, f32[8,128]{1,0:T(8,128)S(1)}, u32[]{:S(2)}, u32[]{:S(2)}) collective-permute-start(f32[8,128]{1,0:T(8,128)S(1)} %get-tuple-element.106), channel_id=1, source_target_pairs={{0,8},{8,0},{16,24},{24,16},{32,40},{40,32},{48,56},{56,48},{64,72... | collective-permute-start | bytes 12296 | tf_op jit(solution)/shard_map/ppermute | solution.py:476
  76.3 13.4 %collective-permute-start.9 = (f32[8,128]{1,0:T(8,128)S(1)}, f32[8,128]{1,0:T(8,128)S(1)}, u32[]{:S(2)}, u32[]{:S(2)}) collective-permute-start(f32[8,128]{1,0:T(8,128)S(1)} %get-tuple-element.107), channel_id=1, source_target_pairs={{8,16},{16,8},{24,32},{32,24},{40,48},{48,40},{56,64},{64,56},{72,... | collective-permute-start | bytes 12296 | tf_op jit(solution)/shard_map/ppermute | solution.py:474
  89.7 0.8 copy-done.6
  90.5 0.8 copy-done.8
  91.3 1.0 copy-done.7
  92.3 1.0 copy-done.9
  93.3 3.4 %shard_map.159 = (f32[456,8,128]{2,1,0:T(8,128)S(1)}, f32[15,16,128]{2,1,0:T(8,128)}) custom-call(s32[1]{0:T(128)} %bitcast.span, f32[228,8,128]{2,1,0:T(8,128)S(1)} %copy-done.3, f32[114,8,128]{2,1,0:T(8,128)S(1)} %copy-done.7, f32[114,8,128]{2,1,0:T(8,128)S(1)} %copy-done.9), custom_call_target="tpu_custom_call" | custom-call | flops 4194304 | bytes 524288 | tf_op jit(solution)/shard_map/pallas_call | solution.py:32
  96.7 2.6 %collective-permute-start.2 = (f32[15,16,128]{2,1,0:T(8,128)}, f32[15,16,128]{2,1,0:T(8,128)S(1)}, u32[]{:S(2)}, u32[]{:S(2)}) collective-permute-start(f32[15,16,128]{2,1,0:T(8,128)} %get-tuple-element.79), channel_id=1, source_target_pairs={{0,1},{1,0},{2,3},{3,2},{4,5},{5,4},{6,7},{7,6},{8,9},{9,8},{10,11... | collective-permute-start | bytes 368648 | tf_op jit(solution)/shard_map/ppermute | solution.py:493
  99.3 1.9 %collective-permute-start.3 = (f32[15,16,128]{2,1,0:T(8,128)}, f32[15,16,128]{2,1,0:T(8,128)S(1)}, u32[]{:S(2)}, u32[]{:S(2)}) collective-permute-start(f32[15,16,128]{2,1,0:T(8,128)} %get-tuple-element.79), channel_id=1, source_target_pairs={{1,2},{2,1},{3,4},{4,3},{5,6},{6,5},{9,10},{10,9},{11,12},{12,11},... | collective-permute-start | bytes 368648 | tf_op jit(solution)/shard_map/ppermute | solution.py:569
  101.3 0.0 copy-start.15
  101.3 1.4 shard_map.164
  102.6 4.8 %all-to-all-start.2 = ((f32[4,9,8,128]{3,2,1,0:T(8,128)}), f32[4,9,8,128]{3,2,1,0:T(8,128)S(1)}, u32[]{:S(2)}, u32[]{:S(2)}) async-start(f32[4,9,8,128]{3,2,1,0:T(8,128)} %get-tuple-element.96), calls=%async_computation.2 | async-start | bytes 294912 | tf_op jit(solution)/shard_map/all_to_all | solution.py:497
  107.4 0.7 copy.44.downwind
  108.1 9.3 %collective-permute-done.3.far = f32[15,16,128]{2,1,0:T(8,128)S(1)} collective-permute-done((f32[15,16,128]{2,1,0:T(8,128)}, f32[15,16,128]{2,1,0:T(8,128)S(1)}, u32[]{:S(2)}, u32[]{:S(2)}) %collective-permute-start.3) | collective-permute-done | bytes 122912 | tf_op jit(solution)/shard_map/ppermute | solution.py:569
  117.5 10.7 %shard_map.160 = (f32[5,16,8,128]{3,2,1,0:T(8,128)S(1)}, f32[15,16,128]{2,1,0:T(8,128)S(1)}) custom-call(s32[1]{0:T(128)} %bitcast.1.odd, f32[456,8,128]{2,1,0:T(8,128)S(1)} %get-tuple-element.78.full, f32[15,16,128]{2,1,0:T(8,128)S(1)} %collective-permute-done.2.near, f32[15,16,128]{2,1,0:T(8,128)S(1)} %collective-permute-done.3.far, ...), custom_call_target="tpu_custom_call" | custom-call | flops 16777216 | bytes 2097152 | tf_op jit(solution)/shard_map/pallas_call | solution.py:32
  128.2 0.1 shard_map.165
  128.3 1.9 %collective-permute-start.11 = (f32[32,128]{1,0:T(8,128)S(1)}, f32[32,128]{1,0:T(8,128)S(1)}, u32[]{:S(2)}, u32[]{:S(2)}) collective-permute-start(f32[32,128]{1,0:T(8,128)S(1)} %get-tuple-element.98), channel_id=1, source_target_pairs={{0,8},{8,0},{16,24},{24,16},{32,40},{40,32},{48,56},{56,48},{64,72... | collective-permute-start | bytes 49160 | tf_op jit(solution)/shard_map/ppermute | solution.py:476
  130.2 7.4 %collective-permute-start.12 = (f32[32,128]{1,0:T(8,128)S(1)}, f32[32,128]{1,0:T(8,128)S(1)}, u32[]{:S(2)}, u32[]{:S(2)}) collective-permute-start(f32[32,128]{1,0:T(8,128)S(1)} %get-tuple-element.98), channel_id=1, source_target_pairs={{8,16},{16,8},{24,32},{32,24},{40,48},{48,40},{56,64},{64,56},{72,... | collective-permute-start | bytes 49160 | tf_op jit(solution)/shard_map/ppermute | solution.py:474
  137.7 1.9 %collective-permute-start.13 = (f32[8,128]{1,0:T(8,128)S(1)}, f32[8,128]{1,0:T(8,128)S(1)}, u32[]{:S(2)}, u32[]{:S(2)}) collective-permute-start(f32[8,128]{1,0:T(8,128)S(1)} %slice.143), channel_id=1, source_target_pairs={{0,16},{8,24},{16,32},{24,40},{32,48},{40,56},{48,64},{56,72},{64,... | collective-permute-start | bytes 12296 | tf_op jit(solution)/shard_map/ppermute | solution.py:467
  139.8 5.5 %collective-permute-done.13 = f32[8,128]{1,0:T(8,128)S(1)} collective-permute-done((f32[8,128]{1,0:T(8,128)S(1)}, f32[8,128]{1,0:T(8,128)S(1)}, u32[]{:S(2)}, u32[]{:S(2)}) %collective-permute-start.13) | collective-permute-done | bytes 4128 | tf_op jit(solution)/shard_map/ppermute | solution.py:467
  145.3 1.9 %collective-permute-start.14 = (f32[24,128]{1,0:T(8,128)S(1)}, f32[24,128]{1,0:T(8,128)S(1)}, u32[]{:S(2)}, u32[]{:S(2)}) collective-permute-start(f32[24,128]{1,0:T(8,128)S(1)} %get-tuple-element.105), channel_id=1, source_target_pairs={{8,16},{16,8},{24,32},{32,24},{40,48},{48,40},{56,64},{64,56},{72,... | collective-permute-start | bytes 36872 | tf_op jit(solution)/shard_map/ppermute | solution.py:622
  147.3 1.9 %collective-permute-start.15 = (f32[24,128]{1,0:T(8,128)S(1)}, f32[24,128]{1,0:T(8,128)S(1)}, u32[]{:S(2)}, u32[]{:S(2)}) collective-permute-start(f32[24,128]{1,0:T(8,128)S(1)} %get-tuple-element.104), channel_id=1, source_target_pairs={{0,8},{8,0},{16,24},{24,16},{32,40},{40,32},{48,56},{56,48},{64,72... | collective-permute-start | bytes 36872 | tf_op jit(solution)/shard_map/ppermute | solution.py:623
  149.3 3.2 %collective-permute-done.14.across = f32[24,128]{1,0:T(8,128)S(1)} collective-permute-done((f32[24,128]{1,0:T(8,128)S(1)}, f32[24,128]{1,0:T(8,128)S(1)}, u32[]{:S(2)}, u32[]{:S(2)}) %collective-permute-start.14) | collective-permute-done | bytes 12320 | tf_op jit(solution)/shard_map/ppermute | solution.py:622
  152.5 5.3 %shard_map.166 = (f32[5,16,8,128]{3,2,1,0:T(8,128)}, f32[6,1024]{1,0:T(8,128)}) custom-call(s32[1]{0:T(128)} %bitcast.span, f32[5]{0:T(128)S(1)} %copy-done.15, f32[3,5,5]{2,1,0:T(8,128)S(1)} %copy.43.upwind, f32[3,5,5]{2,1,0:T(8,128)S(1)} %copy.44.downwind, f32[5,16,8,128]{3,2,1,0:T(8,128)S(1)} %get-tuple-element.80.base, ...), custom_call_target="tpu_custom_call" | custom-call | flops 8388608 | bytes 1048576 | tf_op jit(solution)/shard_map/pallas_call | solution.py:32
  (66 shorter events, 0.3 us)
Async XLA Ops:
  4.5 7.0 %collective-permute-start.4 = (f32[48,128]{1,0:T(8,128)}, f32[48,128]{1,0:T(8,128)S(1)}, u32[]{:S(2)}, u32[]{:S(2)}) collective-permute-start(f32[48,128]{1,0:T(8,128)} %get-tuple-element.83), channel_id=1, source_target_pairs={{8,0},{16,8},{24,16},{32,24},{40,32},{48,40},{56,48},{64,56},{72,6... | collective-permute-start | bytes 73736 | tf_op jit(solution)/shard_map/ppermute | solution.py:467
  9.1 0.8 copy-start.12
  9.8 0.7 copy-start.14
  10.5 52.2 %copy-start.13 = (f32[6,1024]{1,0:T(8,128)S(1)}, f32[6,1024]{1,0:T(8,128)}, u32[]{:S(2)}) copy-start(f32[6,1024]{1,0:T(8,128)} %get-tuple-element.91.refs_7_) | copy-start | bytes 73732
  11.5 0.9 copy-start
  12.5 0.8 copy-start.10
  13.2 29.9 %copy-start.17 = (f32[114,8,128]{2,1,0:T(8,128)S(1)}, f32[114,8,128]{2,1,0:T(8,128)}, u32[]{:S(2)}) copy-start(f32[114,8,128]{2,1,0:T(8,128)} %get-tuple-element.77) | copy-start | bytes 1400836
  13.2 49.5 %copy-start.1 = (f32[49,8,128]{2,1,0:T(8,128)S(1)}, f32[49,8,128]{2,1,0:T(8,128)}, u32[]{:S(2)}) copy-start(f32[49,8,128]{2,1,0:T(8,128)} %get-tuple-element.85.pack.refs_0_) | copy-start | bytes 602116
  13.2 49.5 %copy-start.2 = (f32[6,6,1024]{2,1,0:T(8,128)S(1)}, f32[6,6,1024]{2,1,0:T(8,128)}, u32[]{:S(2)}) copy-start(f32[6,6,1024]{2,1,0:T(8,128)} %get-tuple-element.84.refs_3_.precond) | copy-start | bytes 442372
  13.2 78.0 %copy-start.3 = (f32[228,8,128]{2,1,0:T(8,128)S(1)}, f32[228,8,128]{2,1,0:T(8,128)}, u32[]{:S(2)}) copy-start(f32[228,8,128]{2,1,0:T(8,128)} %get-tuple-element.75.planes) | copy-start | bytes 2801668
  13.7 10.1 %collective-permute-start.5 = (f32[9,8,128]{2,1,0:T(8,128)S(1)}, f32[9,8,128]{2,1,0:T(8,128)S(1)}, u32[]{:S(2)}, u32[]{:S(2)}) collective-permute-start(f32[9,8,128]{2,1,0:T(8,128)S(1)} %get-tuple-element.88), channel_id=1, source_target_pairs={{8,16},{16,8},{24,32},{32,24},{40,48},{48,40},{56,64},{64,56},{72,... | collective-permute-start | bytes 110600 | tf_op jit(solution)/shard_map/ppermute | solution.py:555
  18.8 5.0 %collective-permute-start.6 = (f32[9,8,128]{2,1,0:T(8,128)S(1)}, f32[9,8,128]{2,1,0:T(8,128)S(1)}, u32[]{:S(2)}, u32[]{:S(2)}) collective-permute-start(f32[9,8,128]{2,1,0:T(8,128)S(1)} %get-tuple-element.89), channel_id=1, source_target_pairs={{0,8},{8,0},{16,24},{24,16},{32,40},{40,32},{48,56},{56,48},{64,72... | collective-permute-start | bytes 110600 | tf_op jit(solution)/shard_map/ppermute | solution.py:556
  20.7 5.5 %collective-permute-start.7 = (f32[8,128]{1,0:T(8,128)S(1)}, f32[8,128]{1,0:T(8,128)S(1)}, u32[]{:S(2)}, u32[]{:S(2)}) collective-permute-start(f32[8,128]{1,0:T(8,128)S(1)} %get-tuple-element.90), channel_id=1, source_target_pairs={{16,0},{24,8},{32,16},{40,24},{48,32},{56,40},{64,48},{72,56},{80,... | collective-permute-start | bytes 12296 | tf_op jit(solution)/shard_map/ppermute | solution.py:467
  37.6 25.1 %collective-permute-start.8 = (f32[58,8,128]{2,1,0:T(8,128)S(1)}, f32[58,8,128]{2,1,0:T(8,128)S(1)}, u32[]{:S(2)}, u32[]{:S(2)}) collective-permute-start(f32[58,8,128]{2,1,0:T(8,128)S(1)} %pad_maximum_fusion), channel_id=1, source_target_pairs={{0,4},{1,5},{2,6},{3,7},{4,0},{5,1},{6,2},{7,3},{8,12},{9,13},{10,... | collective-permute-start | bytes 712712 | tf_op jit(solution)/shard_map/ppermute | solution.py:493
  41.2 48.4 %collective-permute-start = (f32[114,8,128]{2,1,0:T(8,128)}, f32[114,8,128]{2,1,0:T(8,128)S(1)}, u32[]{:S(2)}, u32[]{:S(2)}) collective-permute-start(f32[114,8,128]{2,1,0:T(8,128)} %get-tuple-element.76), channel_id=1, source_target_pairs={{0,8},{8,0},{16,24},{24,16},{32,40},{40,32},{48,56},{56,48},{64,72... | collective-permute-start | bytes 1400840 | tf_op jit(solution)/shard_map/ppermute | solution.py:528
  43.2 47.3 %collective-permute-start.1 = (f32[114,8,128]{2,1,0:T(8,128)S(1)}, f32[114,8,128]{2,1,0:T(8,128)S(1)}, u32[]{:S(2)}, u32[]{:S(2)}) collective-permute-start(f32[114,8,128]{2,1,0:T(8,128)S(1)} %copy-done.17), channel_id=1, source_target_pairs={{8,16},{16,8},{24,32},{32,24},{40,48},{48,40},{56,64},{64,56},{72,... | collective-permute-start | bytes 1400840 | tf_op jit(solution)/shard_map/ppermute | solution.py:527
  64.0 43.4 %copy-start.16 = (f32[3,5,5]{2,0,1:T(4,128)S(1)}, f32[3,5,5]{2,0,1:T(4,128)}, u32[]{:S(2)}) copy-start(f32[3,5,5]{2,0,1:T(4,128)} %param.27) | copy-start | bytes 904
  64.1 9.5 %all-to-all-start.1 = ((f32[4,9,8,128]{3,2,1,0:T(8,128)}), f32[4,9,8,128]{3,2,1,0:T(8,128)S(1)}, u32[]{:S(2)}, u32[]{:S(2)}) async-start(f32[4,9,8,128]{3,2,1,0:T(8,128)} %get-tuple-element.93), calls=%async_computation.1 | async-start | bytes 294912 | tf_op jit(solution)/shard_map/all_to_all | solution.py:497
  73.6 0.7 copy-start.4
  74.2 27.0 %copy-start.5 = (f32[4,9,8,128]{3,2,1,0:T(8,128)S(1)}, f32[4,9,8,128]{3,2,1,0:T(8,128)}, u32[]{:S(2)}) copy-start(f32[4,9,8,128]{3,2,1,0:T(8,128)} %copy-done.4) | copy-start | bytes 442372
  74.2 27.0 %collective-permute-start.10 = (f32[8,128]{1,0:T(8,128)S(1)}, f32[8,128]{1,0:T(8,128)S(1)}, u32[]{:S(2)}, u32[]{:S(2)}) collective-permute-start(f32[8,128]{1,0:T(8,128)S(1)} %get-tuple-element.106), channel_id=1, source_target_pairs={{0,8},{8,0},{16,24},{24,16},{32,40},{40,32},{48,56},{56,48},{64,72... | collective-permute-start | bytes 12296 | tf_op jit(solution)/shard_map/ppermute | solution.py:476
  76.3 24.9 %collective-permute-start.9 = (f32[8,128]{1,0:T(8,128)S(1)}, f32[8,128]{1,0:T(8,128)S(1)}, u32[]{:S(2)}, u32[]{:S(2)}) collective-permute-start(f32[8,128]{1,0:T(8,128)S(1)} %get-tuple-element.107), channel_id=1, source_target_pairs={{8,16},{16,8},{24,32},{32,24},{40,48},{48,40},{56,64},{64,56},{72,... | collective-permute-start | bytes 12296 | tf_op jit(solution)/shard_map/ppermute | solution.py:474
  89.7 0.8 copy-start.6
  90.5 0.8 copy-start.8
  91.3 1.0 copy-start.7
  92.3 1.0 copy-start.9
  96.7 31.5 %copy-start.11 = (f32[6,1024]{1,0:T(8,128)S(1)}, f32[6,1024]{1,0:T(8,128)}, u32[]{:S(2)}) copy-start(f32[6,1024]{1,0:T(8,128)} %get-tuple-element.82.shell) | copy-start | bytes 73732
  96.7 11.5 %collective-permute-start.2 = (f32[15,16,128]{2,1,0:T(8,128)}, f32[15,16,128]{2,1,0:T(8,128)S(1)}, u32[]{:S(2)}, u32[]{:S(2)}) collective-permute-start(f32[15,16,128]{2,1,0:T(8,128)} %get-tuple-element.79), channel_id=1, source_target_pairs={{0,1},{1,0},{2,3},{3,2},{4,5},{5,4},{6,7},{7,6},{8,9},{9,8},{10,11... | collective-permute-start | bytes 368648 | tf_op jit(solution)/shard_map/ppermute | solution.py:493
  99.3 18.2 %collective-permute-start.3 = (f32[15,16,128]{2,1,0:T(8,128)}, f32[15,16,128]{2,1,0:T(8,128)S(1)}, u32[]{:S(2)}, u32[]{:S(2)}) collective-permute-start(f32[15,16,128]{2,1,0:T(8,128)} %get-tuple-element.79), channel_id=1, source_target_pairs={{1,2},{2,1},{3,4},{4,3},{5,6},{6,5},{9,10},{10,9},{11,12},{12,11},... | collective-permute-start | bytes 368648 | tf_op jit(solution)/shard_map/ppermute | solution.py:569
  101.3 51.2 %copy-start.15 = (f32[5]{0:T(128)S(1)}, f32[5]{0:T(128)}, u32[]{:S(2)}) copy-start(f32[5]{0:T(128)} %prow.3) | copy-start | bytes 64
  102.6 25.6 %all-to-all-start.2 = ((f32[4,9,8,128]{3,2,1,0:T(8,128)}), f32[4,9,8,128]{3,2,1,0:T(8,128)S(1)}, u32[]{:S(2)}, u32[]{:S(2)}) async-start(f32[4,9,8,128]{3,2,1,0:T(8,128)} %get-tuple-element.96), calls=%async_computation.2 | async-start | bytes 294912 | tf_op jit(solution)/shard_map/all_to_all | solution.py:497
  128.3 11.3 %collective-permute-start.11 = (f32[32,128]{1,0:T(8,128)S(1)}, f32[32,128]{1,0:T(8,128)S(1)}, u32[]{:S(2)}, u32[]{:S(2)}) collective-permute-start(f32[32,128]{1,0:T(8,128)S(1)} %get-tuple-element.98), channel_id=1, source_target_pairs={{0,8},{8,0},{16,24},{24,16},{32,40},{40,32},{48,56},{56,48},{64,72... | collective-permute-start | bytes 49160 | tf_op jit(solution)/shard_map/ppermute | solution.py:476
  130.2 9.4 %collective-permute-start.12 = (f32[32,128]{1,0:T(8,128)S(1)}, f32[32,128]{1,0:T(8,128)S(1)}, u32[]{:S(2)}, u32[]{:S(2)}) collective-permute-start(f32[32,128]{1,0:T(8,128)S(1)} %get-tuple-element.98), channel_id=1, source_target_pairs={{8,16},{16,8},{24,32},{32,24},{40,48},{48,40},{56,64},{64,56},{72,... | collective-permute-start | bytes 49160 | tf_op jit(solution)/shard_map/ppermute | solution.py:474
  137.7 7.6 %collective-permute-start.13 = (f32[8,128]{1,0:T(8,128)S(1)}, f32[8,128]{1,0:T(8,128)S(1)}, u32[]{:S(2)}, u32[]{:S(2)}) collective-permute-start(f32[8,128]{1,0:T(8,128)S(1)} %slice.143), channel_id=1, source_target_pairs={{0,16},{8,24},{16,32},{24,40},{32,48},{40,56},{48,64},{56,72},{64,... | collective-permute-start | bytes 12296 | tf_op jit(solution)/shard_map/ppermute | solution.py:467
  145.3 7.1 %collective-permute-start.14 = (f32[24,128]{1,0:T(8,128)S(1)}, f32[24,128]{1,0:T(8,128)S(1)}, u32[]{:S(2)}, u32[]{:S(2)}) collective-permute-start(f32[24,128]{1,0:T(8,128)S(1)} %get-tuple-element.105), channel_id=1, source_target_pairs={{8,16},{16,8},{24,32},{32,24},{40,48},{48,40},{56,64},{64,56},{72,... | collective-permute-start | bytes 36872 | tf_op jit(solution)/shard_map/ppermute | solution.py:622
  147.3 5.2 %collective-permute-start.15 = (f32[24,128]{1,0:T(8,128)S(1)}, f32[24,128]{1,0:T(8,128)S(1)}, u32[]{:S(2)}, u32[]{:S(2)}) collective-permute-start(f32[24,128]{1,0:T(8,128)S(1)} %get-tuple-element.104), channel_id=1, source_target_pairs={{0,8},{8,0},{16,24},{24,16},{32,40},{40,32},{48,56},{56,48},{64,72... | collective-permute-start | bytes 36872 | tf_op jit(solution)/shard_map/ppermute | solution.py:623

commit v4 on v3

--- a/solution.py
+++ b/solution.py
@@ -419,27 +419,35 @@
             reach[40 * i + 8 * b : 40 * i + 8 * b + 8, :] = value[8 * i : 8 * i + 8]
     walls = edges[FIELDS - 1]
     wall_planes = [pltpu.roll(walls, 128 - 8 * i, 1) if i else walls for i in range(4)]
-    node = jnp.concatenate([tall(full, 227), wall_planes[3]], axis=0)
-    index = node.astype(jnp.int32) - (span[0] - 2) * NODE_DEV
-    block, low = index >> 7, index & 127
-    blocks = [block[8 * q : 8 * q + 8] for q in range(4)]
-    lows = [low[8 * q : 8 * q + 8] for q in range(4)]
-
-    def pick(h, got):
+    lane = iota((16, 128), 1)
+    few = iota((8, 128), 1) < 8
+    packed = jnp.where(few, wall_planes[3][0:8], pltpu.roll(wall_planes[3][8:16], 8, 1))
+    base_node = (span[0] - 2) * NODE_DEV
+    index = [v.astype(jnp.int32) - base_node for v in (full[227], full[PLANES + 227], packed)]
+    tiles, lows = [v >> 7 for v in index], [v & 127 for v in index]
+
+    def pick(h, got, wanted):
         got = list(got)
         for i in range(3):
             row = jnp.broadcast_to(reach[pl.ds(40 * i + h, 1), :], (8, 128))
-            for q in range(4):
+            for q in wanted:
                 value = jnp.take_along_axis(row, lows[q], axis=1)
-                got[4 * i + q] = jnp.where(blocks[q] == h, value, got[4 * i + q])
+                got[3 * i + q] = jnp.where(tiles[q] == h, value, got[3 * i + q])
         return tuple(got)
 
-    got = lax.fori_loop(
-        0, 40, pick, tuple(jnp.zeros((8, 128), F32) for _ in range(12)), unroll=4
-    )
-    lane = iota((16, 128), 1)
-    disp = sum(tall(full, 224 + i) * jnp.concatenate(got[4 * i : 4 * i + 2], axis=0) for i in range(3))
-    side = sum(wall_planes[i] * jnp.concatenate(got[4 * i + 2 : 4 * i + 4], axis=0) for i in range(3))
+    got = tuple(jnp.zeros((8, 128), F32) for _ in range(9))
+    outer, inner = functools.partial(pick, wanted=(1, 2)), functools.partial(pick, wanted=(0, 1, 2))
+    got = lax.fori_loop(0, 8, outer, got, unroll=4)
+    got = lax.fori_loop(8, 32, inner, got, unroll=4)
+    got = lax.fori_loop(32, 40, outer, got, unroll=4)
+    disp = sum(
+        tall(full, 224 + i) * jnp.concatenate(got[3 * i : 3 * i + 2], axis=0) for i in range(3)
+    )
+    side = sum(
+        wall_planes[i]
+        * jnp.concatenate([got[3 * i + 2], pltpu.roll(got[3 * i + 2], 120, 1)], axis=0)
+        for i in range(3)
+    )
     side = jnp.where(lane < 8, side, 0.0)
     state[...] = jnp.zeros(state.shape, F32)
     for j in range(5):

time: 159 us -> 158 us (level)
  no operation moved by 1% of the time
where the time goes in v4:
time: 158 us; the launch traced here: 157 us
  starting transfers between devices  68.7 us (43%)
  waiting for transfers between devices  40.7 us (26%)
  Pallas kernels  26.4 us (17%)
  blocking collectives  10.3 us (7%)
  local copies, waits for them, and re-layouts  8.25 us (5%)
  between operations  1.79 us (1%)
    pallas_call x9, Pallas kernels, call(): pl.pallas_call(body, out_shape=out, in_specs=specs, out_specs=jax.tree.ma...  26.4 us
    ppermute x2, starting transfers between devices, exchange(): across = lax.ppermute(across, 'span', cross_pairs(count))  20.8 us
    ppermute x2, waiting for transfers between devices, swap(): return lax.ppermute(value, CHORD, [(c, c ^ bit) for c in range(count)])  14.2 us
    all_to_all x1, blocking collectives, ring_parts(): return lax.all_to_all(copies, 'y', 0, 0)  10.3 us
    ppermute x3, starting transfers between devices, along_span(): lax.ppermute(value, 'span', [(i, i + steps) for i in range(first, last)])  9.52 us
    ppermute x1, waiting for transfers between devices, per_device(): far = lax.ppermute(edges, CHORD, pairs)  9.32 us
    all_to_all x2, starting transfers between devices, ring_parts(): return lax.all_to_all(copies, 'y', 0, 0)  8.25 us
    unnamed x38, local copies, waits for them, and re-layouts  8.1 us
  transfers between devices with their start and end apart: 18, of which 6 were waited for; matrix products, arithmetic and copies ran while one was open for 1% of the time, Pallas kernels for 11%

profile of v4, /device:TPU:416, one launch (start us, length us, event | category | flops | bytes accessed | tf_op | source)
XLA Modules:
  0.0 157.2 jit_solution(10981083318100032121)
XLA Ops:
  1.3 3.2 %shard_map.158 = (f32[49,8,128]{2,1,0:T(8,128)}, f32[48,128]{1,0:T(8,128)}, f32[228,8,128]{2,1,0:T(8,128)}, f32[114,8,128]{2,1,0:T(8,128)}, f32[114,8,128]{2,1,0...) custom-call(s32[1]{0:T(128)} %bitcast.span, ...), custom_call_target="tpu_custom_call" | custom-call | flops 4194304 | bytes 524288 | tf_op jit(solution)/shard_map/pallas_call | solution.py:32
  4.5 4.5 %collective-permute-start.4 = (f32[48,128]{1,0:T(8,128)}, f32[48,128]{1,0:T(8,128)S(1)}, u32[]{:S(2)}, u32[]{:S(2)}) collective-permute-start(f32[48,128]{1,0:T(8,128)} %get-tuple-element.83), channel_id=1, source_target_pairs={{8,0},{16,8},{24,16},{32,24},{40,32},{48,40},{56,48},{64,56},{72,6... | collective-permute-start | bytes 73736 | tf_op jit(solution)/shard_map/ppermute | solution.py:475
  9.1 0.8 copy-done.12
  9.8 0.7 copy-done.14
  10.5 1.0 shard_map.161.loads
  11.5 0.0 collective-permute-done.4.rim.refs_2_.refs_8_
  11.5 0.0 copy-start
  11.5 0.9 copy-done
  12.5 0.8 copy-done.10
  13.2 0.4 shard_map.162
  13.7 5.1 %collective-permute-start.5 = (f32[9,8,128]{2,1,0:T(8,128)S(1)}, f32[9,8,128]{2,1,0:T(8,128)S(1)}, u32[]{:S(2)}, u32[]{:S(2)}) collective-permute-start(f32[9,8,128]{2,1,0:T(8,128)S(1)} %get-tuple-element.88), channel_id=1, source_target_pairs={{8,16},{16,8},{24,32},{32,24},{40,48},{48,40},{56,64},{64,56},{72,... | collective-permute-start | bytes 110600 | tf_op jit(solution)/shard_map/ppermute | solution.py:563
  18.8 1.9 %collective-permute-start.6 = (f32[9,8,128]{2,1,0:T(8,128)S(1)}, f32[9,8,128]{2,1,0:T(8,128)S(1)}, u32[]{:S(2)}, u32[]{:S(2)}) collective-permute-start(f32[9,8,128]{2,1,0:T(8,128)S(1)} %get-tuple-element.89), channel_id=1, source_target_pairs={{0,8},{8,0},{16,24},{24,16},{32,40},{40,32},{48,56},{56,48},{64,72... | collective-permute-start | bytes 110600 | tf_op jit(solution)/shard_map/ppermute | solution.py:564
  20.7 3.1 %collective-permute-start.7 = (f32[8,128]{1,0:T(8,128)S(1)}, f32[8,128]{1,0:T(8,128)S(1)}, u32[]{:S(2)}, u32[]{:S(2)}) collective-permute-start(f32[8,128]{1,0:T(8,128)S(1)} %get-tuple-element.90), channel_id=1, source_target_pairs={{16,0},{24,8},{32,16},{40,24},{48,32},{56,40},{64,48},{72,56},{80,... | collective-permute-start | bytes 12296 | tf_op jit(solution)/shard_map/ppermute | solution.py:475
  23.9 2.4 %collective-permute-done.7 = f32[8,128]{1,0:T(8,128)S(1)} collective-permute-done((f32[8,128]{1,0:T(8,128)S(1)}, f32[8,128]{1,0:T(8,128)S(1)}, u32[]{:S(2)}, u32[]{:S(2)}) %collective-permute-start.7) | collective-permute-done | bytes 4128 | tf_op jit(solution)/shard_map/ppermute | solution.py:475
  26.3 10.3 %all_to_all.15 = f32[4,9,8,128]{3,2,1,0:T(8,128)S(1)} all-to-all(f32[4,9,8,128]{3,2,1,0:T(8,128)S(1)} %broadcast_in_dim.18), channel_id=1, replica_groups=mesh['span'=64,'far_z'=2,'y'=4] {'y'}, dimensions={0} | all-to-all | bytes 294912 | tf_op jit(solution)/shard_map/all_to_all | solution.py:505
  36.6 0.9 pad_maximum_fusion
  37.6 3.6 %collective-permute-start.8 = (f32[58,8,128]{2,1,0:T(8,128)S(1)}, f32[58,8,128]{2,1,0:T(8,128)S(1)}, u32[]{:S(2)}, u32[]{:S(2)}) collective-permute-start(f32[58,8,128]{2,1,0:T(8,128)S(1)} %pad_maximum_fusion), channel_id=1, source_target_pairs={{0,4},{1,5},{2,6},{3,7},{4,0},{5,1},{6,2},{7,3},{8,12},{9,13},{10,... | collective-permute-start | bytes 712712 | tf_op jit(solution)/shard_map/ppermute | solution.py:501
  41.2 1.9 %collective-permute-start = (f32[114,8,128]{2,1,0:T(8,128)}, f32[114,8,128]{2,1,0:T(8,128)S(1)}, u32[]{:S(2)}, u32[]{:S(2)}) collective-permute-start(f32[114,8,128]{2,1,0:T(8,128)} %get-tuple-element.76), channel_id=1, source_target_pairs={{0,8},{8,0},{16,24},{24,16},{32,40},{40,32},{48,56},{56,48},{64,72... | collective-permute-start | bytes 1400840 | tf_op jit(solution)/shard_map/ppermute | solution.py:536
  43.2 5.3 %collective-permute-start.1 = (f32[114,8,128]{2,1,0:T(8,128)S(1)}, f32[114,8,128]{2,1,0:T(8,128)S(1)}, u32[]{:S(2)}, u32[]{:S(2)}) collective-permute-start(f32[114,8,128]{2,1,0:T(8,128)S(1)} %copy-done.17), channel_id=1, source_target_pairs={{8,16},{16,8},{24,32},{32,24},{40,48},{48,40},{56,64},{64,56},{72,... | collective-permute-start | bytes 1400840 | tf_op jit(solution)/shard_map/ppermute | solution.py:535
  48.4 14.2 %collective-permute-done.8.refs_1_.refs_6_ = f32[58,8,128]{2,1,0:T(8,128)S(1)} collective-permute-done((f32[58,8,128]{2,1,0:T(8,128)S(1)}, f32[58,8,128]{2,1,0:T(8,128)S(1)}, u32[]{:S(2)}, u32[]{:S(2)}) %collective-permute-start.8) | collective-permute-done | bytes 237600 | tf_op jit(solution)/shard_map/ppermute | solution.py:501
  62.7 1.4 shard_map.163
  64.1 3.5 %all-to-all-start.1 = ((f32[4,9,8,128]{3,2,1,0:T(8,128)}), f32[4,9,8,128]{3,2,1,0:T(8,128)S(1)}, u32[]{:S(2)}, u32[]{:S(2)}) async-start(f32[4,9,8,128]{3,2,1,0:T(8,128)} %get-tuple-element.93), calls=%async_computation.1 | async-start | bytes 294912 | tf_op jit(solution)/shard_map/all_to_all | solution.py:505
  67.5 6.0 %all-to-all-done.1.refs_5_ = f32[4,9,8,128]{3,2,1,0:T(8,128)S(1)} async-done(((f32[4,9,8,128]{3,2,1,0:T(8,128)}), f32[4,9,8,128]{3,2,1,0:T(8,128)S(1)}, u32[]{:S(2)}, u32[]{:S(2)}) %all-to-all-start.1) | async-done | bytes 147488 | tf_op jit(solution)/shard_map/all_to_all | solution.py:505
  73.6 0.7 copy-done.4
  74.2 2.0 %collective-permute-start.10 = (f32[8,128]{1,0:T(8,128)S(1)}, f32[8,128]{1,0:T(8,128)S(1)}, u32[]{:S(2)}, u32[]{:S(2)}) collective-permute-start(f32[8,128]{1,0:T(8,128)S(1)} %get-tuple-element.106), channel_id=1, source_target_pairs={{0,8},{8,0},{16,24},{24,16},{32,40},{40,32},{48,56},{56,48},{64,72... | collective-permute-start | bytes 12296 | tf_op jit(solution)/shard_map/ppermute | solution.py:484
  76.3 13.4 %collective-permute-start.9 = (f32[8,128]{1,0:T(8,128)S(1)}, f32[8,128]{1,0:T(8,128)S(1)}, u32[]{:S(2)}, u32[]{:S(2)}) collective-permute-start(f32[8,128]{1,0:T(8,128)S(1)} %get-tuple-element.107), channel_id=1, source_target_pairs={{8,16},{16,8},{24,32},{32,24},{40,48},{48,40},{56,64},{64,56},{72,... | collective-permute-start | bytes 12296 | tf_op jit(solution)/shard_map/ppermute | solution.py:482
  89.7 0.8 copy-done.6
  90.5 0.8 copy-done.8
  91.3 1.0 copy-done.7
  92.3 1.0 copy-done.9
  93.3 3.4 %shard_map.159 = (f32[456,8,128]{2,1,0:T(8,128)S(1)}, f32[15,16,128]{2,1,0:T(8,128)}) custom-call(s32[1]{0:T(128)} %bitcast.span, f32[228,8,128]{2,1,0:T(8,128)S(1)} %copy-done.3, f32[114,8,128]{2,1,0:T(8,128)S(1)} %copy-done.7, f32[114,8,128]{2,1,0:T(8,128)S(1)} %copy-done.9), custom_call_target="tpu_custom_call" | custom-call | flops 4194304 | bytes 524288 | tf_op jit(solution)/shard_map/pallas_call | solution.py:32
  96.7 2.6 %collective-permute-start.2 = (f32[15,16,128]{2,1,0:T(8,128)}, f32[15,16,128]{2,1,0:T(8,128)S(1)}, u32[]{:S(2)}, u32[]{:S(2)}) collective-permute-start(f32[15,16,128]{2,1,0:T(8,128)} %get-tuple-element.79), channel_id=1, source_target_pairs={{0,1},{1,0},{2,3},{3,2},{4,5},{5,4},{6,7},{7,6},{8,9},{9,8},{10,11... | collective-permute-start | bytes 368648 | tf_op jit(solution)/shard_map/ppermute | solution.py:501
  99.3 1.9 %collective-permute-start.3 = (f32[15,16,128]{2,1,0:T(8,128)}, f32[15,16,128]{2,1,0:T(8,128)S(1)}, u32[]{:S(2)}, u32[]{:S(2)}) collective-permute-start(f32[15,16,128]{2,1,0:T(8,128)} %get-tuple-element.79), channel_id=1, source_target_pairs={{1,2},{2,1},{3,4},{4,3},{5,6},{6,5},{9,10},{10,9},{11,12},{12,11},... | collective-permute-start | bytes 368648 | tf_op jit(solution)/shard_map/ppermute | solution.py:577
  101.3 0.0 copy-start.15
  101.3 1.4 shard_map.164
  102.6 4.8 %all-to-all-start.2 = ((f32[4,9,8,128]{3,2,1,0:T(8,128)}), f32[4,9,8,128]{3,2,1,0:T(8,128)S(1)}, u32[]{:S(2)}, u32[]{:S(2)}) async-start(f32[4,9,8,128]{3,2,1,0:T(8,128)} %get-tuple-element.96), calls=%async_computation.2 | async-start | bytes 294912 | tf_op jit(solution)/shard_map/all_to_all | solution.py:505
  107.4 0.7 copy.44.downwind
  108.1 9.3 %collective-permute-done.3.far = f32[15,16,128]{2,1,0:T(8,128)S(1)} collective-permute-done((f32[15,16,128]{2,1,0:T(8,128)}, f32[15,16,128]{2,1,0:T(8,128)S(1)}, u32[]{:S(2)}, u32[]{:S(2)}) %collective-permute-start.3) | collective-permute-done | bytes 122912 | tf_op jit(solution)/shard_map/ppermute | solution.py:577
  117.5 10.7 %shard_map.160 = (f32[5,16,8,128]{3,2,1,0:T(8,128)S(1)}, f32[15,16,128]{2,1,0:T(8,128)S(1)}) custom-call(s32[1]{0:T(128)} %bitcast.1.odd, f32[456,8,128]{2,1,0:T(8,128)S(1)} %get-tuple-element.78.full, f32[15,16,128]{2,1,0:T(8,128)S(1)} %collective-permute-done.2.near, f32[15,16,128]{2,1,0:T(8,128)S(1)} %collective-permute-done.3.far, ...), custom_call_target="tpu_custom_call" | custom-call | flops 16777216 | bytes 2097152 | tf_op jit(solution)/shard_map/pallas_call | solution.py:32
  128.2 0.1 shard_map.165
  128.3 1.9 %collective-permute-start.11 = (f32[32,128]{1,0:T(8,128)S(1)}, f32[32,128]{1,0:T(8,128)S(1)}, u32[]{:S(2)}, u32[]{:S(2)}) collective-permute-start(f32[32,128]{1,0:T(8,128)S(1)} %get-tuple-element.98), channel_id=1, source_target_pairs={{0,8},{8,0},{16,24},{24,16},{32,40},{40,32},{48,56},{56,48},{64,72... | collective-permute-start | bytes 49160 | tf_op jit(solution)/shard_map/ppermute | solution.py:484
  130.2 7.4 %collective-permute-start.12 = (f32[32,128]{1,0:T(8,128)S(1)}, f32[32,128]{1,0:T(8,128)S(1)}, u32[]{:S(2)}, u32[]{:S(2)}) collective-permute-start(f32[32,128]{1,0:T(8,128)S(1)} %get-tuple-element.98), channel_id=1, source_target_pairs={{8,16},{16,8},{24,32},{32,24},{40,48},{48,40},{56,64},{64,56},{72,... | collective-permute-start | bytes 49160 | tf_op jit(solution)/shard_map/ppermute | solution.py:482
  137.7 1.9 %collective-permute-start.13 = (f32[8,128]{1,0:T(8,128)S(1)}, f32[8,128]{1,0:T(8,128)S(1)}, u32[]{:S(2)}, u32[]{:S(2)}) collective-permute-start(f32[8,128]{1,0:T(8,128)S(1)} %slice.143), channel_id=1, source_target_pairs={{0,16},{8,24},{16,32},{24,40},{32,48},{40,56},{48,64},{56,72},{64,... | collective-permute-start | bytes 12296 | tf_op jit(solution)/shard_map/ppermute | solution.py:475
  139.8 5.5 %collective-permute-done.13 = f32[8,128]{1,0:T(8,128)S(1)} collective-permute-done((f32[8,128]{1,0:T(8,128)S(1)}, f32[8,128]{1,0:T(8,128)S(1)}, u32[]{:S(2)}, u32[]{:S(2)}) %collective-permute-start.13) | collective-permute-done | bytes 4128 | tf_op jit(solution)/shard_map/ppermute | solution.py:475
  145.3 1.9 %collective-permute-start.14 = (f32[24,128]{1,0:T(8,128)S(1)}, f32[24,128]{1,0:T(8,128)S(1)}, u32[]{:S(2)}, u32[]{:S(2)}) collective-permute-start(f32[24,128]{1,0:T(8,128)S(1)} %get-tuple-element.105), channel_id=1, source_target_pairs={{8,16},{16,8},{24,32},{32,24},{40,48},{48,40},{56,64},{64,56},{72,... | collective-permute-start | bytes 36872 | tf_op jit(solution)/shard_map/ppermute | solution.py:630
  147.3 1.9 %collective-permute-start.15 = (f32[24,128]{1,0:T(8,128)S(1)}, f32[24,128]{1,0:T(8,128)S(1)}, u32[]{:S(2)}, u32[]{:S(2)}) collective-permute-start(f32[24,128]{1,0:T(8,128)S(1)} %get-tuple-element.104), channel_id=1, source_target_pairs={{0,8},{8,0},{16,24},{24,16},{32,40},{40,32},{48,56},{56,48},{64,72... | collective-permute-start | bytes 36872 | tf_op jit(solution)/shard_map/ppermute | solution.py:631
  149.3 3.2 %collective-permute-done.14.across = f32[24,128]{1,0:T(8,128)S(1)} collective-permute-done((f32[24,128]{1,0:T(8,128)S(1)}, f32[24,128]{1,0:T(8,128)S(1)}, u32[]{:S(2)}, u32[]{:S(2)}) %collective-permute-start.14) | collective-permute-done | bytes 12320 | tf_op jit(solution)/shard_map/ppermute | solution.py:630
  152.5 4.8 %shard_map.166 = (f32[5,16,8,128]{3,2,1,0:T(8,128)}, f32[6,1024]{1,0:T(8,128)}) custom-call(s32[1]{0:T(128)} %bitcast.span, f32[5]{0:T(128)S(1)} %copy-done.15, f32[3,5,5]{2,1,0:T(8,128)S(1)} %copy.43.upwind, f32[3,5,5]{2,1,0:T(8,128)S(1)} %copy.44.downwind, f32[5,16,8,128]{3,2,1,0:T(8,128)S(1)} %get-tuple-element.80.base, ...), custom_call_target="tpu_custom_call" | custom-call | flops 8388608 | bytes 1048576 | tf_op jit(solution)/shard_map/pallas_call | solution.py:32
  (66 shorter events, 0.3 us)
Async XLA Ops:
  4.5 7.0 %collective-permute-start.4 = (f32[48,128]{1,0:T(8,128)}, f32[48,128]{1,0:T(8,128)S(1)}, u32[]{:S(2)}, u32[]{:S(2)}) collective-permute-start(f32[48,128]{1,0:T(8,128)} %get-tuple-element.83), channel_id=1, source_target_pairs={{8,0},{16,8},{24,16},{32,24},{40,32},{48,40},{56,48},{64,56},{72,6... | collective-permute-start | bytes 73736 | tf_op jit(solution)/shard_map/ppermute | solution.py:475
  9.1 0.8 copy-start.12
  9.8 0.7 copy-start.14
  10.5 52.2 %copy-start.13 = (f32[6,1024]{1,0:T(8,128)S(1)}, f32[6,1024]{1,0:T(8,128)}, u32[]{:S(2)}) copy-start(f32[6,1024]{1,0:T(8,128)} %get-tuple-element.91.refs_7_) | copy-start | bytes 73732
  11.5 0.9 copy-start
  12.5 0.8 copy-start.10
  13.2 29.9 %copy-start.17 = (f32[114,8,128]{2,1,0:T(8,128)S(1)}, f32[114,8,128]{2,1,0:T(8,128)}, u32[]{:S(2)}) copy-start(f32[114,8,128]{2,1,0:T(8,128)} %get-tuple-element.77) | copy-start | bytes 1400836
  13.2 49.5 %copy-start.1 = (f32[49,8,128]{2,1,0:T(8,128)S(1)}, f32[49,8,128]{2,1,0:T(8,128)}, u32[]{:S(2)}) copy-start(f32[49,8,128]{2,1,0:T(8,128)} %get-tuple-element.85.pack.refs_0_) | copy-start | bytes 602116
  13.2 49.5 %copy-start.2 = (f32[6,6,1024]{2,1,0:T(8,128)S(1)}, f32[6,6,1024]{2,1,0:T(8,128)}, u32[]{:S(2)}) copy-start(f32[6,6,1024]{2,1,0:T(8,128)} %get-tuple-element.84.refs_3_.precond) | copy-start | bytes 442372
  13.2 78.0 %copy-start.3 = (f32[228,8,128]{2,1,0:T(8,128)S(1)}, f32[228,8,128]{2,1,0:T(8,128)}, u32[]{:S(2)}) copy-start(f32[228,8,128]{2,1,0:T(8,128)} %get-tuple-element.75.planes) | copy-start | bytes 2801668
  13.7 10.1 %collective-permute-start.5 = (f32[9,8,128]{2,1,0:T(8,128)S(1)}, f32[9,8,128]{2,1,0:T(8,128)S(1)}, u32[]{:S(2)}, u32[]{:S(2)}) collective-permute-start(f32[9,8,128]{2,1,0:T(8,128)S(1)} %get-tuple-element.88), channel_id=1, source_target_pairs={{8,16},{16,8},{24,32},{32,24},{40,48},{48,40},{56,64},{64,56},{72,... | collective-permute-start | bytes 110600 | tf_op jit(solution)/shard_map/ppermute | solution.py:563
  18.8 5.0 %collective-permute-start.6 = (f32[9,8,128]{2,1,0:T(8,128)S(1)}, f32[9,8,128]{2,1,0:T(8,128)S(1)}, u32[]{:S(2)}, u32[]{:S(2)}) collective-permute-start(f32[9,8,128]{2,1,0:T(8,128)S(1)} %get-tuple-element.89), channel_id=1, source_target_pairs={{0,8},{8,0},{16,24},{24,16},{32,40},{40,32},{48,56},{56,48},{64,72... | collective-permute-start | bytes 110600 | tf_op jit(solution)/shard_map/ppermute | solution.py:564
  20.7 5.5 %collective-permute-start.7 = (f32[8,128]{1,0:T(8,128)S(1)}, f32[8,128]{1,0:T(8,128)S(1)}, u32[]{:S(2)}, u32[]{:S(2)}) collective-permute-start(f32[8,128]{1,0:T(8,128)S(1)} %get-tuple-element.90), channel_id=1, source_target_pairs={{16,0},{24,8},{32,16},{40,24},{48,32},{56,40},{64,48},{72,56},{80,... | collective-permute-start | bytes 12296 | tf_op jit(solution)/shard_map/ppermute | solution.py:475
  37.6 25.1 %collective-permute-start.8 = (f32[58,8,128]{2,1,0:T(8,128)S(1)}, f32[58,8,128]{2,1,0:T(8,128)S(1)}, u32[]{:S(2)}, u32[]{:S(2)}) collective-permute-start(f32[58,8,128]{2,1,0:T(8,128)S(1)} %pad_maximum_fusion), channel_id=1, source_target_pairs={{0,4},{1,5},{2,6},{3,7},{4,0},{5,1},{6,2},{7,3},{8,12},{9,13},{10,... | collective-permute-start | bytes 712712 | tf_op jit(solution)/shard_map/ppermute | solution.py:501
  41.2 48.4 %collective-permute-start = (f32[114,8,128]{2,1,0:T(8,128)}, f32[114,8,128]{2,1,0:T(8,128)S(1)}, u32[]{:S(2)}, u32[]{:S(2)}) collective-permute-start(f32[114,8,128]{2,1,0:T(8,128)} %get-tuple-element.76), channel_id=1, source_target_pairs={{0,8},{8,0},{16,24},{24,16},{32,40},{40,32},{48,56},{56,48},{64,72... | collective-permute-start | bytes 1400840 | tf_op jit(solution)/shard_map/ppermute | solution.py:536
  43.2 47.3 %collective-permute-start.1 = (f32[114,8,128]{2,1,0:T(8,128)S(1)}, f32[114,8,128]{2,1,0:T(8,128)S(1)}, u32[]{:S(2)}, u32[]{:S(2)}) collective-permute-start(f32[114,8,128]{2,1,0:T(8,128)S(1)} %copy-done.17), channel_id=1, source_target_pairs={{8,16},{16,8},{24,32},{32,24},{40,48},{48,40},{56,64},{64,56},{72,... | collective-permute-start | bytes 1400840 | tf_op jit(solution)/shard_map/ppermute | solution.py:535
  64.0 43.4 %copy-start.16 = (f32[3,5,5]{2,0,1:T(4,128)S(1)}, f32[3,5,5]{2,0,1:T(4,128)}, u32[]{:S(2)}) copy-start(f32[3,5,5]{2,0,1:T(4,128)} %param.27) | copy-start | bytes 904
  64.1 9.5 %all-to-all-start.1 = ((f32[4,9,8,128]{3,2,1,0:T(8,128)}), f32[4,9,8,128]{3,2,1,0:T(8,128)S(1)}, u32[]{:S(2)}, u32[]{:S(2)}) async-start(f32[4,9,8,128]{3,2,1,0:T(8,128)} %get-tuple-element.93), calls=%async_computation.1 | async-start | bytes 294912 | tf_op jit(solution)/shard_map/all_to_all | solution.py:505
  73.6 0.7 copy-start.4
  74.2 27.0 %copy-start.5 = (f32[4,9,8,128]{3,2,1,0:T(8,128)S(1)}, f32[4,9,8,128]{3,2,1,0:T(8,128)}, u32[]{:S(2)}) copy-start(f32[4,9,8,128]{3,2,1,0:T(8,128)} %copy-done.4) | copy-start | bytes 442372
  74.2 27.0 %collective-permute-start.10 = (f32[8,128]{1,0:T(8,128)S(1)}, f32[8,128]{1,0:T(8,128)S(1)}, u32[]{:S(2)}, u32[]{:S(2)}) collective-permute-start(f32[8,128]{1,0:T(8,128)S(1)} %get-tuple-element.106), channel_id=1, source_target_pairs={{0,8},{8,0},{16,24},{24,16},{32,40},{40,32},{48,56},{56,48},{64,72... | collective-permute-start | bytes 12296 | tf_op jit(solution)/shard_map/ppermute | solution.py:484
  76.3 24.9 %collective-permute-start.9 = (f32[8,128]{1,0:T(8,128)S(1)}, f32[8,128]{1,0:T(8,128)S(1)}, u32[]{:S(2)}, u32[]{:S(2)}) collective-permute-start(f32[8,128]{1,0:T(8,128)S(1)} %get-tuple-element.107), channel_id=1, source_target_pairs={{8,16},{16,8},{24,32},{32,24},{40,48},{48,40},{56,64},{64,56},{72,... | collective-permute-start | bytes 12296 | tf_op jit(solution)/shard_map/ppermute | solution.py:482
  89.7 0.8 copy-start.6
  90.5 0.8 copy-start.8
  91.3 1.0 copy-start.7
  92.3 1.0 copy-start.9
  96.7 31.5 %copy-start.11 = (f32[6,1024]{1,0:T(8,128)S(1)}, f32[6,1024]{1,0:T(8,128)}, u32[]{:S(2)}) copy-start(f32[6,1024]{1,0:T(8,128)} %get-tuple-element.82.shell) | copy-start | bytes 73732
  96.7 11.5 %collective-permute-start.2 = (f32[15,16,128]{2,1,0:T(8,128)}, f32[15,16,128]{2,1,0:T(8,128)S(1)}, u32[]{:S(2)}, u32[]{:S(2)}) collective-permute-start(f32[15,16,128]{2,1,0:T(8,128)} %get-tuple-element.79), channel_id=1, source_target_pairs={{0,1},{1,0},{2,3},{3,2},{4,5},{5,4},{6,7},{7,6},{8,9},{9,8},{10,11... | collective-permute-start | bytes 368648 | tf_op jit(solution)/shard_map/ppermute | solution.py:501
  99.3 18.2 %collective-permute-start.3 = (f32[15,16,128]{2,1,0:T(8,128)}, f32[15,16,128]{2,1,0:T(8,128)S(1)}, u32[]{:S(2)}, u32[]{:S(2)}) collective-permute-start(f32[15,16,128]{2,1,0:T(8,128)} %get-tuple-element.79), channel_id=1, source_target_pairs={{1,2},{2,1},{3,4},{4,3},{5,6},{6,5},{9,10},{10,9},{11,12},{12,11},... | collective-permute-start | bytes 368648 | tf_op jit(solution)/shard_map/ppermute | solution.py:577
  101.3 51.2 %copy-start.15 = (f32[5]{0:T(128)S(1)}, f32[5]{0:T(128)}, u32[]{:S(2)}) copy-start(f32[5]{0:T(128)} %prow.3) | copy-start | bytes 64
  102.6 25.6 %all-to-all-start.2 = ((f32[4,9,8,128]{3,2,1,0:T(8,128)}), f32[4,9,8,128]{3,2,1,0:T(8,128)S(1)}, u32[]{:S(2)}, u32[]{:S(2)}) async-start(f32[4,9,8,128]{3,2,1,0:T(8,128)} %get-tuple-element.96), calls=%async_computation.2 | async-start | bytes 294912 | tf_op jit(solution)/shard_map/all_to_all | solution.py:505
  128.3 11.3 %collective-permute-start.11 = (f32[32,128]{1,0:T(8,128)S(1)}, f32[32,128]{1,0:T(8,128)S(1)}, u32[]{:S(2)}, u32[]{:S(2)}) collective-permute-start(f32[32,128]{1,0:T(8,128)S(1)} %get-tuple-element.98), channel_id=1, source_target_pairs={{0,8},{8,0},{16,24},{24,16},{32,40},{40,32},{48,56},{56,48},{64,72... | collective-permute-start | bytes 49160 | tf_op jit(solution)/shard_map/ppermute | solution.py:484
  130.2 9.4 %collective-permute-start.12 = (f32[32,128]{1,0:T(8,128)S(1)}, f32[32,128]{1,0:T(8,128)S(1)}, u32[]{:S(2)}, u32[]{:S(2)}) collective-permute-start(f32[32,128]{1,0:T(8,128)S(1)} %get-tuple-element.98), channel_id=1, source_target_pairs={{8,16},{16,8},{24,32},{32,24},{40,48},{48,40},{56,64},{64,56},{72,... | collective-permute-start | bytes 49160 | tf_op jit(solution)/shard_map/ppermute | solution.py:482
  137.7 7.6 %collective-permute-start.13 = (f32[8,128]{1,0:T(8,128)S(1)}, f32[8,128]{1,0:T(8,128)S(1)}, u32[]{:S(2)}, u32[]{:S(2)}) collective-permute-start(f32[8,128]{1,0:T(8,128)S(1)} %slice.143), channel_id=1, source_target_pairs={{0,16},{8,24},{16,32},{24,40},{32,48},{40,56},{48,64},{56,72},{64,... | collective-permute-start | bytes 12296 | tf_op jit(solution)/shard_map/ppermute | solution.py:475
  145.3 7.1 %collective-permute-start.14 = (f32[24,128]{1,0:T(8,128)S(1)}, f32[24,128]{1,0:T(8,128)S(1)}, u32[]{:S(2)}, u32[]{:S(2)}) collective-permute-start(f32[24,128]{1,0:T(8,128)S(1)} %get-tuple-element.105), channel_id=1, source_target_pairs={{8,16},{16,8},{24,32},{32,24},{40,48},{48,40},{56,64},{64,56},{72,... | collective-permute-start | bytes 36872 | tf_op jit(solution)/shard_map/ppermute | solution.py:630
  147.3 5.2 %collective-permute-start.15 = (f32[24,128]{1,0:T(8,128)S(1)}, f32[24,128]{1,0:T(8,128)S(1)}, u32[]{:S(2)}, u32[]{:S(2)}) collective-permute-start(f32[24,128]{1,0:T(8,128)S(1)} %get-tuple-element.104), channel_id=1, source_target_pairs={{0,8},{8,0},{16,24},{24,16},{32,40},{40,32},{48,56},{56,48},{64,72... | collective-permute-start | bytes 36872 | tf_op jit(solution)/shard_map/ppermute | solution.py:631
